TPU v7x, 32 devices: a whole 2x2x4 slice. The times are simulated.
32 devices in a mesh: tensor: 4 (over y, core), seq: 8 (over z, x).
Axes of the slice: x: 2, y: 2, z: 4, core: 2. Of those that a mesh axis runs over, the one named last changes fastest.
Arguments:
- frames: bfloat16 [4096, 1536], P('seq', 'tensor'), may hold values from -8 to 8
- segment: int32 [4096], replicated, may hold values from 0 to 15, never falling along the last dimension, each value on 1 to 512 neighbouring positions
- time_token: bfloat16 [2, 1536], replicated, may hold values from -6 to 6
- context: bfloat16 [2, 128, 768], replicated, may hold values from -6 to 6
- gain_attn: float32 [1536], P('tensor'), may hold values from 0.5 to 1.5
- bias_attn: float32 [1536], P('tensor'), may hold values from -1.75 to 1.75
- gain_cross: float32 [1536], P('tensor'), may hold values from 0.5 to 1.5
- bias_cross: float32 [1536], P('tensor'), may hold values from -1.75 to 1.75
- gain_ffn: float32 [1536], P('tensor'), may hold values from 0.5 to 1.5
- bias_ffn: float32 [1536], P('tensor'), may hold values from -1.75 to 1.75
- w_query: bfloat16 [1536, 1536], P(None, 'tensor'), may hold values from -0.15625 to 0.15625
- w_key: bfloat16 [1536, 1536], P(None, 'tensor'), may hold values from -0.15625 to 0.15625
- w_value: bfloat16 [1536, 1536], P(None, 'tensor'), may hold values from -0.15625 to 0.15625
- w_out: bfloat16 [1536, 1536], P('tensor'), may hold values from -1.25 to 1.25
- c_query: bfloat16 [1536, 1536], P(None, 'tensor'), may hold values from -0.15625 to 0.15625
- c_key: bfloat16 [768, 1536], P(None, 'tensor'), may hold values from -0.21875 to 0.21875
- c_value: bfloat16 [768, 1536], P(None, 'tensor'), may hold values from -0.21875 to 0.21875
- c_out: bfloat16 [1536, 1536], P('tensor'), may hold values from -1.25 to 1.25
- w_gate: bfloat16 [1536, 6144], P(None, 'tensor'), may hold values from -1 to 1
- w_up: bfloat16 [1536, 6144], P(None, 'tensor'), may hold values from -1 to 1
- w_down: bfloat16 [6144, 1536], P('tensor'), may hold values from -0.078125 to 0.078125
- out_grad: bfloat16 [4096, 1536], P('seq', 'tensor'), may hold values from -8 to 8
Outputs:
- block_out: bfloat16 [4096, 1536], P('seq', 'tensor')
- d_frames: float32 [4096, 1536], P('seq', 'tensor')
- d_gain_attn: float32 [1536], P(('tensor', 'seq'))
- d_bias_attn: float32 [1536], P(('tensor', 'seq'))
- d_gain_cross: float32 [1536], P(('tensor', 'seq'))
- d_bias_cross: float32 [1536], P(('tensor', 'seq'))
- d_gain_ffn: float32 [1536], P(('tensor', 'seq'))
- d_bias_ffn: float32 [1536], P(('tensor', 'seq'))
- d_w_query: float32 [1536, 1536], P('seq', 'tensor')
- d_w_key: float32 [1536, 1536], P('seq', 'tensor')
- d_w_value: float32 [1536, 1536], P('seq', 'tensor')
- d_w_out: float32 [1536, 1536], P(('tensor', 'seq'))
- d_c_query: float32 [1536, 1536], P('seq', 'tensor')
- d_c_key: float32 [768, 1536], P('seq', 'tensor')
- d_c_value: float32 [768, 1536], P('seq', 'tensor')
- d_c_out: float32 [1536, 1536], P(('tensor', 'seq'))
- d_w_gate: float32 [1536, 6144], P('seq', 'tensor')
- d_w_up: float32 [1536, 6144], P('seq', 'tensor')
- d_w_down: float32 [6144, 1536], P(('tensor', 'seq'))
Inputs may be any that keep to these rules, and one draw needn't show every extreme that they name: `segment`: clip numbers never fall along the frames; each clip covers 1 to 512 frames and one covers exactly 512.
All inputs are finite; a program needn't handle non-finite values.
Results may differ from a plain program's by a relative error of at most 0.03.
Values may be sent and summed in bfloat16 or wider, within the bound.
No kernel may reach another device: no remote copies, remote signals or barrier semaphores. Data moves between devices by JAX's collectives and lax.ppermute only.
A program may use at most 192 MiB of HBM per device.

v0:
```python
import math

import jax
import jax.numpy as jnp
from jax import lax
from jax.sharding import PartitionSpec as P

HEAD_SIZE = 64
ROW_MIN = 2048


def with_halo(cells, sides, width):
    for axis, dim in sides:
        count = lax.axis_size(axis)
        ends = count - 1
        head = lax.slice_in_dim(cells, 0, width, axis=dim)
        tail = lax.slice_in_dim(cells, cells.shape[dim] - width, cells.shape[dim], axis=dim)
        cells = jnp.concatenate(
            [
                lax.ppermute(tail, axis, [(i, (i + 1) % count) for i in range(ends)]),
                cells,
                lax.ppermute(head, axis, [((i + 1) % count, i) for i in range(ends)]),
            ],
            axis=dim,
        )
    return cells


def from_behind(value, axis, by):
    peers = lax.axis_size(axis)
    pairs = [(i, i + by) for i in range(peers) if 0 <= i + by < peers]
    return lax.ppermute(value, axis, pairs)


def frame_clip_labels(segment, row_length):
    frame_index = jnp.arange(segment.shape[0], dtype=jnp.int32)
    border = (frame_index % row_length == 0) | (segment != jnp.roll(segment, 1))
    clip_starts = lax.cummax(jnp.where(border, frame_index, 0), axis=0)
    return (clip_starts, (frame_index - clip_starts + 1).astype(jnp.float32))


def rotary_tables(frame_positions, col_count):
    half_dim = HEAD_SIZE // 2
    frequency = jnp.exp(jnp.arange(half_dim, dtype=jnp.float32) * (-math.log(10000.0) / half_dim))
    angles = frame_positions[:, None] * frequency[None, :]
    number_of_heads = col_count // HEAD_SIZE
    row_total = frame_positions.shape[0]
    cosine = jnp.broadcast_to(
        jnp.cos(angles)[:, None, None, :], (row_total, number_of_heads, 2, half_dim)
    ).reshape(row_total, col_count)
    sine_part = jnp.sin(angles)
    signed = jnp.broadcast_to(
        jnp.stack([-sine_part, sine_part], 1)[:, None, :, :],
        (row_total, number_of_heads, 2, half_dim),
    ).reshape(row_total, col_count)
    return (cosine, signed)


def partner(value_rows):
    row_total, col_count = value_rows.shape
    halves = value_rows.reshape(row_total, col_count // HEAD_SIZE, 2, HEAD_SIZE // 2)
    return halves[:, :, ::-1, :].reshape(row_total, col_count)


def rotate(value_rows, tables):
    return value_rows * tables[0] + partner(value_rows) * tables[1]


def rotate_back(gradient, tables):
    return gradient * tables[0] + partner(gradient * tables[1])


def product(left, right):
    return jnp.dot(left, right, preferred_element_type=jnp.float32)


def inner_rows(left, right):
    return jnp.einsum("nd,nf->df", left, right, preferred_element_type=jnp.float32)


def back_project(gradient, weight):
    return jnp.einsum("nf,df->nd", gradient, weight, preferred_element_type=jnp.float32)


def norm_forward(value_rows, norm_gain, norm_bias, model_width):
    first_sum = jnp.sum(value_rows, -1, keepdims=True)
    square_sum = jnp.sum(value_rows * value_rows, -1, keepdims=True)
    first_sum, square_sum = lax.psum((first_sum, square_sum), "tensor")
    row_means = first_sum / model_width
    inverse = lax.rsqrt(square_sum / model_width - row_means * row_means + 1e-05)
    scaled = (value_rows - row_means) * inverse
    return (scaled * norm_gain + norm_bias, scaled, inverse)


def norm_backward(gradient, scaled, inverse, norm_gain, model_width):
    scaled_grad = gradient * norm_gain
    plain_sum = jnp.sum(scaled_grad, -1, keepdims=True)
    cross_sum = jnp.sum(scaled_grad * scaled, -1, keepdims=True)
    plain_sum, cross_sum = lax.psum((plain_sum, cross_sum), "tensor")
    inputs_grad = inverse * (
        scaled_grad - plain_sum / model_width - scaled * cross_sum / model_width
    )
    return (inputs_grad, jnp.sum(gradient * scaled, 0), jnp.sum(gradient, 0))


def spread_normed(normed):
    return lax.all_gather(normed.astype(jnp.bfloat16), "tensor", axis=1, tiled=True)


def collect_branch(partial_sum):
    return lax.psum_scatter(
        partial_sum.astype(jnp.bfloat16), "tensor", scatter_dimension=1, tiled=True
    ).astype(jnp.float32)


def spread_grad(gradient):
    return lax.all_gather(gradient.astype(jnp.bfloat16), "tensor", axis=1, tiled=True)


def collect_grad(partial_sum):
    return lax.psum_scatter(
        partial_sum.astype(jnp.bfloat16), "tensor", scatter_dimension=1, tiled=True
    ).astype(jnp.float32)


def per_device(
    frames,
    segment,
    time_token,
    context,
    gain_attn,
    bias_attn,
    gain_cross,
    bias_cross,
    gain_ffn,
    bias_ffn,
    w_query,
    w_key,
    w_value,
    w_out,
    c_query,
    c_key,
    c_value,
    c_out,
    w_gate,
    w_up,
    w_down,
    out_grad,
):
    local_rows = frames.shape[0]
    local_width = frames.shape[1]
    model_width = w_query.shape[0]
    head_cols = w_query.shape[1]
    number_of_heads = head_cols // HEAD_SIZE
    number_of_frames = lax.axis_size("seq") * local_rows
    row_length = min(max(ROW_MIN, 64 * lax.axis_size("seq")), number_of_frames)
    first_frame = lax.axis_index("seq") * local_rows
    clip_starts, frame_positions = frame_clip_labels(segment, row_length)
    own_labels = lax.dynamic_slice_in_dim(clip_starts, first_frame, local_rows)
    own_positions = lax.dynamic_slice_in_dim(frame_positions, first_frame, local_rows)
    blanks = jnp.full((local_rows,), -1, jnp.int32)
    key_labels = lax.dynamic_slice_in_dim(
        jnp.concatenate([blanks, clip_starts, blanks]), first_frame, 3 * local_rows
    )
    row_index = first_frame // row_length
    time_row = lax.dynamic_slice_in_dim(time_token, row_index, 1, 0)
    time_slice = lax.dynamic_slice_in_dim(
        time_row, lax.axis_index("tensor") * local_width, local_width, 1
    ).astype(jnp.float32)
    row_context = lax.dynamic_slice_in_dim(context, row_index, 1, 0)[0]
    context_rows = row_context.shape[0]
    tables = rotary_tables(own_positions, head_cols)
    residual = frames.astype(jnp.float32)
    score_scale = 1.0 / math.sqrt(HEAD_SIZE)
    stacked = jnp.concatenate([time_slice, residual], 0)
    normed_one, scaled_one, inverse_one = norm_forward(stacked, gain_attn, bias_attn, model_width)
    gathered_one = spread_normed(normed_one)
    time_normed = gathered_one[:1]
    frame_normed = gathered_one[1:]
    query_rows = rotate(product(frame_normed, w_query), tables).astype(jnp.bfloat16)
    own_keys = rotate(product(frame_normed, w_key), tables).astype(jnp.bfloat16)
    own_values = product(frame_normed, w_value).astype(jnp.bfloat16)
    timestep_keys = (
        product(time_normed, w_key).astype(jnp.bfloat16).reshape(number_of_heads, HEAD_SIZE)
    )
    timestep_values = (
        product(time_normed, w_value).astype(jnp.bfloat16).reshape(number_of_heads, HEAD_SIZE)
    )
    rim_blocks = with_halo(jnp.stack([own_keys, own_values]), (("seq", 1),), local_rows)
    wide_keys = rim_blocks[0].reshape(3 * local_rows, number_of_heads, HEAD_SIZE)
    wide_values = rim_blocks[1].reshape(3 * local_rows, number_of_heads, HEAD_SIZE)
    rows_per_block = min(512, local_rows)
    count_of_blocks = local_rows // rows_per_block
    query_blocks = query_rows.reshape(count_of_blocks, rows_per_block, number_of_heads, HEAD_SIZE)
    label_blocks = own_labels.reshape(count_of_blocks, rows_per_block)

    def block_scores(query_block, label_block):
        main_scores = (
            jnp.einsum("qhd,khd->hqk", query_block, wide_keys, preferred_element_type=jnp.float32)
            * score_scale
        )
        allowed = label_block[:, None] == key_labels[None, :]
        main_scores = jnp.where(allowed[None], main_scores, -1e30)
        time_scores = (
            jnp.einsum("qhd,hd->hq", query_block, timestep_keys, preferred_element_type=jnp.float32)
            * score_scale
        )
        return (main_scores, time_scores)

    def forward_block(pieces):
        main_scores, time_scores = block_scores(pieces[0], pieces[1])
        largest = jnp.maximum(jnp.max(main_scores, -1), time_scores)
        main_exp = jnp.exp(main_scores - largest[:, :, None])
        time_exp = jnp.exp(time_scores - largest)
        totals = jnp.sum(main_exp, -1) + time_exp
        main_weights = (main_exp / totals[:, :, None]).astype(jnp.bfloat16)
        time_weights = (time_exp / totals).astype(jnp.bfloat16)
        mixture = jnp.einsum(
            "hqk,khd->qhd", main_weights, wide_values, preferred_element_type=jnp.float32
        )
        mixture = mixture + jnp.einsum(
            "hq,hd->qhd", time_weights, timestep_values, preferred_element_type=jnp.float32
        )
        return (mixture, largest + jnp.log(totals))

    attended_output, log_totals = lax.map(forward_block, (query_blocks, label_blocks))
    attended_output = attended_output.reshape(local_rows, head_cols).astype(jnp.bfloat16)
    residual_one = residual + collect_branch(product(attended_output, w_out))
    normed_two, scaled_two, inverse_two = norm_forward(
        residual_one, gain_cross, bias_cross, model_width
    )
    gathered_two = spread_normed(normed_two)
    cross_queries = (
        product(gathered_two, c_query)
        .astype(jnp.bfloat16)
        .reshape(local_rows, number_of_heads, HEAD_SIZE)
    )
    cross_keys = (
        product(row_context, c_key)
        .astype(jnp.bfloat16)
        .reshape(context_rows, number_of_heads, HEAD_SIZE)
    )
    cross_values = (
        product(row_context, c_value)
        .astype(jnp.bfloat16)
        .reshape(context_rows, number_of_heads, HEAD_SIZE)
    )
    cross_scores = (
        jnp.einsum("qhd,khd->hqk", cross_queries, cross_keys, preferred_element_type=jnp.float32)
        * score_scale
    )
    cross_probs = jax.nn.softmax(cross_scores, axis=-1)
    cross_weights = cross_probs.astype(jnp.bfloat16)
    crossed = jnp.einsum(
        "hqk,khd->qhd", cross_weights, cross_values, preferred_element_type=jnp.float32
    )
    crossed = crossed.reshape(local_rows, head_cols).astype(jnp.bfloat16)
    residual_two = residual_one + collect_branch(product(crossed, c_out))
    normed_three, scaled_three, inverse_three = norm_forward(
        residual_two, gain_ffn, bias_ffn, model_width
    )
    gathered_three = spread_normed(normed_three)
    gate_pre = product(gathered_three, w_gate)
    lifted = product(gathered_three, w_up)
    hidden = (jax.nn.silu(gate_pre) * lifted).astype(jnp.bfloat16)
    residual_three = residual_two + collect_branch(product(hidden, w_down))
    block_out = residual_three.astype(jnp.bfloat16)
    grad_three = out_grad.astype(jnp.float32)
    grad_full = spread_grad(grad_three)
    grad_down = inner_rows(hidden, grad_full)
    hidden_grad = back_project(grad_full, w_down).astype(jnp.bfloat16).astype(jnp.float32)
    sigmoid_gate = jax.nn.sigmoid(gate_pre)
    gate_grad = (
        hidden_grad * lifted * sigmoid_gate * (1.0 + gate_pre * (1.0 - sigmoid_gate))
    ).astype(jnp.bfloat16)
    lifted_grad = (hidden_grad * gate_pre * sigmoid_gate).astype(jnp.bfloat16)
    grad_gate_w = inner_rows(gathered_three, gate_grad)
    grad_up_w = inner_rows(gathered_three, lifted_grad)
    normed_grad = back_project(gate_grad, w_gate) + back_project(lifted_grad, w_up)
    inputs_grad, grad_gain_ffn, grad_bias_ffn = norm_backward(
        collect_grad(normed_grad), scaled_three, inverse_three, gain_ffn, model_width
    )
    grad_two = grad_three + inputs_grad
    cross_full = spread_grad(grad_two)
    grad_c_out = inner_rows(crossed, cross_full)
    crossed_grad = (
        back_project(cross_full, c_out)
        .astype(jnp.bfloat16)
        .reshape(local_rows, number_of_heads, HEAD_SIZE)
    )
    prob_grad = jnp.einsum(
        "qhd,khd->hqk", crossed_grad, cross_values, preferred_element_type=jnp.float32
    )
    value_grad = jnp.einsum(
        "hqk,qhd->khd", cross_weights, crossed_grad, preferred_element_type=jnp.float32
    ).reshape(context_rows, head_cols)
    row_delta = jnp.sum(prob_grad * cross_probs, -1, keepdims=True)
    score_grad = (cross_probs * (prob_grad - row_delta)).astype(jnp.bfloat16)
    query_grad = (
        jnp.einsum("hqk,khd->qhd", score_grad, cross_keys, preferred_element_type=jnp.float32)
        * score_scale
    )
    query_grad = query_grad.astype(jnp.bfloat16).reshape(local_rows, head_cols)
    key_grad = (
        jnp.einsum("hqk,qhd->khd", score_grad, cross_queries, preferred_element_type=jnp.float32)
        * score_scale
    ).reshape(context_rows, head_cols)
    wide_context = row_context.astype(jnp.float32)
    grad_c_query = inner_rows(gathered_two, query_grad)
    grad_c_key = jnp.dot(wide_context.T, key_grad, precision=lax.Precision.HIGHEST)
    grad_c_value = jnp.dot(wide_context.T, value_grad, precision=lax.Precision.HIGHEST)
    inputs_grad, grad_gain_cross, grad_bias_cross = norm_backward(
        collect_grad(back_project(query_grad, c_query)),
        scaled_two,
        inverse_two,
        gain_cross,
        model_width,
    )
    grad_one = grad_two + inputs_grad
    attend_full = spread_grad(grad_one)
    grad_w_out = inner_rows(attended_output, attend_full)
    attended_grad = (
        back_project(attend_full, w_out)
        .astype(jnp.bfloat16)
        .reshape(count_of_blocks, rows_per_block, number_of_heads, HEAD_SIZE)
    )

    def backward_block(accums, pieces):
        key_acc, value_acc, time_key_acc, time_value_acc = accums
        query_block, label_block, log_block, grad_block = pieces
        main_scores, time_scores = block_scores(query_block, label_block)
        main_probs = jnp.exp(main_scores - log_block[:, :, None])
        time_probs = jnp.exp(time_scores - log_block)
        main_grad = jnp.einsum(
            "qhd,khd->hqk", grad_block, wide_values, preferred_element_type=jnp.float32
        )
        time_grad = jnp.einsum(
            "qhd,hd->hq", grad_block, timestep_values, preferred_element_type=jnp.float32
        )
        value_acc = value_acc + jnp.einsum(
            "hqk,qhd->khd",
            main_probs.astype(jnp.bfloat16),
            grad_block,
            preferred_element_type=jnp.float32,
        )
        time_value_acc = time_value_acc + jnp.einsum(
            "hq,qhd->hd",
            time_probs.astype(jnp.bfloat16),
            grad_block,
            preferred_element_type=jnp.float32,
        )
        block_delta = jnp.sum(main_grad * main_probs, -1) + time_grad * time_probs
        main_change = (main_probs * (main_grad - block_delta[:, :, None])).astype(jnp.bfloat16)
        time_change = (time_probs * (time_grad - block_delta)).astype(jnp.bfloat16)
        block_query = jnp.einsum(
            "hqk,khd->qhd", main_change, wide_keys, preferred_element_type=jnp.float32
        )
        block_query = (
            block_query
            + jnp.einsum(
                "hq,hd->qhd", time_change, timestep_keys, preferred_element_type=jnp.float32
            )
        ) * score_scale
        key_acc = (
            key_acc
            + jnp.einsum(
                "hqk,qhd->khd", main_change, query_block, preferred_element_type=jnp.float32
            )
            * score_scale
        )
        time_key_acc = (
            time_key_acc
            + jnp.einsum("hq,qhd->hd", time_change, query_block, preferred_element_type=jnp.float32)
            * score_scale
        )
        return ((key_acc, value_acc, time_key_acc, time_value_acc), block_query)

    wide_zeros = jnp.zeros((3 * local_rows, number_of_heads, HEAD_SIZE), jnp.float32)
    head_zeros = jnp.zeros((number_of_heads, HEAD_SIZE), jnp.float32)
    accums, query_grads = lax.scan(
        backward_block,
        (wide_zeros, wide_zeros, head_zeros, head_zeros),
        (query_blocks, label_blocks, log_totals, attended_grad),
    )
    wide_grads = jnp.stack([accums[0], accums[1]]).reshape(2, 3 * local_rows, head_cols)
    from_next = from_behind(wide_grads[:, :local_rows].astype(jnp.bfloat16), "seq", -1).astype(
        jnp.float32
    )
    from_prev = from_behind(wide_grads[:, 2 * local_rows :].astype(jnp.bfloat16), "seq", 1).astype(
        jnp.float32
    )
    own_grads = wide_grads[:, local_rows : 2 * local_rows] + from_next + from_prev
    query_raw = rotate_back(query_grads.reshape(local_rows, head_cols), tables).astype(jnp.bfloat16)
    key_raw = rotate_back(own_grads[0], tables).astype(jnp.bfloat16)
    value_raw = own_grads[1].astype(jnp.bfloat16)
    time_key_grad = accums[2].reshape(1, head_cols)
    time_value_grad = accums[3].reshape(1, head_cols)
    time_wide = time_normed.astype(jnp.float32)
    grad_w_query = inner_rows(frame_normed, query_raw)
    grad_w_key = inner_rows(frame_normed, key_raw) + jnp.dot(
        time_wide.T, time_key_grad, precision=lax.Precision.HIGHEST
    )
    grad_w_value = inner_rows(frame_normed, value_raw) + jnp.dot(
        time_wide.T, time_value_grad, precision=lax.Precision.HIGHEST
    )
    frame_grad = (
        back_project(query_raw, w_query)
        + back_project(key_raw, w_key)
        + back_project(value_raw, w_value)
    )
    time_grad = jnp.dot(time_key_grad, w_key.astype(jnp.float32).T, precision=lax.Precision.HIGHEST)
    time_grad = time_grad + jnp.dot(
        time_value_grad, w_value.astype(jnp.float32).T, precision=lax.Precision.HIGHEST
    )
    inputs_grad, grad_gain_attn, grad_bias_attn = norm_backward(
        collect_grad(jnp.concatenate([time_grad, frame_grad], 0)),
        scaled_one,
        inverse_one,
        gain_attn,
        model_width,
    )
    input_grad = grad_one + inputs_grad[1:]
    summed = (
        lax.psum_scatter(grad_gain_attn, "seq", scatter_dimension=0, tiled=True),
        lax.psum_scatter(grad_bias_attn, "seq", scatter_dimension=0, tiled=True),
        lax.psum_scatter(grad_gain_cross, "seq", scatter_dimension=0, tiled=True),
        lax.psum_scatter(grad_bias_cross, "seq", scatter_dimension=0, tiled=True),
        lax.psum_scatter(grad_gain_ffn, "seq", scatter_dimension=0, tiled=True),
        lax.psum_scatter(grad_bias_ffn, "seq", scatter_dimension=0, tiled=True),
        lax.psum_scatter(grad_w_query, "seq", scatter_dimension=0, tiled=True),
        lax.psum_scatter(grad_w_key, "seq", scatter_dimension=0, tiled=True),
        lax.psum_scatter(grad_w_value, "seq", scatter_dimension=0, tiled=True),
        lax.psum_scatter(grad_w_out, "seq", scatter_dimension=0, tiled=True),
        lax.psum_scatter(grad_c_query, "seq", scatter_dimension=0, tiled=True),
        lax.psum_scatter(grad_c_key, "seq", scatter_dimension=0, tiled=True),
        lax.psum_scatter(grad_c_value, "seq", scatter_dimension=0, tiled=True),
        lax.psum_scatter(grad_c_out, "seq", scatter_dimension=0, tiled=True),
        lax.psum_scatter(grad_gate_w, "seq", scatter_dimension=0, tiled=True),
        lax.psum_scatter(grad_up_w, "seq", scatter_dimension=0, tiled=True),
        lax.psum_scatter(grad_down, "seq", scatter_dimension=0, tiled=True),
    )
    return (
        block_out,
        input_grad,
        summed[0],
        summed[1],
        summed[2],
        summed[3],
        summed[4],
        summed[5],
        summed[6],
        summed[7],
        summed[8],
        summed[9],
        summed[10],
        summed[11],
        summed[12],
        summed[13],
        summed[14],
        summed[15],
        summed[16],
    )


def solution(mesh):
    return jax.shard_map(
        per_device,
        mesh=mesh,
        in_specs=(
            P("seq", "tensor"),
            P(),
            P(),
            P(),
            P("tensor"),
            P("tensor"),
            P("tensor"),
            P("tensor"),
            P("tensor"),
            P("tensor"),
            P(None, "tensor"),
            P(None, "tensor"),
            P(None, "tensor"),
            P("tensor", None),
            P(None, "tensor"),
            P(None, "tensor"),
            P(None, "tensor"),
            P("tensor", None),
            P(None, "tensor"),
            P(None, "tensor"),
            P("tensor", None),
            P("seq", "tensor"),
        ),
        out_specs=(
            P("seq", "tensor"),
            P("seq", "tensor"),
            P(("tensor", "seq")),
            P(("tensor", "seq")),
            P(("tensor", "seq")),
            P(("tensor", "seq")),
            P(("tensor", "seq")),
            P(("tensor", "seq")),
            P("seq", "tensor"),
            P("seq", "tensor"),
            P("seq", "tensor"),
            P(("tensor", "seq"), None),
            P("seq", "tensor"),
            P("seq", "tensor"),
            P("seq", "tensor"),
            P(("tensor", "seq"), None),
            P("seq", "tensor"),
            P("seq", "tensor"),
            P(("tensor", "seq"), None),
        ),
        check_vma=False,
    )
```

profile of v0, /device:TPU:0, one launch (start us, length us, event | category | flops | bytes accessed | tf_op | source)
XLA Modules:
  0.0 1648.6 jit_solution(11281341005138984822)
XLA Ops:
  9.5 8.5 all-reduce.12
  22.2 17.4 %all-gather.7.cloned.1.call-done = bf16[513,1536]{1,0:T(8,128)(2,1)} async-done(((bf16[513,384]{1,0:T(8,128)(2,1)}), bf16[513,1536]{1,0:T(8,128)(2,1)}) %all-gather.7.cloned.1.call-update) | async-done | bytes 1575952 | tf_op jit(solution)/shard_map/all_gather | solution.py:107
  47.4 5.6 collective-permute-start
  55.8 12.2 collective-permute-done.1
  68.0 16.7 %collective-permute-done = bf16[2,512,384]{1,2,0:T(8,128)(2,1)} collective-permute-done((bf16[2,512,384]{1,2,0:T(8,128)(2,1)}, bf16[2,512,384]{1,2,0:T(8,128)(2,1)}, u32[]{:S(2)}, u32[]{:S(2)}) %collective-permute-start) | collective-permute-done | bytes 786464 | tf_op jit(solution)/shard_map/ppermute | solution.py:20
  86.5 8.3 fusion.129
  94.8 9.0 fusion.1
  104.5 8.4 fusion.23
  116.3 28.4 %reduce-scatter.52.cloned.1.call-done = bf16[384,512]{1,0:T(8,128)(2,1)} async-done(((bf16[1536,512]{1,0:T(8,128)(2,1)}), bf16[384,512]{1,0:T(8,128)(2,1)}) %reduce-scatter.52.cloned.1.call-update) | async-done | bytes 393232
  146.2 5.8 all-reduce.11
  161.3 13.2 all-gather.9.cloned.1.call-done
  174.5 3.0 convolution_convert_fusion.8
  185.2 27.6 %reduce-scatter.54.cloned.1.call-done = bf16[384,512]{1,0:T(8,128)(2,1)} async-done(((bf16[1536,512]{1,0:T(8,128)(2,1)}), bf16[384,512]{1,0:T(8,128)(2,1)}) %reduce-scatter.54.cloned.1.call-update) | async-done | bytes 393232
  214.3 5.8 all-reduce.10
  221.2 12.7 all-gather.13.cloned.1.call-done
  233.9 6.6 convolution_convert_fusion.1
  240.5 15.0 all-gather.11.cloned.1.call-done
  255.6 5.1 fusion.132
  260.7 7.9 fusion.10
  269.8 3.7 convolution_convert_fusion.2
  273.4 2.6 copy.81
  276.2 5.1 fusion.133
  281.3 6.4 fusion.13
  287.8 2.6 copy.83
  290.6 13.8 reduce-scatter.56.cloned.1.call-done
  306.4 29.0 %reduce-scatter.58.cloned.1.call-done = bf16[384,512]{1,0:T(8,128)(2,1)} async-done(((bf16[1536,512]{1,0:T(8,128)(2,1)}), bf16[384,512]{1,0:T(8,128)(2,1)}) %reduce-scatter.58.cloned.1.call-update) | async-done | bytes 393232
  338.3 6.4 all-reduce.9
  345.4 2.6 fusion.125
  348.1 20.8 %all-gather.15.cloned.1.call-done = bf16[512,1536]{1,0:T(8,128)(2,1)} async-done(((bf16[512,384]{1,0:T(8,128)(2,1)}), bf16[512,1536]{1,0:T(8,128)(2,1)}) %all-gather.15.cloned.1.call-update) | async-done | bytes 1572880 | tf_op jit(solution)/shard_map/all_gather | solution.py:117
  368.9 2.6 convolution_convert_fusion.7
  377.4 28.3 %reduce-scatter.60.cloned.1.call-done = bf16[384,512]{1,0:T(8,128)(2,1)} async-done(((bf16[1536,512]{1,0:T(8,128)(2,1)}), bf16[384,512]{1,0:T(8,128)(2,1)}) %reduce-scatter.60.cloned.1.call-update) | async-done | bytes 393232
  407.9 5.7 all-reduce.8
  416.5 19.5 %all-gather.17.cloned.1.call-done = bf16[512,1536]{1,0:T(8,128)(2,1)} async-done(((bf16[512,384]{1,0:T(8,128)(2,1)}), bf16[512,1536]{1,0:T(8,128)(2,1)}) %all-gather.17.cloned.1.call-update) | async-done | bytes 1572880 | tf_op jit(solution)/shard_map/all_gather | solution.py:117
  438.5 8.2 fusion.3
  446.7 12.8 multiply_reduce_fusion
  461.7 2.9 convolution_reduce_fusion
  466.4 12.9 multiply_convert_fusion
  479.4 3.7 convolution_multiply_fusion
  489.0 4.8 collective-permute-start.3
  493.9 2.9 fusion.20
  496.8 12.4 collective-permute-done.2
  509.2 16.7 %collective-permute-done.3 = bf16[2,512,384]{1,2,0:T(8,128)(2,1)S(1)} collective-permute-done((bf16[2,512,384]{1,2,0:T(8,128)(2,1)S(1)}, bf16[2,512,384]{1,2,0:T(8,128)(2,1)S(1)}, u32[]{:S(2)}, u32[]{:S(2)}) %collective-permute-start.3) | collective-permute-done | bytes 786464 | tf_op jit(solution)/shard_map/ppermute | solution.py:32
  539.8 3.8 copy.87
  549.7 2.7 fusion.71
  552.5 3.7 fusion.138
  557.2 3.9 fusion.137
  562.1 3.6 fusion.136
  566.6 4.0 convolution_add_fusion.4
  571.4 4.0 convolution_add_fusion.3
  580.8 7.6 fusion.116
  588.5 6.4 fusion.139
  596.3 6.5 fusion.140
  606.5 35.8 %all-reduce.6 = (f32[384]{0:T(512)S(1)}, f32[384]{0:T(512)S(1)}, f32[384]{0:T(512)S(1)}, f32[384]{0:T(512)S(1)}, f32[384]{0:T(512)S(1)}, /*index=5*/f32[384]{0:T(512)S(1)}) all-reduce(f32[384]{0:T(512)S(1)} %get-tuple-element.79, f32[384]{0:T(512)S(1)} %get-tuple-element.107, ...), channel_id=8, replica_groups=mesh['tensor'=4,'seq'=8] {'seq'}, use_global_device_ids=true, to_apply=%region_39.40.clone | all-reduce | flops 2304 | bytes 18432
  645.8 5.8 all-reduce.7
  654.2 55.4 %reduce-scatter.40.cloned.1.call-done = f32[96,384]{1,0:T(8,128)} async-done(((f32[768,384]{1,0:T(8,128)}), f32[96,384]{1,0:T(8,128)}) %reduce-scatter.40.cloned.1.call-update) | async-done | bytes 147472 | tf_op jit(solution)/shard_map/reduce_scatter | solution.py:435
  709.6 71.8 %reduce-scatter.44.cloned.1.call-done = f32[48,1536]{1,0:T(8,128)} async-done(((f32[384,1536]{1,0:T(8,128)}), f32[48,1536]{1,0:T(8,128)}) %reduce-scatter.44.cloned.1.call-update) | async-done | bytes 294928 | tf_op jit(solution)/shard_map/reduce_scatter | solution.py:437
  781.4 72.0 %reduce-scatter.38.cloned.1.call-done = f32[192,384]{1,0:T(8,128)} async-done(((f32[1536,384]{1,0:T(8,128)}), f32[192,384]{1,0:T(8,128)}) %reduce-scatter.38.cloned.1.call-update) | async-done | bytes 294928 | tf_op jit(solution)/shard_map/reduce_scatter | solution.py:434
  853.4 72.0 %reduce-scatter.36.cloned.1.call-done = f32[48,1536]{1,0:T(8,128)} async-done(((f32[384,1536]{1,0:T(8,128)}), f32[48,1536]{1,0:T(8,128)}) %reduce-scatter.36.cloned.1.call-update) | async-done | bytes 294928 | tf_op jit(solution)/shard_map/reduce_scatter | solution.py:433
  925.4 72.0 %reduce-scatter.32.cloned.1.call-done = f32[192,384]{1,0:T(8,128)} async-done(((f32[1536,384]{1,0:T(8,128)}), f32[192,384]{1,0:T(8,128)}) %reduce-scatter.32.cloned.1.call-update) | async-done | bytes 294928 | tf_op jit(solution)/shard_map/reduce_scatter | solution.py:431
  997.4 72.1 %reduce-scatter.34.cloned.1.call-done = f32[192,384]{1,0:T(8,128)} async-done(((f32[1536,384]{1,0:T(8,128)}), f32[192,384]{1,0:T(8,128)}) %reduce-scatter.34.cloned.1.call-update) | async-done | bytes 294928 | tf_op jit(solution)/shard_map/reduce_scatter | solution.py:432
  1069.5 71.9 %reduce-scatter.30.cloned.1.call-done = f32[192,384]{1,0:T(8,128)} async-done(((f32[1536,384]{1,0:T(8,128)}), f32[192,384]{1,0:T(8,128)}) %reduce-scatter.30.cloned.1.call-update) | async-done | bytes 294928 | tf_op jit(solution)/shard_map/reduce_scatter | solution.py:430
  1141.4 166.7 %reduce-scatter.48.cloned.1.call-done = f32[192,1536]{1,0:T(8,128)} async-done(((f32[1536,1536]{1,0:T(8,128)}), f32[192,1536]{1,0:T(8,128)}) %reduce-scatter.48.cloned.1.call-update) | async-done | bytes 1179664 | tf_op jit(solution)/shard_map/reduce_scatter | solution.py:439
  1308.1 166.7 %reduce-scatter.46.cloned.1.call-done = f32[192,1536]{1,0:T(8,128)} async-done(((f32[1536,1536]{1,0:T(8,128)}), f32[192,1536]{1,0:T(8,128)}) %reduce-scatter.46.cloned.1.call-update) | async-done | bytes 1179664 | tf_op jit(solution)/shard_map/reduce_scatter | solution.py:438
  1474.9 166.7 %reduce-scatter.50.cloned.1.call-done = f32[192,1536]{1,0:T(8,128)} async-done(((f32[1536,1536]{1,0:T(8,128)}), f32[192,1536]{1,0:T(8,128)}) %reduce-scatter.50.cloned.1.call-update) | async-done | bytes 1179664 | tf_op jit(solution)/shard_map/reduce_scatter | solution.py:440
  (371 shorter events, 113.1 us)
Async XLA Ops:
  7.2 34.8 %copy-start = (bf16[1536,384]{1,0:T(8,128)(2,1)S(1)}, bf16[1536,384]{1,0:T(8,128)(2,1)}, u32[]{:S(2)}) copy-start(bf16[1536,384]{1,0:T(8,128)(2,1)} %param.33) | copy-start | bytes 3538948
  7.2 10.8 copy-start.79
  7.2 10.8 copy-start.82
  7.2 32.4 %all-gather.7.cloned.1.call-start = ((), (), s32[]{:S(2)}) async-start(), calls=%async_computation.17 | async-start | bytes 1996800 | tf_op jit(solution)/shard_map/all_gather | solution.py:107
  9.2 10.2 copy-start.53
  18.0 21.6 %copy-start.43 = (bf16[1536,384]{1,0:T(8,128)(2,1)S(1)}, bf16[1536,384]{1,0:T(8,128)(2,1)}, u32[]{:S(2)}) copy-start(bf16[1536,384]{1,0:T(8,128)(2,1)} %param.32) | copy-start | bytes 3538948
  19.4 125.3 %reduce-scatter.52.cloned.1.call-start = ((), (), s32[]{:S(2)}) async-start(), calls=%async_computation.34 | async-start | bytes 1966080
  21.8 21.0 %copy-start.41 = (f32[512,2,32]{0,2,1:T(8,128)}, f32[512,2,32]{0,2,1:T(8,128)S(1)}, u32[]{:S(2)}) copy-start(f32[512,2,32]{0,2,1:T(8,128)S(1)} %pad_maximum_fusion.5) | copy-start | bytes 393220
  22.2 20.9 %copy-start.45 = (f32[512,32]{0,1:T(8,128)}, f32[512,32]{0,1:T(8,128)S(1)}, u32[]{:S(2)}) copy-start(f32[512,32]{0,1:T(8,128)S(1)} %multiply_cosine_fusion) | copy-start | bytes 196612
  44.3 42.1 %copy-start.16 = (bf16[512,384]{0,1:T(8,128)(2,1)}, bf16[512,384]{0,1:T(8,128)(2,1)S(1)}, u32[]{:S(2)}) copy-start(bf16[512,384]{0,1:T(8,128)(2,1)S(1)} %get-tuple-element.160) | copy-start | bytes 1179652
  46.1 21.9 %collective-permute-start.1 = (bf16[2,512,384]{1,2,0:T(8,128)(2,1)}, bf16[2,512,384]{1,2,0:T(8,128)(2,1)}, u32[]{:S(2)}, u32[]{:S(2)}) collective-permute-start(bf16[2,512,384]{1,2,0:T(8,128)(2,1)} %pad_maximum_fusion.4), channel_id=1, source_target_pairs={{1,0},{2,1},{3,2},{4,3},{5,4},{6,5},{7,6},{9,8},{10,9},{11,10},{12... | collective-permute-start | bytes 2359304 | tf_op jit(solution)/shard_map/ppermute | solution.py:22
  47.4 37.3 %collective-permute-start = (bf16[2,512,384]{1,2,0:T(8,128)(2,1)}, bf16[2,512,384]{1,2,0:T(8,128)(2,1)}, u32[]{:S(2)}, u32[]{:S(2)}) collective-permute-start(bf16[2,512,384]{1,2,0:T(8,128)(2,1)} %pad_maximum_fusion.4), channel_id=1, source_target_pairs={{0,1},{1,2},{2,3},{3,4},{4,5},{5,6},{6,7},{8,9},{9,10},{10,11},{11... | collective-permute-start | bytes 2359304 | tf_op jit(solution)/shard_map/ppermute | solution.py:20
  55.6 29.2 %copy-start.72 = (bf16[384]{0:T(512)(128)(2,1)}, bf16[384]{0:T(512)(128)(2,1)S(1)}, u32[]{:S(2)}) copy-start(bf16[384]{0:T(512)(128)(2,1)S(1)} %convolution_reduce_fusion.3) | copy-start | bytes 2308
  55.8 38.9 %copy-start.47 = (f32[6,1,512]{2,1,0:T(1,128)}, f32[6,1,512]{2,1,0:T(1,128)S(1)}, u32[]{:S(2)}) copy-start(f32[6,1,512]{2,1,0:T(1,128)S(1)} %fusion.131) | copy-start | bytes 36868
  86.4 18.0 %copy-start.18 = (bf16[1,1536,384]{1,2,0:T(8,128)(2,1)}, bf16[1,1536,384]{1,2,0:T(8,128)(2,1)S(1)}, u32[]{:S(2)}) copy-start(bf16[1,1536,384]{1,2,0:T(8,128)(2,1)S(1)} %get-tuple-element.151) | copy-start | bytes 3538948
  94.7 9.0 copy-start.48
  94.7 9.7 copy-start.81
  104.4 9.1 copy-start.40
  116.2 29.7 %copy-start.4 = (bf16[512,384]{1,0:T(8,128)(2,1)S(1)}, bf16[512,384]{1,0:T(8,128)(2,1)}, u32[]{:S(2)}) copy-start(bf16[512,384]{1,0:T(8,128)(2,1)} %param.22) | copy-start | bytes 1179652
  116.2 36.4 %copy-start.65 = (f32[384]{0:T(512)S(1)}, f32[384]{0:T(512)}, u32[]{:S(2)}) copy-start(f32[384]{0:T(512)} %param.28) | copy-start | bytes 4612
  116.2 36.4 %copy-start.83 = (f32[384]{0:T(512)S(1)}, f32[384]{0:T(512)}, u32[]{:S(2)}) copy-start(f32[384]{0:T(512)} %param.29) | copy-start | bytes 4612
  116.2 58.3 %all-gather.9.cloned.1.call-start = ((), (), s32[]{:S(2)}) async-start(), calls=%async_computation.18 | async-start | bytes 1966080 | tf_op jit(solution)/shard_map/all_gather | solution.py:107
  144.7 9.4 copy-start.31
  153.6 20.9 %copy-start.38 = (bf16[1536,384]{1,0:T(8,128)(2,1)S(1)}, bf16[1536,384]{1,0:T(8,128)(2,1)}, u32[]{:S(2)}) copy-start(bf16[1536,384]{1,0:T(8,128)(2,1)} %param.36) | copy-start | bytes 3538948
  153.6 59.2 %reduce-scatter.54.cloned.1.call-start = ((), (), s32[]{:S(2)}) async-start(), calls=%async_computation.35 | async-start | bytes 1966080
  184.5 35.6 %copy-start.64 = (f32[384]{0:T(512)S(1)}, f32[384]{0:T(512)}, u32[]{:S(2)}) copy-start(f32[384]{0:T(512)} %param.30) | copy-start | bytes 4612
  184.5 35.6 %copy-start.84 = (f32[384]{0:T(512)S(1)}, f32[384]{0:T(512)}, u32[]{:S(2)}) copy-start(f32[384]{0:T(512)} %param.31) | copy-start | bytes 4612
  184.6 49.4 %all-gather.13.cloned.1.call-start = ((), (), s32[]{:S(2)}) async-start(), calls=%async_computation.20 | async-start | bytes 1966080 | tf_op jit(solution)/shard_map/all_gather | solution.py:117
  185.1 70.4 %all-gather.11.cloned.1.call-start = ((), (), s32[]{:S(2)}) async-start(), calls=%async_computation.19 | async-start | bytes 1966080 | tf_op jit(solution)/shard_map/all_gather | solution.py:107
  220.1 20.4 %copy-start.55 = (f32[512,1]{0,1:T(1,128)}, f32[512,1]{0,1:T(1,128)S(1)}, u32[]{:S(2)}) copy-start(f32[512,1]{0,1:T(1,128)S(1)} %get-tuple-element.165) | copy-start | bytes 6148
  220.1 20.4 %copy-start.56 = (f32[512,1]{0,1:T(1,128)}, f32[512,1]{0,1:T(1,128)S(1)}, u32[]{:S(2)}) copy-start(f32[512,1]{0,1:T(1,128)S(1)} %get-tuple-element.166) | copy-start | bytes 6148
  221.1 83.3 %reduce-scatter.56.cloned.1.call-start = ((), (), s32[]{:S(2)}) async-start(), calls=%async_computation.36 | async-start | bytes 1966080
  255.6 14.2 slice-start
  260.7 9.1 slice-start.1
  276.1 59.2 %reduce-scatter.58.cloned.1.call-start = ((), (), s32[]{:S(2)}) async-start(), calls=%async_computation.37 | async-start | bytes 1966080
  290.4 55.1 %copy-start.28 = (bf16[512,384]{1,0:T(8,128)(2,1)S(1)}, bf16[512,384]{1,0:T(8,128)(2,1)}, u32[]{:S(2)}) copy-start(bf16[512,384]{1,0:T(8,128)(2,1)} %param.43) | copy-start | bytes 1179652
  290.4 78.5 %all-gather.15.cloned.1.call-start = ((), (), s32[]{:S(2)}) async-start(), calls=%async_computation.21 | async-start | bytes 1966080 | tf_op jit(solution)/shard_map/all_gather | solution.py:117
  348.0 23.5 %copy-start.30 = (f32[6,512,128]{1,2,0:T(8,128)S(1)}, f32[6,512,128]{1,2,0:T(8,128)}, u32[]{:S(2)}) copy-start(f32[6,512,128]{1,2,0:T(8,128)} %copy-done.29) | copy-start | bytes 4718596
  348.1 57.6 %reduce-scatter.60.cloned.1.call-start = ((), (), s32[]{:S(2)}) async-start(), calls=%async_computation.38 | async-start | bytes 1966080
  377.3 29.6 %copy-start.59 = (f32[512,1]{0,1:T(1,128)S(1)}, f32[512,1]{0,1:T(1,128)}, u32[]{:S(2)}) copy-start(f32[512,1]{0,1:T(1,128)} %copy-done.58) | copy-start | bytes 6148
  377.3 29.6 %copy-start.61 = (f32[512,1]{0,1:T(1,128)S(1)}, f32[512,1]{0,1:T(1,128)}, u32[]{:S(2)}) copy-start(f32[512,1]{0,1:T(1,128)} %copy-done.60) | copy-start | bytes 6148
  377.3 29.6 %copy-start.66 = (f32[384]{0:T(512)S(1)}, f32[384]{0:T(512)}, u32[]{:S(2)}) copy-start(f32[384]{0:T(512)} %param.28) | copy-start | bytes 4612
  377.3 36.4 %copy-start.23 = (f32[512,384]{1,0:T(8,128)S(1)}, f32[512,384]{1,0:T(8,128)}, u32[]{:S(2)}) copy-start(f32[512,384]{1,0:T(8,128)} %get-tuple-element.140) | copy-start | bytes 2359300
  377.3 58.6 %all-gather.17.cloned.1.call-start = ((), (), s32[]{:S(2)}) async-start(), calls=%async_computation.22 | async-start | bytes 1966080 | tf_op jit(solution)/shard_map/all_gather | solution.py:117
  415.1 189.7 %reduce-scatter.62.cloned.1.call-start = ((), (), s32[]{:S(2)}) async-start(), calls=%async_computation.39 | async-start | bytes 2457600
  438.5 21.0 %copy-start.20 = (bf16[512,384]{0,1:T(8,128)(2,1)}, bf16[512,384]{0,1:T(8,128)(2,1)S(1)}, u32[]{:S(2)}) copy-start(bf16[512,384]{0,1:T(8,128)(2,1)S(1)} %convolution_convert_fusion.6) | copy-start | bytes 1179652
  446.7 12.8 copy-start.78
  466.4 12.9 copy-start.17
  483.9 9.9 copy-start.8
  487.4 21.8 %collective-permute-start.2 = (bf16[2,512,384]{1,2,0:T(8,128)(2,1)S(1)}, bf16[2,512,384]{1,2,0:T(8,128)(2,1)S(1)}, u32[]{:S(2)}, u32[]{:S(2)}) collective-permute-start(bf16[2,512,384]{1,2,0:T(8,128)(2,1)S(1)} %get-tuple-element.148), channel_id=1, source_target_pairs={{1,0},{2,1},{3,2},{4,3},{5,4},{6,5},{7,6},{9,8},{10,9},{11,10},{12... | collective-permute-start | bytes 2359304 | tf_op jit(solution)/shard_map/ppermute | solution.py:32
  489.0 37.0 %collective-permute-start.3 = (bf16[2,512,384]{1,2,0:T(8,128)(2,1)S(1)}, bf16[2,512,384]{1,2,0:T(8,128)(2,1)S(1)}, u32[]{:S(2)}, u32[]{:S(2)}) collective-permute-start(bf16[2,512,384]{1,2,0:T(8,128)(2,1)S(1)} %get-tuple-element.149), channel_id=1, source_target_pairs={{0,1},{1,2},{2,3},{3,4},{4,5},{5,6},{6,7},{8,9},{9,10},{10,11},{11... | collective-permute-start | bytes 2359304 | tf_op jit(solution)/shard_map/ppermute | solution.py:32
  493.9 32.1 %copy-start.3 = (f32[6,64,1536]{2,1,0:T(8,128)S(1)}, f32[6,64,1536]{2,1,0:T(8,128)}, u32[]{:S(2)}) copy-start(f32[6,64,1536]{2,1,0:T(8,128)} %convolution_multiply_fusion) | copy-start | bytes 7077892
  496.8 29.6 %copy-start.14 = (f32[6,64,512]{2,1,0:T(8,128)}, f32[6,64,512]{2,1,0:T(8,128)S(1)}, u32[]{:S(2)}) copy-start(f32[6,64,512]{2,1,0:T(8,128)S(1)} %fusion.20) | copy-start | bytes 2359300
  543.6 110.6 %reduce-scatter.42.cloned.1.call-start = ((), (), s32[]{:S(2)}) async-start(), calls=%async_computation.29 | async-start | bytes 1327104 | tf_op jit(solution)/shard_map/reduce_scatter | solution.py:436
  548.2 161.4 %reduce-scatter.40.cloned.1.call-start = ((), (), s32[]{:S(2)}) async-start(), calls=%async_computation.28 | async-start | bytes 1327104 | tf_op jit(solution)/shard_map/reduce_scatter | solution.py:435
  552.4 229.0 %reduce-scatter.44.cloned.1.call-start = ((), (), s32[]{:S(2)}) async-start(), calls=%async_computation.30 | async-start | bytes 2654208 | tf_op jit(solution)/shard_map/reduce_scatter | solution.py:437
  556.2 297.2 %reduce-scatter.38.cloned.1.call-start = ((), (), s32[]{:S(2)}) async-start(), calls=%async_computation.27 | async-start | bytes 2654208 | tf_op jit(solution)/shard_map/reduce_scatter | solution.py:434
  561.1 364.3 %reduce-scatter.36.cloned.1.call-start = ((), (), s32[]{:S(2)}) async-start(), calls=%async_computation.26 | async-start | bytes 2654208 | tf_op jit(solution)/shard_map/reduce_scatter | solution.py:433
  565.7 431.8 %reduce-scatter.32.cloned.1.call-start = ((), (), s32[]{:S(2)}) async-start(), calls=%async_computation.24 | async-start | bytes 2654208 | tf_op jit(solution)/shard_map/reduce_scatter | solution.py:431
  570.7 498.9 %reduce-scatter.34.cloned.1.call-start = ((), (), s32[]{:S(2)}) async-start(), calls=%async_computation.25 | async-start | bytes 2654208 | tf_op jit(solution)/shard_map/reduce_scatter | solution.py:432
  575.5 566.0 %reduce-scatter.30.cloned.1.call-start = ((), (), s32[]{:S(2)}) async-start(), calls=%async_computation.23 | async-start | bytes 2654208 | tf_op jit(solution)/shard_map/reduce_scatter | solution.py:430
  579.4 728.7 %reduce-scatter.48.cloned.1.call-start = ((), (), s32[]{:S(2)}) async-start(), calls=%async_computation.32 | async-start | bytes 10616832 | tf_op jit(solution)/shard_map/reduce_scatter | solution.py:439
  588.4 886.4 %reduce-scatter.46.cloned.1.call-start = ((), (), s32[]{:S(2)}) async-start(), calls=%async_computation.31 | async-start | bytes 10616832 | tf_op jit(solution)/shard_map/reduce_scatter | solution.py:438
  595.0 1046.6 %reduce-scatter.50.cloned.1.call-start = ((), (), s32[]{:S(2)}) async-start(), calls=%async_computation.33 | async-start | bytes 10616832 | tf_op jit(solution)/shard_map/reduce_scatter | solution.py:440
  (63 other events, 171.0 us)
Sparse Core Ops, SparseCore 0:
  19.5 20.0 all-gather.6
  116.3 28.2 reduce-scatter.51
  153.7 20.7 all-gather.8
  184.6 28.1 reduce-scatter.53
  214.2 19.6 all-gather.12
  235.9 19.6 all-gather.10
  276.2 28.1 reduce-scatter.55
  307.1 28.1 reduce-scatter.57
  348.2 20.7 all-gather.14
  377.4 28.1 reduce-scatter.59
  415.2 20.7 all-gather.16
  543.7 30.7 reduce-scatter.61
  578.5 64.0 reduce-scatter.41
  646.4 63.1 reduce-scatter.39
  713.5 67.8 reduce-scatter.43
  785.4 68.0 reduce-scatter.37
  857.4 68.0 reduce-scatter.35
  929.4 68.0 reduce-scatter.31
  1001.5 67.9 reduce-scatter.33
  1073.5 67.9 reduce-scatter.29
  1145.6 162.4 reduce-scatter.47
  1312.3 162.5 reduce-scatter.45
  1479.0 162.5 reduce-scatter.49
where the time goes:
time: 1650 us
  waiting for transfers between devices  1270 us (77%)
  matrix products  162 us (10%)
  blocking collectives  73.8 us (4%)
  local copies, waits for them, and re-layouts  54.7 us (3%)
  other arithmetic  53.9 us (3%)
  between operations  16.5 us (1%)
    reduce_scatter x1, waiting for transfers between devices, per_device(): lax.psum_scatter(grad_down, 'seq', scatter_dimension=0, tiled=True)  167 us
    reduce_scatter x1, waiting for transfers between devices, per_device(): lax.psum_scatter(grad_gate_w, 'seq', scatter_dimension=0, tiled=True)  167 us
    reduce_scatter x1, waiting for transfers between devices, per_device(): lax.psum_scatter(grad_up_w, 'seq', scatter_dimension=0, tiled=True)  167 us
    unnamed x29, waiting for transfers between devices  128 us
    reduce_scatter x1, waiting for transfers between devices, per_device(): lax.psum_scatter(grad_w_value, 'seq', scatter_dimension=0, tiled=True)  72.1 us
    reduce_scatter x1, waiting for transfers between devices, per_device(): lax.psum_scatter(grad_c_query, 'seq', scatter_dimension=0, tiled=True)  72 us
    reduce_scatter x1, waiting for transfers between devices, per_device(): lax.psum_scatter(grad_w_key, 'seq', scatter_dimension=0, tiled=True)  72 us
    reduce_scatter x1, waiting for transfers between devices, per_device(): lax.psum_scatter(grad_w_out, 'seq', scatter_dimension=0, tiled=True)  72 us
  transfers between devices with their start and end apart: 27, of which 25 were waited for; matrix products, arithmetic and copies ran while one was open for 6% of the time, Pallas kernels for 0%

commit v1 on v0

v1 whole, which is shorter than its diff:
```python
import math

import jax
import jax.numpy as jnp
from jax import lax
from jax.experimental import pallas as pl
from jax.experimental.pallas import tpu as pltpu
from jax.sharding import PartitionSpec as P

HEAD_SIZE = 64
ROW_MIN = 2048
TILE = 256
GROUP = 3
BF16 = jnp.bfloat16
F32 = jnp.float32


def after(value, token):
    return lax.optimization_barrier((value, token))[0]


def swap(value, axis, by):
    return lax.ppermute(value, axis, [(i, i ^ by) for i in range(lax.axis_size(axis))])


def shift(value, axis, by):
    peers = lax.axis_size(axis)
    pairs = [(i, i + by) for i in range(peers) if 0 <= i + by < peers]
    return lax.ppermute(value, axis, pairs)


def tensor_place():
    place = lax.axis_index("tensor")
    return place // 2, place % 2


def ordered(own, far, mate, far_mate, axis):
    side, core = tensor_place()
    near = (jnp.where(core == 0, own, mate), jnp.where(core == 0, mate, own))
    away = (jnp.where(core == 0, far, far_mate), jnp.where(core == 0, far_mate, far))
    low = [jnp.where(side == 0, n, a) for n, a in zip(near, away)]
    high = [jnp.where(side == 0, a, n) for n, a in zip(near, away)]
    return jnp.concatenate(low + high, axis)


def gather(own, axis):
    far = swap(own, "tensor", 2)
    mate = swap(own, "tensor", 1)
    return ordered(own, far, mate, swap(far, "tensor", 1), axis)


def scatter_sum(make):
    side, core = tensor_place()
    away = jnp.stack([make(1 - core), make(3 - core)]).astype(BF16)
    got = swap(away, "tensor", 1)
    near = jnp.stack([make(core), make(2 + core)]) + got.astype(F32)
    own = jnp.where(side == 0, near[0], near[1])
    far = jnp.where(side == 0, near[1], near[0]).astype(BF16)
    return own + swap(far, "tensor", 2).astype(F32), far


def rows_to_cols(rows):
    side, core = tensor_place()
    size, width = rows.shape[0], rows.shape[1] // 4
    halves = [rows[:, : 2 * width], rows[:, 2 * width :]]
    keep = jnp.where(side == 0, halves[0], halves[1])
    far = swap(jnp.where(side == 0, halves[1], halves[0]), "tensor", 2)
    pair = jnp.concatenate([jnp.where(side == 0, keep, far), jnp.where(side == 0, far, keep)], 0)
    first, second = pair[:, :width], pair[:, width:]
    own = jnp.where(core == 0, first, second)
    mate = swap(jnp.where(core == 0, second, first), "tensor", 1)
    even = jnp.where(core == 0, own, mate)
    odd = jnp.where(core == 0, mate, own)
    return jnp.concatenate([even[:size], odd[:size], even[size:], odd[size:]], 0)


def paired():
    return lax.axis_size("seq") == 8


def seq_place():
    place = lax.axis_index("seq")
    return place // 2, place % 2


def blocks_for(rows, column):
    count, cols = rows.shape
    return lax.dynamic_index_in_dim(rows.reshape(4, 2, count // 8, cols), column, 1, False)


def trade(value, start, done):
    return after(swap(after(value, start), "seq", 1), done)


def pair_up(rows, start, done):
    _, column = seq_place()
    count, size = rows.shape
    own = blocks_for(rows, column).reshape(count // 2, size)
    away = blocks_for(rows, 1 - column).reshape(count // 2, size)
    return own, trade(away, start, done)


def line_sum(own, tokens):
    level, _ = seq_place()

    def piece(index):
        return lax.dynamic_index_in_dim(own, jnp.clip(index, 0, 3), 0, False)

    up = down = None
    for step in range(3):
        rise = piece(3 - step + level)
        fall = piece(step - 3 + level)
        if step:
            up, down, _ = lax.optimization_barrier((up, down, tokens[step]))
            rise = (rise.astype(F32) + up.astype(F32)).astype(BF16)
            fall = (fall.astype(F32) + down.astype(F32)).astype(BF16)
        climbs = [(2 * z + x, 2 * z + 2 + x) for z in range(step + 1) for x in (0, 1)]
        drops = [(6 - 2 * z + x, 4 - 2 * z + x) for z in range(step + 1) for x in (0, 1)]
        rise, fall, _ = lax.optimization_barrier((rise, fall, tokens[step]))
        up = lax.ppermute(rise, "seq", climbs)
        down = lax.ppermute(fall, "seq", drops)
    up, down, _ = lax.optimization_barrier((up, down, tokens[3]))
    return piece(level).astype(F32) + up.astype(F32) + down.astype(F32)


def line_trade(own, start, done):
    level, _ = seq_place()

    def piece(index):
        return lax.dynamic_index_in_dim(own, jnp.clip(index, 0, 3), 0, False)

    total = piece(level).astype(F32)
    sent = [piece(level + by) for by in (-3, -2, -1, 1, 2, 3)]
    sent = lax.optimization_barrier((*sent, start))[:6]
    got = []
    for by, value in zip((-3, -2, -1, 1, 2, 3), sent):
        pairs = [(i, i + 2 * by) for i in range(8) if 0 <= i + 2 * by < 8]
        got.append(lax.ppermute(value, "seq", pairs))
    got = lax.optimization_barrier((*got, done))[:6]
    for value in got:
        total = total + value.astype(F32)
    return total


def fold_pair(rows, start, done):
    _, column = seq_place()
    got = trade(blocks_for(rows, 1 - column), start, done)
    return (blocks_for(rows, column).astype(F32) + got.astype(F32)).astype(BF16)


def plain_sum(grad):
    return lax.psum_scatter(
        grad.astype(BF16), "seq", scatter_dimension=0, tiled=True
    ).astype(F32)


def reduce_small(vectors):
    count = lax.axis_size("seq")
    if count != 8:
        return lax.psum_scatter(vectors, "seq", scatter_dimension=1, tiled=True)
    place = lax.axis_index("seq")
    kinds, width = vectors.shape
    parts = vectors.reshape(kinds, 8, width // 8).transpose(1, 0, 2)
    for by in (4, 2, 1):
        bit = (place // by) % 2
        pair = parts.reshape(2, by, kinds, width // 8)
        send = lax.dynamic_index_in_dim(pair, 1 - bit, 0, False)
        keep = lax.dynamic_index_in_dim(pair, bit, 0, False)
        parts = keep + swap(send, "seq", by)
    return parts[0]


def frame_clip_labels(segment, row_length):
    frame_index = jnp.arange(segment.shape[0], dtype=jnp.int32)
    border = (frame_index % row_length == 0) | (segment != jnp.roll(segment, 1))
    clip_starts = lax.cummax(jnp.where(border, frame_index, 0), axis=0)
    return (clip_starts, (frame_index - clip_starts + 1).astype(jnp.float32))


def tile_ranges(q_labels, key_labels):
    q = q_labels.reshape(-1, TILE)
    k = key_labels.reshape(-1, TILE)
    meets = (k[None, :, 0] <= q[:, None, -1]) & (k[None, :, -1] >= q[:, None, 0])
    index = jnp.arange(k.shape[0], dtype=jnp.int32)[None]
    low = jnp.min(jnp.where(meets, index, k.shape[0]), 1)
    high = jnp.max(jnp.where(meets, index + 1, 0), 1)
    return jnp.stack([low, high], 1).reshape(-1)

def head_rows(g):
    return slice(g * HEAD_SIZE, (g + 1) * HEAD_SIZE)

def fill_natural(dest, refs):
    size = refs[0].shape[1]
    for part, ref in enumerate(refs):
        dest[part * size : (part + 1) * size, :] = ref[...].T

def sums_over(left, right):
    return lax.dot_general(left, right, (((1,), (0,)), ((), ())), preferred_element_type=F32)

def across(left, right):
    return lax.dot_general(left, right, (((1,), (1,)), ((), ())), preferred_element_type=F32)

def forward_body(span, q, k0, k1, k2, v0, v1, v2, tk, tv, qlab, klab, out, lse, keys, vals):
    rows, size = q.shape
    group = rows // HEAD_SIZE
    fill_natural(keys, (k0, k1, k2))
    for part, ref in enumerate((v0, v1, v2)):
        for piece in range(size // TILE):
            vals[part * (size // TILE) + piece] = ref[:, piece * TILE : (piece + 1) * TILE]
    for tile in range(size // TILE):
        cols = slice(tile * TILE, (tile + 1) * TILE)
        lab = qlab[:, cols]
        state = []
        for g in range(group):
            part = q[head_rows(g), cols].astype(F32)
            top = jnp.sum(part * tk[head_rows(g), :], 0, keepdims=True)
            state += [
                top,
                jnp.ones_like(top),
                jnp.broadcast_to(tv[head_rows(g), :], (HEAD_SIZE, TILE)),
            ]

        def step(j, state):
            start = pl.multiple_of(j * TILE, TILE)
            seen = klab[pl.ds(start, TILE), :] == lab
            fresh = []
            for g in range(group):
                top, total, acc = state[3 * g : 3 * g + 3]
                s = sums_over(keys[pl.ds(start, TILE), head_rows(g)], q[head_rows(g), cols])
                s = jnp.where(seen, s, -1e30)
                new = jnp.maximum(top, jnp.max(s, 0, keepdims=True))
                fade = jnp.exp(top - new)
                p = jnp.exp(s - new)
                total = total * fade + jnp.sum(p, 0, keepdims=True)
                acc = acc * fade + sums_over(vals[j, head_rows(g), :], p.astype(BF16))
                fresh += [new, total, acc]
            return tuple(fresh)

        state = lax.fori_loop(span[2 * tile], span[2 * tile + 1], step, tuple(state))
        for g in range(group):
            top, total, acc = state[3 * g : 3 * g + 3]
            out[head_rows(g), cols] = (acc / total).astype(BF16)
            lse[0, g : g + 1, cols] = top + jnp.log(total)

def backward_body(span, q, k0, k1, k2, v0, v1, v2, tk, tv, qlab, klab, out, lse, og,
                  dq, dk0, dk1, dk2, dv0, dv1, dv2, dtk, dtv, keys, vals, tkeys, ak, av):
    rows, size = q.shape
    group = rows // HEAD_SIZE
    pieces = size // TILE
    fill_natural(keys, (k0, k1, k2))
    fill_natural(vals, (v0, v1, v2))
    for part, ref in enumerate((k0, k1, k2)):
        for piece in range(pieces):
            tkeys[part * pieces + piece] = ref[:, piece * TILE : (piece + 1) * TILE]
    ak[...] = jnp.zeros_like(ak)
    av[...] = jnp.zeros_like(av)
    for tile in range(pieces):
        cols = slice(tile * TILE, (tile + 1) * TILE)
        lab = qlab[:, cols]
        state, norms, deltas = [], [], []
        for g in range(group):
            hr = head_rows(g)
            qf = q[hr, cols].astype(F32)
            gf = og[hr, cols].astype(F32)
            norm = lse[0, g : g + 1, cols]
            delta = jnp.sum(gf * out[hr, cols].astype(F32), 0, keepdims=True)
            pt = jnp.exp(jnp.sum(qf * tk[hr, :], 0, keepdims=True) - norm)
            st = pt * (jnp.sum(gf * tv[hr, :], 0, keepdims=True) - delta)
            gk = jnp.sum(qf * st, 1, keepdims=True)
            gv = jnp.sum(gf * pt, 1, keepdims=True)
            if tile == 0:
                dtk[hr, :] = gk
                dtv[hr, :] = gv
            else:
                dtk[hr, :] += gk
                dtv[hr, :] += gv
            state.append(tk[hr, :] * st)
            norms.append(norm)
            deltas.append(delta)

        def step(j, state):
            start = pl.multiple_of(j * TILE, TILE)
            seen = klab[pl.ds(start, TILE), :] == lab
            fresh = []
            for g in range(group):
                hr = head_rows(g)
                s = sums_over(keys[pl.ds(start, TILE), hr], q[hr, cols])
                p = jnp.exp(jnp.where(seen, s, -1e30) - norms[g])
                m = sums_over(vals[pl.ds(start, TILE), hr], og[hr, cols])
                ds = (p * (m - deltas[g])).astype(BF16)
                av[j, hr, :] += across(og[hr, cols], p.astype(BF16))
                ak[j, hr, :] += across(q[hr, cols], ds)
                fresh.append(state[g] + sums_over(tkeys[j, hr, :], ds))
            return tuple(fresh)

        state = lax.fori_loop(span[2 * tile], span[2 * tile + 1], step, tuple(state))
        for g in range(group):
            dq[head_rows(g), cols] = state[g]
    for part, (dk, dv) in enumerate(((dk0, dv0), (dk1, dv1), (dk2, dv2))):
        for piece in range(pieces):
            at = slice(piece * TILE, (piece + 1) * TILE)
            dk[:, at] = ak[part * pieces + piece].astype(dk.dtype)
            dv[:, at] = av[part * pieces + piece].astype(dv.dtype)

def attend(span, q, ks, vs, tk, tv, qlab, klab):
    cols, size = q.shape
    gr = GROUP * HEAD_SIZE
    steps = cols // gr
    block = pl.BlockSpec((gr, size), lambda i, s: (i, 0))
    column = pl.BlockSpec((gr, 1), lambda i, s: (i, 0))
    return pl.pallas_call(
        forward_body,
        grid_spec=pltpu.PrefetchScalarGridSpec(
            num_scalar_prefetch=1,
            grid=(steps,),
            in_specs=[block] * 7 + [column] * 2
            + [pl.BlockSpec((1, size), lambda i, s: (0, 0)), pl.BlockSpec((3 * size, 1), lambda i, s: (0, 0))],
            out_specs=[block, pl.BlockSpec((1, GROUP, size), lambda i, s: (i, 0, 0))],
            scratch_shapes=[pltpu.VMEM((3 * size, gr), BF16), pltpu.VMEM((3 * size // TILE, gr, TILE), BF16)],
        ),
        out_shape=[jax.ShapeDtypeStruct((cols, size), BF16), jax.ShapeDtypeStruct((steps, GROUP, size), F32)],
        name="attend",
    )(span, q, *ks, *vs, tk, tv, qlab, klab)

def attend_back(span, q, ks, vs, tk, tv, qlab, klab, out, lse, og):
    cols, size = q.shape
    gr = GROUP * HEAD_SIZE
    steps = cols // gr
    tiles = 3 * size // TILE
    block = pl.BlockSpec((gr, size), lambda i, s: (i, 0))
    column = pl.BlockSpec((gr, 1), lambda i, s: (i, 0))
    small = jax.ShapeDtypeStruct((cols, 1), F32)
    wide = jax.ShapeDtypeStruct((cols, size), F32)
    low = jax.ShapeDtypeStruct((cols, size), BF16)
    return pl.pallas_call(
        backward_body,
        grid_spec=pltpu.PrefetchScalarGridSpec(
            num_scalar_prefetch=1,
            grid=(steps,),
            in_specs=[block] * 7 + [column] * 2
            + [pl.BlockSpec((1, size), lambda i, s: (0, 0)), pl.BlockSpec((3 * size, 1), lambda i, s: (0, 0)),
               block, pl.BlockSpec((1, GROUP, size), lambda i, s: (i, 0, 0)), block],
            out_specs=[block] * 7 + [column] * 2,
            scratch_shapes=[pltpu.VMEM((3 * size, gr), BF16), pltpu.VMEM((3 * size, gr), BF16),
                            pltpu.VMEM((tiles, gr, TILE), BF16),
                            pltpu.VMEM((tiles, gr, TILE), F32), pltpu.VMEM((tiles, gr, TILE), F32)],
        ),
        out_shape=[wide, low, wide, low, low, wide, low, small, small],
        name="attend_back",
    )(span, q, *ks, *vs, tk, tv, qlab, klab, out, lse, og)


def rotary_tables(frame_positions):
    half_dim = HEAD_SIZE // 2
    frequency = jnp.exp(jnp.arange(half_dim, dtype=jnp.float32) * (-math.log(10000.0) / half_dim))
    angles = frequency[:, None] * frame_positions[None, :]
    return (jnp.cos(angles), jnp.sin(angles))


def rotate(rows, tables, sign=1.0):
    count, size = rows.shape
    halves = rows.reshape(count // HEAD_SIZE, 2, HEAD_SIZE // 2, size)
    cosine, sine = tables[0][None], tables[1][None] * sign
    first = halves[:, 0] * cosine - halves[:, 1] * sine
    second = halves[:, 1] * cosine + halves[:, 0] * sine
    return jnp.stack([first, second], 1).reshape(count, size)


def product(left, right):
    return jnp.dot(left, right, preferred_element_type=jnp.float32)


def inner_rows(left, right):
    return jnp.einsum("nd,nf->df", left, right, preferred_element_type=jnp.float32)


def back_project(gradient, weight):
    return jnp.einsum("nf,df->nd", gradient, weight, preferred_element_type=jnp.float32)


def by_feature(left, right):
    return jnp.einsum("nd,df->fn", left, right, preferred_element_type=jnp.float32)


def columns(weight, start, size):
    return lax.dynamic_slice_in_dim(weight, start, size, 1)


def rows_of(weight, start, size):
    return lax.dynamic_slice_in_dim(weight, start, size, 0)


def normalize(value_rows):
    means = jnp.mean(value_rows, -1, keepdims=True)
    centred = value_rows - means
    inverse = lax.rsqrt(jnp.mean(centred * centred, -1, keepdims=True) + 1e-05)
    return centred * inverse, inverse


def norm_backward(gradient, scaled, inverse, norm_gain):
    scaled_grad = gradient * norm_gain
    plain = jnp.mean(scaled_grad, -1, keepdims=True)
    cross = jnp.mean(scaled_grad * scaled, -1, keepdims=True)
    return inverse * (scaled_grad - plain - scaled * cross)


def per_device(
    frames,
    segment,
    time_token,
    context,
    gain_attn,
    bias_attn,
    gain_cross,
    bias_cross,
    gain_ffn,
    bias_ffn,
    w_query,
    w_key,
    w_value,
    w_out,
    c_query,
    c_key,
    c_value,
    c_out,
    w_gate,
    w_up,
    w_down,
    out_grad,
):
    local_rows = frames.shape[0]
    local_width = frames.shape[1]
    model_width = w_query.shape[0]
    head_cols = w_query.shape[1]
    heads = head_cols // HEAD_SIZE
    number_of_frames = lax.axis_size("seq") * local_rows
    row_length = min(max(ROW_MIN, 64 * lax.axis_size("seq")), number_of_frames)
    first_frame = lax.axis_index("seq") * local_rows
    own_start = lax.axis_index("tensor") * local_width

    def own_cols(value):
        return lax.dynamic_slice_in_dim(value, own_start, local_width, value.ndim - 1)

    place = lax.axis_index("tensor")
    share = local_rows // 4

    def own_rows(value):
        return rows_of(value, place * share, share)

    def row_block(value, index):
        return rows_of(value, index * share, share)

    frames_full = gather(frames, 1)
    norms = gather(
        jnp.stack([gain_attn, bias_attn, gain_cross, bias_cross, gain_ffn, bias_ffn]), 1
    )
    gain_one, bias_one, gain_two, bias_two, gain_three, bias_three = [
        norms[i : i + 1] for i in range(6)
    ]
    clip_starts, frame_positions = frame_clip_labels(segment, row_length)
    own_labels = lax.dynamic_slice_in_dim(clip_starts, first_frame, local_rows)
    own_positions = lax.dynamic_slice_in_dim(frame_positions, first_frame, local_rows)
    blanks = jnp.full((local_rows,), -1, jnp.int32)
    key_labels = lax.dynamic_slice_in_dim(
        jnp.concatenate([blanks, clip_starts, blanks]), first_frame, 3 * local_rows
    )
    spans = tile_ranges(own_labels, key_labels)
    label_row, label_column = own_labels[None, :], key_labels[:, None]
    row_index = first_frame // row_length
    time_row = lax.dynamic_slice_in_dim(time_token, row_index, 1, 0).astype(F32)
    row_context = lax.dynamic_slice_in_dim(context, row_index, 1, 0)[0]
    context_rows = row_context.shape[0]
    tables = rotary_tables(own_positions)
    score_scale = 1.0 / math.sqrt(HEAD_SIZE)
    all_heads = model_width // HEAD_SIZE

    scaled_one, inverse_one = normalize(frames_full.astype(F32))
    frame_normed = (scaled_one * gain_one + bias_one).astype(BF16)
    own_keys = rotate(by_feature(frame_normed, w_key), tables).astype(BF16)
    own_values = by_feature(frame_normed, w_value).astype(BF16)
    both = jnp.stack([own_keys, own_values])
    behind, ahead = shift(both, "seq", 1), shift(both, "seq", -1)
    frame_late, time_late = after((frame_normed, time_row), both)
    queries = (rotate(by_feature(frame_late, w_query), tables) * score_scale).astype(BF16)
    scaled_time, _ = normalize(time_late)
    time_normed = (scaled_time * gain_one + bias_one).astype(BF16)
    time_keys = by_feature(time_normed, w_key).astype(BF16).astype(F32)
    time_values = by_feature(time_normed, w_value).astype(BF16).astype(F32)
    context_late = after(row_context, both)
    cross_rows = gather(
        jnp.concatenate([product(context_late, c_key), product(context_late, c_value)], 0).astype(
            BF16
        ),
        1,
    )
    query_full = gather(after(c_query, both), 1)
    out_full = gather(after(c_out, query_full), 0)
    behind, ahead, _ = lax.optimization_barrier((behind, ahead, (queries, query_full, cross_rows)))
    keys = (behind[0], own_keys, ahead[0])
    values = (behind[1], own_values, ahead[1])
    attended, log_totals = attend(
        spans, queries, keys, values, time_keys, time_values, label_row, label_column
    )
    branch, one_near = scatter_sum(
        lambda b: jnp.einsum(
            "fn,fd->nd",
            lax.dynamic_slice_in_dim(attended, b * share, share, 1),
            w_out,
            preferred_element_type=F32,
        )
    )
    residual_one = own_rows(frames_full).astype(F32) + branch
    scaled_two, inverse_two = normalize(residual_one)
    normed_two = (scaled_two * gain_two + bias_two).astype(BF16)
    cross_queries = product(normed_two, query_full).astype(BF16).reshape(share, all_heads, HEAD_SIZE)
    cross_keys = cross_rows[:context_rows].reshape(context_rows, all_heads, HEAD_SIZE)
    cross_values = cross_rows[context_rows:].reshape(context_rows, all_heads, HEAD_SIZE)
    cross_scores = (
        jnp.einsum("qhd,khd->hqk", cross_queries, cross_keys, preferred_element_type=F32)
        * score_scale
    )
    cross_probs = jax.nn.softmax(cross_scores, axis=-1)
    cross_weights = cross_probs.astype(BF16)
    crossed = jnp.einsum("hqk,khd->qhd", cross_weights, cross_values, preferred_element_type=F32)
    crossed = crossed.reshape(share, model_width).astype(BF16)
    residual_two = residual_one + product(crossed, out_full)
    scaled_three, inverse_three = normalize(residual_two)
    normed_share = (scaled_three * gain_three + bias_three).astype(BF16)
    normed_three = gather(normed_share, 0)
    grad_low = gather(after(out_grad, one_near), 1)
    gate_pre = product(normed_three, w_gate)
    lifted = product(normed_three, w_up)
    sigmoid_gate = jax.nn.sigmoid(gate_pre)
    hidden = (gate_pre * sigmoid_gate * lifted).astype(BF16)

    hidden_grad = back_project(after(grad_low, normed_share), w_down).astype(BF16).astype(F32)
    gate_grad = (
        hidden_grad * lifted * sigmoid_gate * (1.0 + gate_pre * (1.0 - sigmoid_gate))
    ).astype(BF16)
    lifted_grad = (hidden_grad * gate_pre * sigmoid_gate).astype(BF16)
    normed_grad, three_near = scatter_sum(
        lambda b: back_project(row_block(gate_grad, b), w_gate)
        + back_project(row_block(lifted_grad, b), w_up)
    )
    grad_two = own_rows(grad_low).astype(F32) + norm_backward(
        normed_grad, scaled_three, inverse_three, gain_three
    )

    cross_full = grad_two.astype(BF16)
    crossed_grad = (
        back_project(cross_full, out_full).astype(BF16).reshape(share, all_heads, HEAD_SIZE)
    )
    prob_grad = jnp.einsum("qhd,khd->hqk", crossed_grad, cross_values, preferred_element_type=F32)
    row_delta = jnp.sum(prob_grad * cross_probs, -1, keepdims=True)
    score_grad = (cross_probs * (prob_grad - row_delta)).astype(BF16)
    cross_query_grad = (
        jnp.einsum("hqk,khd->qhd", score_grad, cross_keys, preferred_element_type=F32)
        * score_scale
    )
    cross_query_grad = cross_query_grad.astype(BF16).reshape(share, model_width)
    normed_back = back_project(cross_query_grad, query_full)
    grad_one = (grad_two + norm_backward(normed_back, scaled_two, inverse_two, gain_two)).astype(
        BF16
    )
    attend_full = gather(grad_one, 0)
    grad_heads = jnp.einsum(
        "nd,fd->fn", attend_full, w_out, preferred_element_type=F32
    ).astype(BF16)
    back = attend_back(
        spans, queries, keys, values, time_keys, time_values, label_row, label_column,
        attended, log_totals, grad_heads,
    )
    query_grad, key_prev, key_own, key_next, value_prev, value_own, value_next = back[:7]
    time_key_grad, time_value_grad = back[7], back[8]
    from_next = shift(jnp.stack([key_prev, value_prev]), "seq", -1)
    from_prev = shift(jnp.stack([key_next, value_next]), "seq", 1)
    query_raw = (rotate(query_grad, tables, -1.0) * score_scale).astype(BF16)
    key_raw = rotate(
        key_own + from_next[0].astype(F32) + from_prev[0].astype(F32), tables, -1.0
    ).astype(BF16)
    value_raw = (value_own + from_next[1].astype(F32) + from_prev[1].astype(F32)).astype(BF16)

    def to_frames(rows, weight):
        return jnp.einsum("fn,df->nd", rows, weight, preferred_element_type=F32)

    frame_grad, last_near = scatter_sum(
        lambda b: to_frames(query_raw, rows_of(w_query, b * local_width, local_width))
        + to_frames(key_raw, rows_of(w_key, b * local_width, local_width))
        + to_frames(value_raw, rows_of(w_value, b * local_width, local_width)),
    )
    time_grad = to_frames(time_key_grad.astype(BF16), w_key) + to_frames(
        time_value_grad.astype(BF16), w_value
    )
    late = after((normed_grad, scaled_three, normed_back, scaled_two), query_grad)
    norm_grads = [
        jnp.sum(late[0] * late[1], 0),
        jnp.sum(late[0], 0),
        jnp.sum(late[2] * late[3], 0),
        jnp.sum(late[2], 0),
    ]
    own_scaled = own_cols(scaled_one)
    scaled_grad = frame_grad * gain_attn[None]
    sums = jnp.concatenate(
        [jnp.sum(scaled_grad, -1), jnp.sum(scaled_grad * own_scaled, -1), time_grad[0]]
        + norm_grads
    )[None]
    sums = sums + swap(sums, "tensor", 1)
    sums = sums + swap(sums, "tensor", 2)
    plain = sums[0, :local_rows, None] / model_width
    cross = sums[0, local_rows : 2 * local_rows, None] / model_width
    vectors = own_cols(sums[0, 2 * local_rows :].reshape(5, model_width))
    d_frames = own_cols(attend_full).astype(F32) + inverse_one * (
        scaled_grad - plain - own_scaled * cross
    )
    d_gain_attn = jnp.sum(frame_grad * own_scaled, 0) + vectors[0] * own_cols(scaled_time)[0]
    d_bias_attn = jnp.sum(frame_grad, 0) + vectors[0]
    small = reduce_small(
        jnp.stack([d_gain_attn, d_bias_attn, vectors[3], vectors[4], vectors[1], vectors[2]])
    )

    hidden_late = after(hidden, normed_grad)
    down_sum, _ = scatter_sum(lambda b: product(row_block(hidden_late, b), w_down))
    block_out = rows_to_cols((residual_two + down_sum).astype(BF16))

    late = after((score_grad, cross_weights, crossed_grad, cross_queries), grad_heads)
    key_grad = jnp.einsum("hqk,qhd->khd", late[0], late[3], preferred_element_type=F32)
    value_grad = jnp.einsum("hqk,qhd->khd", late[1], late[2], preferred_element_type=F32)
    context_sums = jnp.concatenate(
        [
            key_grad.reshape(context_rows, model_width) * score_scale,
            value_grad.reshape(context_rows, model_width),
        ],
        0,
    )
    context_own, _ = scatter_sum(
        lambda b: lax.dynamic_slice_in_dim(context_sums, b * head_cols, head_cols, 1)
    )
    two_full = gather(after(normed_two, hidden), 0)
    crossed_own = rows_to_cols(after(crossed, hidden))
    cross_grad_full = gather(after(cross_full, attend_full), 0)
    cross_query_own = rows_to_cols(after(cross_query_grad, attend_full))
    time_column = time_normed.astype(F32).T

    def context_grads(kv):
        left = row_context.T
        both_grads = jnp.concatenate([kv[:context_rows], kv[context_rows:]], 1)
        return product(left, both_grads.astype(BF16))

    if paired():
        _, column = seq_place()

        def meet(rows, cols, spec):
            blocks = sum(
                jnp.einsum(spec, r, c, preferred_element_type=F32) for r, c in zip(rows, cols)
            )
            return blocks.astype(BF16).reshape(4, blocks.shape[0] // 4, blocks.shape[1])

        normed_pair = pair_up(frame_normed.T, behind, normed_three)
        grad_pair = (grad_low, trade(grad_low, one_near, gate_grad))
        three_pair = pair_up(normed_three.T, normed_three, three_near)
        hidden_pair = pair_up(hidden.T, hidden, normed_grad)
        gate_pair = (gate_grad, trade(gate_grad, three_near, grad_heads))
        lifted_pair = (lifted_grad, trade(lifted_grad, grad_two, query_grad))

        down_blocks = meet(hidden_pair, grad_pair, "dn,nf->df")
        grad_down = line_trade(down_blocks, grad_two, query_grad)
        gate_blocks = meet(three_pair, gate_pair, "dn,nf->df")
        grad_gate_w = line_sum(gate_blocks, (query_grad, query_grad, from_next, key_raw))
        up_blocks = meet(three_pair, lifted_pair, "dn,nf->df")
        grad_up_w = line_sum(up_blocks, (query_grad, from_next, key_raw, last_near))

        late = after((crossed_own, cross_grad_full), query_grad)
        grad_c_out = inner_rows(*late).astype(BF16)
        late = after((two_full, cross_query_own), query_grad)
        grad_c_query = inner_rows(*late).astype(BF16)
        grad_c_kv = context_grads(context_own).astype(BF16)
        late = after((attended, attend_full), query_grad)
        grad_w_out = product(*late).astype(BF16)
        part = head_cols // 8
        bundle = jnp.concatenate(
            [
                value.reshape(8, part, model_width)
                for value in (grad_c_out, grad_c_query, grad_c_kv, grad_w_out)
            ],
            1,
        ).reshape(8 * 4 * part, model_width)
        folded = fold_pair(bundle, from_next, last_near)
        middle = line_sum(folded, (last_near, frame_grad, frame_grad, frame_grad))
        grad_c_out = middle[:part]
        grad_c_query = middle[part : 2 * part].reshape(model_width // 8, head_cols)
        grad_c_kv = middle[2 * part : 3 * part].reshape(-1, 2 * head_cols)
        grad_w_out = middle[3 * part :]

        raw = jnp.concatenate([query_raw, key_raw, value_raw], 0)
        raw_pair = (raw, trade(raw, key_raw, last_near))
        time_both = jnp.concatenate([time_key_grad, time_value_grad], 0)
        time_both = time_both + trade(time_both, from_next, key_raw)
        own_time_rows = blocks_for(time_column, column).reshape(-1, 1)
        outer = own_time_rows * jnp.concatenate(
            [jnp.zeros((head_cols, 1), F32), time_both], 0
        ).T
        blocks = sum(
            jnp.einsum("dn,fn->df", r, c, preferred_element_type=F32)
            for r, c in zip(normed_pair, raw_pair)
        )
        blocks = (blocks + outer).astype(BF16).reshape(4, -1, 3 * head_cols)
        heads_sum = line_sum(blocks, (frame_grad, frame_grad, frame_grad, frame_grad))
        grad_w_query, grad_w_key, grad_w_value = (
            heads_sum[:, i * head_cols : (i + 1) * head_cols] for i in range(3)
        )
    else:
        grad_down = plain_sum(inner_rows(hidden, grad_low))
        grad_gate_w = plain_sum(inner_rows(normed_three, gate_grad))
        grad_up_w = plain_sum(inner_rows(normed_three, lifted_grad))
        grad_c_out = plain_sum(inner_rows(crossed_own, cross_grad_full))
        grad_c_query = plain_sum(inner_rows(two_full, cross_query_own))
        grad_c_kv = plain_sum(context_grads(context_own))
        grad_w_out = plain_sum(product(attended, attend_full))

        def with_time(rows, time_part):
            grads = jnp.einsum("nd,fn->df", frame_normed, rows, preferred_element_type=F32)
            return grads + time_column * time_part.T

        grad_w_query = plain_sum(
            jnp.einsum("nd,fn->df", frame_normed, query_raw, preferred_element_type=F32)
        )
        grad_w_key = plain_sum(with_time(key_raw, time_key_grad))
        grad_w_value = plain_sum(with_time(value_raw, time_value_grad))
    return (
        block_out,
        d_frames,
        small[0],
        small[1],
        small[2],
        small[3],
        small[4],
        small[5],
        grad_w_query,
        grad_w_key,
        grad_w_value,
        grad_w_out,
        grad_c_query,
        grad_c_kv[:, :head_cols],
        grad_c_kv[:, head_cols:],
        grad_c_out,
        grad_gate_w,
        grad_up_w,
        grad_down,
    )


def solution(mesh):
    return jax.shard_map(
        per_device,
        mesh=mesh,
        in_specs=(
            P("seq", "tensor"),
            P(),
            P(),
            P(),
            P("tensor"),
            P("tensor"),
            P("tensor"),
            P("tensor"),
            P("tensor"),
            P("tensor"),
            P(None, "tensor"),
            P(None, "tensor"),
            P(None, "tensor"),
            P("tensor", None),
            P(None, "tensor"),
            P(None, "tensor"),
            P(None, "tensor"),
            P("tensor", None),
            P(None, "tensor"),
            P(None, "tensor"),
            P("tensor", None),
            P("seq", "tensor"),
        ),
        out_specs=(
            P("seq", "tensor"),
            P("seq", "tensor"),
            P(("tensor", "seq")),
            P(("tensor", "seq")),
            P(("tensor", "seq")),
            P(("tensor", "seq")),
            P(("tensor", "seq")),
            P(("tensor", "seq")),
            P("seq", "tensor"),
            P("seq", "tensor"),
            P("seq", "tensor"),
            P(("tensor", "seq"), None),
            P("seq", "tensor"),
            P("seq", "tensor"),
            P("seq", "tensor"),
            P(("tensor", "seq"), None),
            P("seq", "tensor"),
            P("seq", "tensor"),
            P(("tensor", "seq"), None),
        ),
        check_vma=False,
    )
```

time: 1650 us -> 698 us (0.42)
  waiting for transfers between devices: 1270 us -> 217 us
  starting transfers between devices: 15.1 us -> 149 us
  blocking collectives: 73.8 us -> 0 us
  matrix products: 162 us -> 119 us
  other arithmetic: 53.9 us -> 93.3 us
  Pallas kernels: 0 us -> 30.4 us
  local copies, waits for them, and re-layouts: 54.7 us -> 73.2 us
    reduce_scatter x11 -> x0, waiting for transfers between devices: 987 us -> none  [the longest x1 167 us: per_device(): lax.psum_scatter(grad_down, 'seq', scatter_dimension=0, tiled=True)]
    ppermute x4 -> x94, waiting for transfers between devices: 58.1 us -> 217 us  [the longest x60 117 us: swap(): lax.ppermute(value, axis, [(i, i ^ by) for i in range(lax.axis_size(axis))])]
    ppermute x4 -> x94, starting transfers between devices: 13.3 us -> 149 us  [the longest x12 52.7 us: line_sum(): up = lax.ppermute(rise, 'seq', climbs)]
    unnamed x29 -> x0, waiting for transfers between devices: 128 us -> none
    all_gather x6 -> x0, waiting for transfers between devices: 98.7 us -> none  [the longest x3 53 us: spread_grad(): lax.all_gather(gradient.astype(jnp.bfloat16), 'tensor', axis=1, tiled=True)]
    dot_general x9 -> x2, matrix products: 42.1 us -> 2.82 us  [inner_rows(): jnp.einsum('nd,nf->df', left, right, preferred_element_type=jnp.float32)]
    psum x6 -> x0, blocking collectives: 38 us -> none  [the longest x3 20 us: norm_forward(): first_sum, square_sum = lax.psum((first_sum, square_sum), 'tensor')]
    unnamed x1 -> x0, blocking collectives: 35.8 us -> none
  transfers between devices with their start and end apart: 27 -> 94, of which waited for: 25 -> 29; matrix products, arithmetic and copies ran while one was open for 6% -> 36% of each run, Pallas kernels for 0% -> 2%
where the time goes in v1:
time: 698 us; the launch traced here: 687 us
  waiting for transfers between devices  217 us (31%)
  starting transfers between devices  149 us (21%)
  matrix products  119 us (17%)
  other arithmetic  93.3 us (13%)
  local copies, waits for them, and re-layouts  73.2 us (10%)
  Pallas kernels  30.4 us (4%)
    ppermute x60, waiting for transfers between devices, swap(): lax.ppermute(value, axis, [(i, i ^ by) for i in range(lax.axis_size(axis))])  117 us
    ppermute x12, starting transfers between devices, line_sum(): up = lax.ppermute(rise, 'seq', climbs)  52.7 us
    ppermute x60, starting transfers between devices, swap(): lax.ppermute(value, axis, [(i, i ^ by) for i in range(lax.axis_size(axis))])  51.9 us
    ppermute x12, waiting for transfers between devices, line_sum(): up = lax.ppermute(rise, 'seq', climbs)  50 us
    dot_general x11, matrix products, back_project(): jnp.einsum('nf,df->nd', gradient, weight, preferred_element_type=jnp.floa...  41.9 us
    ppermute x4, waiting for transfers between devices, shift(): return lax.ppermute(value, axis, pairs)  29.7 us
    dot_general x12, matrix products, product(): return jnp.dot(left, right, preferred_element_type=jnp.float32)  24.5 us
    dot_general x6, matrix products, meet(): jnp.einsum(spec, r, c, preferred_element_type=F32)  22.1 us
  transfers between devices with their start and end apart: 94, of which 29 were waited for; matrix products, arithmetic and copies ran while one was open for 36% of the time, Pallas kernels for 2%

profile of v1, /device:TPU:0, one launch (start us, length us, event | category | flops | bytes accessed | tf_op | source)
XLA Modules:
  0.0 687.1 jit_solution(5550577983889400204)
XLA Ops:
  4.9 3.0 collective-permute-start.4
  16.0 3.7 collective-permute-done.1
  39.6 18.5 %collective-permute-done.9 = bf16[1536,384]{1,0:T(8,128)(2,1)} collective-permute-done((bf16[1536,384]{1,0:T(8,128)(2,1)}, bf16[1536,384]{1,0:T(8,128)(2,1)}, u32[]{:S(2)}, u32[]{:S(2)}) %collective-permute-start.9) | collective-permute-done | bytes 1179680 | tf_op jit(solution)/shard_map/ppermute | solution.py:23
  65.9 4.9 collective-permute-start.6
  77.5 6.5 collective-permute-done.7
  84.0 16.8 %collective-permute-done.6 = bf16[2,384,512]{2,1,0:T(8,128)(2,1)S(1)} collective-permute-done((bf16[2,384,512]{2,1,0:T(8,128)(2,1)S(1)}, bf16[2,384,512]{2,1,0:T(8,128)(2,1)S(1)}, u32[]{:S(2)}, u32[]{:S(2)}) %collective-permute-start.6) | collective-permute-done | bytes 786464 | tf_op jit(solution)/shard_map/ppermute | solution.py:29
  102.6 13.7 %attend.1 = (bf16[384,512]{1,0:T(8,128)(2,1)}, f32[2,3,512]{2,1,0:T(4,128)}) custom-call(s32[4]{0:T(128)} %reshape.507.span, bf16[384,512]{1,0:T(8,128)(2,1)} %bitcast.462, bf16[384,512]{1,0:T(8,128)(2,1)} %get-tuple-element.399.k0, bf16[384,512]{1,0:T(8,128)(2,1)} %bitcast.451, bf16[384,512]{1,0:T(8,128)(2,1)} %get-tuple-element.397.k2, ...), custom_call_target="tpu_custom_call" | custom-call | tf_op jit(solution)/shard_map/attend/pallas_call | solution.py:311
  133.9 6.1 collective-permute-start.43
  145.5 21.4 %collective-permute-done.17 = bf16[384,1536]{1,0:T(8,128)(2,1)} collective-permute-done((bf16[384,1536]{1,0:T(8,128)(2,1)}, bf16[384,1536]{1,0:T(8,128)(2,1)}, u32[]{:S(2)}, u32[]{:S(2)}) %collective-permute-start.17) | collective-permute-done | bytes 1179680 | tf_op jit(solution)/shard_map/ppermute | solution.py:23
  166.9 3.9 convolution_convert_fusion.7
  175.0 2.9 fusion.206
  190.6 6.1 collective-permute-start.87
  198.6 4.1 convolution_convert_fusion
  206.8 6.8 fusion.9
  213.6 3.5 fusion.85
  217.1 3.6 fusion.88
  220.7 3.5 fusion.91
  226.8 4.9 fusion.12
  231.7 2.8 copy.185
  237.9 4.5 fusion.20
  242.3 4.2 fusion.21
  246.6 2.8 fusion.17
  250.8 5.4 fusion.212
  258.8 4.9 fusion.211
  267.3 6.1 collective-permute-start.71
  275.7 16.2 %collective-permute-done.71 = bf16[768,512]{1,0:T(8,128)(2,1)S(1)} collective-permute-done((bf16[768,512]{1,0:T(8,128)(2,1)S(1)}, bf16[768,512]{1,0:T(8,128)(2,1)S(1)}, u32[]{:S(2)}, u32[]{:S(2)}) %collective-permute-start.71) | collective-permute-done | bytes 786464 | tf_op jit(solution)/shard_map/ppermute | solution.py:23
  297.3 6.1 convolution_convert_fusion.4
  309.1 4.4 multiply_reduce_fusion.10
  316.9 3.2 fusion.213
  332.1 5.4 collective-permute-start.91
  340.5 16.8 %attend_back.1 = (f32[384,512]{1,0:T(8,128)}, bf16[384,512]{1,0:T(8,128)(2,1)}, f32[384,512]{1,0:T(8,128)}, bf16[384,512]{1,0:T(8,128)(2,1)}, bf16[384,512]{1,0:...) custom-call(s32[4]{0:T(128)} %reshape.507.span, ...), custom_call_target="tpu_custom_call" | custom-call | tf_op jit(solution)/shard_map/attend_back/pallas_call | solution.py:335
  367.1 8.9 %collective-permute-start.92 = (bf16[192,1536]{1,0:T(8,128)(2,1)}, bf16[192,1536]{1,0:T(8,128)(2,1)}, u32[]{:S(2)}, u32[]{:S(2)}) collective-permute-start(bf16[192,1536]{1,0:T(8,128)(2,1)} %get-tuple-element.245), channel_id=1, source_target_pairs={{0,4},{1,5},{2,6},{3,7},{8,12},{9,13},{10,14},{11,15},{16,20},{17,... | collective-permute-start | bytes 1769480 | tf_op jit(solution)/shard_map/ppermute | solution.py:138
  380.7 3.7 collective-permute-start.72
  389.3 11.1 %collective-permute-done.93 = bf16[192,1536]{1,0:T(8,128)(2,1)} collective-permute-done((bf16[192,1536]{1,0:T(8,128)(2,1)}, bf16[192,1536]{1,0:T(8,128)(2,1)}, u32[]{:S(2)}, u32[]{:S(2)}) %collective-permute-start.93) | collective-permute-done | bytes 589856 | tf_op jit(solution)/shard_map/ppermute | solution.py:138
  403.1 3.8 fusion.40
  409.1 10.9 %collective-permute-done.72 = bf16[512,1536]{1,0:T(8,128)(2,1)} collective-permute-done((bf16[512,1536]{1,0:T(8,128)(2,1)}, bf16[512,1536]{1,0:T(8,128)(2,1)}, u32[]{:S(2)}, u32[]{:S(2)}) %collective-permute-start.72) | collective-permute-done | bytes 1572896 | tf_op jit(solution)/shard_map/ppermute | solution.py:23
  420.1 2.8 add_convert_fusion.2
  427.4 3.1 concatenate.115
  430.5 4.9 collective-permute-start.35
  438.9 5.0 collective-permute-done.63
  444.8 5.5 collective-permute-done.29
  453.9 2.9 concatenate.118
  456.8 13.3 %collective-permute-done.79 = bf16[512,1536]{1,0:T(8,128)(2,1)} collective-permute-done((bf16[512,1536]{1,0:T(8,128)(2,1)}, bf16[512,1536]{1,0:T(8,128)(2,1)}, u32[]{:S(2)}, u32[]{:S(2)}) %collective-permute-start.79) | collective-permute-done | bytes 1572896 | tf_op jit(solution)/shard_map/ppermute | solution.py:23
  471.6 4.4 add_convert_fusion.1
  478.4 6.4 collective-permute-done.35
  515.0 10.3 %collective-permute-done.75 = bf16[192,1536]{1,0:T(8,128)(2,1)S(1)} collective-permute-done((bf16[192,1536]{1,0:T(8,128)(2,1)S(1)}, bf16[192,1536]{1,0:T(8,128)(2,1)S(1)}, u32[]{:S(2)}, u32[]{:S(2)}) %collective-permute-start.75) | collective-permute-done | bytes 589856 | tf_op jit(solution)/shard_map/ppermute | solution.py:120
  525.2 4.4 collective-permute-start.82
  533.2 9.1 %collective-permute-done.82 = bf16[192,1536]{1,0:T(8,128)(2,1)S(1)} collective-permute-done((bf16[192,1536]{1,0:T(8,128)(2,1)S(1)}, bf16[192,1536]{1,0:T(8,128)(2,1)S(1)}, u32[]{:S(2)}, u32[]{:S(2)}) %collective-permute-start.82) | collective-permute-done | bytes 589856 | tf_op jit(solution)/shard_map/ppermute | solution.py:120
  542.3 5.2 collective-permute-start.77
  549.0 2.9 multiply_reduce_fusion.1
  554.9 3.6 fusion.5
  569.3 3.2 collective-permute-start.46
  574.5 7.9 %collective-permute-done.41 = f32[2,6,48]{2,1,0:T(8,128)S(1)} collective-permute-done((f32[2,6,48]{2,1,0:T(8,128)S(1)}, f32[2,6,48]{2,1,0:T(8,128)S(1)}, u32[]{:S(2)}, u32[]{:S(2)}) %collective-permute-start.41) | collective-permute-done | bytes 2336 | tf_op jit(solution)/shard_map/ppermute | solution.py:23
  585.1 6.6 collective-permute-done.42
  595.7 3.0 fusion.1
  598.8 5.6 collective-permute-start.65
  611.5 17.6 %collective-permute-done.48 = bf16[192,1152]{1,0:T(8,128)(2,1)S(1)} collective-permute-done((bf16[192,1152]{1,0:T(8,128)(2,1)S(1)}, bf16[192,1152]{1,0:T(8,128)(2,1)S(1)}, u32[]{:S(2)}, u32[]{:S(2)}) %collective-permute-start.48) | collective-permute-done | bytes 442400 | tf_op jit(solution)/shard_map/ppermute | solution.py:120
  629.4 4.4 collective-permute-start.67
  634.8 12.2 %collective-permute-start.50 = (bf16[192,1152]{1,0:T(8,128)(2,1)S(1)}, bf16[192,1152]{1,0:T(8,128)(2,1)S(1)}, u32[]{:S(2)}, u32[]{:S(2)}) collective-permute-start(bf16[192,1152]{1,0:T(8,128)(2,1)S(1)} %get-tuple-element.175), channel_id=1, source_target_pairs={{0,2},{1,3},{2,4},{3,5},{4,6},{5,7},{8,10},{9,11},{10,12},{11,13},... | collective-permute-start | bytes 1327112 | tf_op jit(solution)/shard_map/ppermute | solution.py:120
  650.6 4.5 collective-permute-done.50
  655.1 4.2 collective-permute-done.51
  659.6 10.8 %collective-permute-start.69 = (bf16[192,1536]{1,0:T(8,128)(2,1)S(1)}, bf16[192,1536]{1,0:T(8,128)(2,1)S(1)}, u32[]{:S(2)}, u32[]{:S(2)}) collective-permute-start(bf16[192,1536]{1,0:T(8,128)(2,1)S(1)} %get-tuple-element.203), channel_id=1, source_target_pairs={{0,2},{1,3},{2,4},{3,5},{4,6},{5,7},{8,10},{9,11},{10,12},{11,13},... | collective-permute-start | bytes 1769480 | tf_op jit(solution)/shard_map/ppermute | solution.py:120
  672.7 7.3 %collective-permute-done.69 = bf16[192,1536]{1,0:T(8,128)(2,1)S(1)} collective-permute-done((bf16[192,1536]{1,0:T(8,128)(2,1)S(1)}, bf16[192,1536]{1,0:T(8,128)(2,1)S(1)}, u32[]{:S(2)}, u32[]{:S(2)}) %collective-permute-start.69) | collective-permute-done | bytes 589856 | tf_op jit(solution)/shard_map/ppermute | solution.py:120
  680.0 4.1 collective-permute-done.70
  (739 shorter events, 251.7 us)
Async XLA Ops:
  8.0 13.6 %collective-permute-start.3 = (f32[6,384]{1,0:T(8,128)S(1)}, f32[6,384]{1,0:T(8,128)S(1)}, u32[]{:S(2)}, u32[]{:S(2)}) collective-permute-start(f32[6,384]{1,0:T(8,128)S(1)} %stack.204), channel_id=1, source_target_pairs={{0,8},{8,0},{16,24},{24,16},{1,9},{9,1},{17,25},{25,17},{2,10},{10... | collective-permute-start | bytes 27656 | tf_op jit(solution)/shard_map/ppermute | solution.py:23
  8.0 14.3 %collective-permute-start = (bf16[512,384]{1,0:T(8,128)(2,1)}, bf16[512,384]{1,0:T(8,128)(2,1)S(1)}, u32[]{:S(2)}, u32[]{:S(2)}) collective-permute-start(bf16[512,384]{1,0:T(8,128)(2,1)} %param.22), channel_id=1, source_target_pairs={{0,8},{8,0},{16,24},{24,16},{1,9},{9,1},{17,25},{25,17},{2,10},{10... | collective-permute-start | bytes 1179656 | tf_op jit(solution)/shard_map/ppermute | solution.py:23
  29.0 29.1 %collective-permute-start.9 = (bf16[1536,384]{1,0:T(8,128)(2,1)}, bf16[1536,384]{1,0:T(8,128)(2,1)}, u32[]{:S(2)}, u32[]{:S(2)}) collective-permute-start(bf16[1536,384]{1,0:T(8,128)(2,1)} %param.36), channel_id=1, source_target_pairs={{0,16},{8,24},{16,0},{24,8},{1,17},{9,25},{17,1},{25,9},{2,18},{10... | collective-permute-start | bytes 3538952 | tf_op jit(solution)/shard_map/ppermute | solution.py:23
  30.6 31.2 %collective-permute-start.12 = (bf16[256,384]{1,0:T(8,128)(2,1)}, bf16[256,384]{1,0:T(8,128)(2,1)}, u32[]{:S(2)}, u32[]{:S(2)}) collective-permute-start(bf16[256,384]{1,0:T(8,128)(2,1)} %pad_maximum_fusion.28), channel_id=1, source_target_pairs={{0,16},{8,24},{16,0},{24,8},{1,17},{9,25},{17,1},{25,9},{2,18},{10... | collective-permute-start | bytes 589832 | tf_op jit(solution)/shard_map/ppermute | solution.py:23
  32.3 33.6 %collective-permute-start.11 = (bf16[256,384]{1,0:T(8,128)(2,1)}, bf16[256,384]{1,0:T(8,128)(2,1)}, u32[]{:S(2)}, u32[]{:S(2)}) collective-permute-start(bf16[256,384]{1,0:T(8,128)(2,1)} %pad_maximum_fusion.28), channel_id=1, source_target_pairs={{0,8},{8,0},{16,24},{24,16},{1,9},{9,1},{17,25},{25,17},{2,10},{10... | collective-permute-start | bytes 589832 | tf_op jit(solution)/shard_map/ppermute | solution.py:23
  32.3 40.7 %collective-permute-start.8 = (bf16[1536,384]{1,0:T(8,128)(2,1)}, bf16[1536,384]{1,0:T(8,128)(2,1)S(1)}, u32[]{:S(2)}, u32[]{:S(2)}) collective-permute-start(bf16[1536,384]{1,0:T(8,128)(2,1)} %param.36), channel_id=1, source_target_pairs={{0,8},{8,0},{16,24},{24,16},{1,9},{9,1},{17,25},{25,17},{2,10},{10... | collective-permute-start | bytes 3538952 | tf_op jit(solution)/shard_map/ppermute | solution.py:23
  58.0 14.9 %collective-permute-start.10 = (bf16[1536,384]{1,0:T(8,128)(2,1)}, bf16[1536,384]{1,0:T(8,128)(2,1)S(1)}, u32[]{:S(2)}, u32[]{:S(2)}) collective-permute-start(bf16[1536,384]{1,0:T(8,128)(2,1)} %collective-permute-done.9), channel_id=1, source_target_pairs={{0,8},{8,0},{16,24},{24,16},{1,9},{9,1},{17,25},{25,17},{2,10},{10... | collective-permute-start | bytes 3538952 | tf_op jit(solution)/shard_map/ppermute | solution.py:23
  62.2 21.8 %collective-permute-start.7 = (bf16[2,384,512]{2,1,0:T(8,128)(2,1)S(1)}, bf16[2,384,512]{2,1,0:T(8,128)(2,1)S(1)}, u32[]{:S(2)}, u32[]{:S(2)}) collective-permute-start(bf16[2,384,512]{2,1,0:T(8,128)(2,1)S(1)} %copy-done.96), channel_id=1, source_target_pairs={{1,0},{2,1},{3,2},{4,3},{5,4},{6,5},{7,6},{9,8},{10,9},{11,10},{12... | collective-permute-start | bytes 2359304 | tf_op jit(solution)/shard_map/ppermute | solution.py:29
  65.9 34.9 %collective-permute-start.6 = (bf16[2,384,512]{2,1,0:T(8,128)(2,1)S(1)}, bf16[2,384,512]{2,1,0:T(8,128)(2,1)S(1)}, u32[]{:S(2)}, u32[]{:S(2)}) collective-permute-start(bf16[2,384,512]{2,1,0:T(8,128)(2,1)S(1)} %copy-done.96), channel_id=1, source_target_pairs={{0,1},{1,2},{2,3},{3,4},{4,5},{5,6},{6,7},{8,9},{9,10},{10,11},{11... | collective-permute-start | bytes 2359304 | tf_op jit(solution)/shard_map/ppermute | solution.py:29
  132.3 34.6 %collective-permute-start.17 = (bf16[384,1536]{1,0:T(8,128)(2,1)}, bf16[384,1536]{1,0:T(8,128)(2,1)}, u32[]{:S(2)}, u32[]{:S(2)}) collective-permute-start(bf16[384,1536]{1,0:T(8,128)(2,1)} %param.39), channel_id=1, source_target_pairs={{0,16},{8,24},{16,0},{24,8},{1,17},{9,25},{17,1},{25,9},{2,18},{10... | collective-permute-start | bytes 3538952 | tf_op jit(solution)/shard_map/ppermute | solution.py:23
  133.9 46.0 %collective-permute-start.16 = (bf16[384,1536]{1,0:T(8,128)(2,1)}, bf16[384,1536]{1,0:T(8,128)(2,1)}, u32[]{:S(2)}, u32[]{:S(2)}) collective-permute-start(bf16[384,1536]{1,0:T(8,128)(2,1)} %param.39), channel_id=1, source_target_pairs={{0,8},{8,0},{16,24},{24,16},{1,9},{9,1},{17,25},{25,17},{2,10},{10... | collective-permute-start | bytes 3538952 | tf_op jit(solution)/shard_map/ppermute | solution.py:23
  133.9 133.3 %collective-permute-start.43 = (bf16[768,512]{1,0:T(8,128)(2,1)}, bf16[768,512]{1,0:T(8,128)(2,1)}, u32[]{:S(2)}, u32[]{:S(2)}) collective-permute-start(bf16[768,512]{1,0:T(8,128)(2,1)} %bitcast.480), channel_id=1, source_target_pairs={{0,1},{1,0},{2,3},{3,2},{4,5},{5,4},{6,7},{7,6},{8,9},{9,8},{10,11... | collective-permute-start | bytes 2359304 | tf_op jit(solution)/shard_map/ppermute | solution.py:23
  140.0 35.0 %collective-permute-start.23 = (bf16[512,384]{1,0:T(8,128)(2,1)}, bf16[512,384]{1,0:T(8,128)(2,1)}, u32[]{:S(2)}, u32[]{:S(2)}) collective-permute-start(bf16[512,384]{1,0:T(8,128)(2,1)} %param.43), channel_id=1, source_target_pairs={{0,16},{8,24},{16,0},{24,8},{1,17},{9,25},{17,1},{25,9},{2,18},{10... | collective-permute-start | bytes 1179656 | tf_op jit(solution)/shard_map/ppermute | solution.py:23
  141.6 45.9 %collective-permute-start.22 = (bf16[512,384]{1,0:T(8,128)(2,1)}, bf16[512,384]{1,0:T(8,128)(2,1)}, u32[]{:S(2)}, u32[]{:S(2)}) collective-permute-start(bf16[512,384]{1,0:T(8,128)(2,1)} %param.43), channel_id=1, source_target_pairs={{0,8},{8,0},{16,24},{24,16},{1,9},{9,1},{17,25},{25,17},{2,10},{10... | collective-permute-start | bytes 1179656 | tf_op jit(solution)/shard_map/ppermute | solution.py:23
  166.9 13.5 %collective-permute-start.18 = (bf16[384,1536]{1,0:T(8,128)(2,1)}, bf16[384,1536]{1,0:T(8,128)(2,1)}, u32[]{:S(2)}, u32[]{:S(2)}) collective-permute-start(bf16[384,1536]{1,0:T(8,128)(2,1)} %collective-permute-done.17), channel_id=1, source_target_pairs={{0,8},{8,0},{16,24},{24,16},{1,9},{9,1},{17,25},{25,17},{2,10},{10... | collective-permute-start | bytes 3538952 | tf_op jit(solution)/shard_map/ppermute | solution.py:23
  175.0 12.6 %collective-permute-start.24 = (bf16[512,384]{1,0:T(8,128)(2,1)}, bf16[512,384]{1,0:T(8,128)(2,1)}, u32[]{:S(2)}, u32[]{:S(2)}) collective-permute-start(bf16[512,384]{1,0:T(8,128)(2,1)} %collective-permute-done.23), channel_id=1, source_target_pairs={{0,8},{8,0},{16,24},{24,16},{1,9},{9,1},{17,25},{25,17},{2,10},{10... | collective-permute-start | bytes 1179656 | tf_op jit(solution)/shard_map/ppermute | solution.py:23
  190.6 76.7 %collective-permute-start.87 = (bf16[512,1536]{1,0:T(8,128)(2,1)}, bf16[512,1536]{1,0:T(8,128)(2,1)}, u32[]{:S(2)}, u32[]{:S(2)}) collective-permute-start(bf16[512,1536]{1,0:T(8,128)(2,1)} %pad_maximum_fusion.5), channel_id=1, source_target_pairs={{0,1},{1,0},{2,3},{3,2},{4,5},{5,4},{6,7},{7,6},{8,9},{9,8},{10,11... | collective-permute-start | bytes 4718600 | tf_op jit(solution)/shard_map/ppermute | solution.py:23
  235.8 28.1 %collective-permute-start.52 = (bf16[128,768]{1,0:T(8,128)(2,1)S(1)}, bf16[128,768]{1,0:T(8,128)(2,1)S(1)}, u32[]{:S(2)}, u32[]{:S(2)}) collective-permute-start(bf16[128,768]{1,0:T(8,128)(2,1)S(1)} %broadcast_select_fusion.74), channel_id=1, source_target_pairs={{0,16},{8,24},{16,0},{24,8},{1,17},{9,25},{17,1},{25,9},{2,18},{10... | collective-permute-start | bytes 589832 | tf_op jit(solution)/shard_map/ppermute | solution.py:23
  236.3 37.2 %collective-permute-start.58 = (bf16[128,1536]{1,0:T(8,128)(2,1)}, bf16[128,1536]{1,0:T(8,128)(2,1)S(1)}, u32[]{:S(2)}, u32[]{:S(2)}) collective-permute-start(bf16[128,1536]{1,0:T(8,128)(2,1)} %copy-done.38), channel_id=1, source_target_pairs={{0,16},{8,24},{16,0},{24,8},{1,17},{9,25},{17,1},{25,9},{2,18},{10... | collective-permute-start | bytes 1179656 | tf_op jit(solution)/shard_map/ppermute | solution.py:23
  267.3 24.5 %collective-permute-start.71 = (bf16[768,512]{1,0:T(8,128)(2,1)S(1)}, bf16[768,512]{1,0:T(8,128)(2,1)S(1)}, u32[]{:S(2)}, u32[]{:S(2)}) collective-permute-start(bf16[768,512]{1,0:T(8,128)(2,1)S(1)} %bitcast.483), channel_id=1, source_target_pairs={{0,1},{1,0},{2,3},{3,2},{4,5},{5,4},{6,7},{7,6},{8,9},{9,8},{10,11... | collective-permute-start | bytes 2359304 | tf_op jit(solution)/shard_map/ppermute | solution.py:23
  273.4 43.4 %collective-permute-start.86 = (bf16[768,512]{1,0:T(8,128)(2,1)}, bf16[768,512]{1,0:T(8,128)(2,1)}, u32[]{:S(2)}, u32[]{:S(2)}) collective-permute-start(bf16[768,512]{1,0:T(8,128)(2,1)} %bitcast.141), channel_id=1, source_target_pairs={{0,1},{1,0},{2,3},{3,2},{4,5},{5,4},{6,7},{7,6},{8,9},{9,8},{10,11... | collective-permute-start | bytes 2359304 | tf_op jit(solution)/shard_map/ppermute | solution.py:23
  274.9 18.3 %collective-permute-start.26 = (bf16[128,1536]{1,0:T(8,128)(2,1)S(1)}, bf16[128,1536]{1,0:T(8,128)(2,1)S(1)}, u32[]{:S(2)}, u32[]{:S(2)}) collective-permute-start(bf16[128,1536]{1,0:T(8,128)(2,1)S(1)} %fusion.68), channel_id=1, source_target_pairs={{0,16},{8,24},{16,0},{24,8},{1,17},{9,25},{17,1},{25,9},{2,18},{10... | collective-permute-start | bytes 1179656 | tf_op jit(solution)/shard_map/ppermute | solution.py:23
  314.4 16.4 %collective-permute-start.31 = (bf16[128,1536]{1,0:T(8,128)(2,1)S(1)}, bf16[128,1536]{1,0:T(8,128)(2,1)S(1)}, u32[]{:S(2)}, u32[]{:S(2)}) collective-permute-start(bf16[128,1536]{1,0:T(8,128)(2,1)S(1)} %add_convert_fusion.4), channel_id=1, source_target_pairs={{0,8},{8,0},{16,24},{24,16},{1,9},{9,1},{17,25},{25,17},{2,10},{10... | collective-permute-start | bytes 1179656 | tf_op jit(solution)/shard_map/ppermute | solution.py:23
  322.6 44.6 %collective-permute-start.27 = (bf16[2,128,1536]{2,1,0:T(8,128)(2,1)}, bf16[2,128,1536]{2,1,0:T(8,128)(2,1)}, u32[]{:S(2)}, u32[]{:S(2)}) collective-permute-start(bf16[2,128,1536]{2,1,0:T(8,128)(2,1)} %pad_maximum_fusion.16), channel_id=1, source_target_pairs={{0,8},{8,0},{16,24},{24,16},{1,9},{9,1},{17,25},{25,17},{2,10},{10... | collective-permute-start | bytes 2359304 | tf_op jit(solution)/shard_map/ppermute | solution.py:23
  326.6 50.9 %collective-permute-start.88 = (bf16[192,1536]{1,0:T(8,128)(2,1)}, bf16[192,1536]{1,0:T(8,128)(2,1)}, u32[]{:S(2)}, u32[]{:S(2)}) collective-permute-start(bf16[192,1536]{1,0:T(8,128)(2,1)} %get-tuple-element.241), channel_id=1, source_target_pairs={{6,0},{7,1},{14,8},{15,9},{22,16},{23,17},{30,24},{31,25}} | collective-permute-start | bytes 1769480 | tf_op jit(solution)/shard_map/ppermute | solution.py:138
  327.9 52.8 %collective-permute-start.89 = (bf16[192,1536]{1,0:T(8,128)(2,1)}, bf16[192,1536]{1,0:T(8,128)(2,1)}, u32[]{:S(2)}, u32[]{:S(2)}) collective-permute-start(bf16[192,1536]{1,0:T(8,128)(2,1)} %get-tuple-element.242), channel_id=1, source_target_pairs={{4,0},{5,1},{6,2},{7,3},{12,8},{13,9},{14,10},{15,11},{20,16},{21,... | collective-permute-start | bytes 1769480 | tf_op jit(solution)/shard_map/ppermute | solution.py:138
  330.8 56.4 %collective-permute-start.90 = (bf16[192,1536]{1,0:T(8,128)(2,1)}, bf16[192,1536]{1,0:T(8,128)(2,1)}, u32[]{:S(2)}, u32[]{:S(2)}) collective-permute-start(bf16[192,1536]{1,0:T(8,128)(2,1)} %get-tuple-element.243), channel_id=1, source_target_pairs={{2,0},{3,1},{4,2},{5,3},{6,4},{7,5},{10,8},{11,9},{12,10},{13,11},... | collective-permute-start | bytes 1769480 | tf_op jit(solution)/shard_map/ppermute | solution.py:138
  332.1 55.2 %collective-permute-start.91 = (bf16[192,1536]{1,0:T(8,128)(2,1)}, bf16[192,1536]{1,0:T(8,128)(2,1)}, u32[]{:S(2)}, u32[]{:S(2)}) collective-permute-start(bf16[192,1536]{1,0:T(8,128)(2,1)} %get-tuple-element.244), channel_id=1, source_target_pairs={{0,2},{1,3},{2,4},{3,5},{4,6},{5,7},{8,10},{9,11},{10,12},{11,13},... | collective-permute-start | bytes 1769480 | tf_op jit(solution)/shard_map/ppermute | solution.py:138
  367.1 22.1 %collective-permute-start.92 = (bf16[192,1536]{1,0:T(8,128)(2,1)}, bf16[192,1536]{1,0:T(8,128)(2,1)}, u32[]{:S(2)}, u32[]{:S(2)}) collective-permute-start(bf16[192,1536]{1,0:T(8,128)(2,1)} %get-tuple-element.245), channel_id=1, source_target_pairs={{0,4},{1,5},{2,6},{3,7},{8,12},{9,13},{10,14},{11,15},{16,20},{17,... | collective-permute-start | bytes 1769480 | tf_op jit(solution)/shard_map/ppermute | solution.py:138
  377.5 22.9 %collective-permute-start.93 = (bf16[192,1536]{1,0:T(8,128)(2,1)}, bf16[192,1536]{1,0:T(8,128)(2,1)}, u32[]{:S(2)}, u32[]{:S(2)}) collective-permute-start(bf16[192,1536]{1,0:T(8,128)(2,1)} %get-tuple-element.246), channel_id=1, source_target_pairs={{0,6},{1,7},{8,14},{9,15},{16,22},{17,23},{24,30},{25,31}} | collective-permute-start | bytes 1769480 | tf_op jit(solution)/shard_map/ppermute | solution.py:138
  380.7 39.4 %collective-permute-start.72 = (bf16[512,1536]{1,0:T(8,128)(2,1)}, bf16[512,1536]{1,0:T(8,128)(2,1)}, u32[]{:S(2)}, u32[]{:S(2)}) collective-permute-start(bf16[512,1536]{1,0:T(8,128)(2,1)} %get-tuple-element.209), channel_id=1, source_target_pairs={{0,1},{1,0},{2,3},{3,2},{4,5},{5,4},{6,7},{7,6},{8,9},{9,8},{10,11... | collective-permute-start | bytes 4718600 | tf_op jit(solution)/shard_map/ppermute | solution.py:23
  387.3 82.9 %collective-permute-start.79 = (bf16[512,1536]{1,0:T(8,128)(2,1)}, bf16[512,1536]{1,0:T(8,128)(2,1)}, u32[]{:S(2)}, u32[]{:S(2)}) collective-permute-start(bf16[512,1536]{1,0:T(8,128)(2,1)} %get-tuple-element.223), channel_id=1, source_target_pairs={{0,1},{1,0},{2,3},{3,2},{4,5},{5,4},{6,7},{7,6},{8,9},{9,8},{10,11... | collective-permute-start | bytes 4718600 | tf_op jit(solution)/shard_map/ppermute | solution.py:23
  387.4 88.9 %collective-permute-start.55 = (bf16[128,1536]{1,0:T(8,128)(2,1)}, bf16[128,1536]{1,0:T(8,128)(2,1)}, u32[]{:S(2)}, u32[]{:S(2)}) collective-permute-start(bf16[128,1536]{1,0:T(8,128)(2,1)} %copy-done.76), channel_id=1, source_target_pairs={{0,16},{8,24},{16,0},{24,8},{1,17},{9,25},{17,1},{25,9},{2,18},{10... | collective-permute-start | bytes 1179656 | tf_op jit(solution)/shard_map/ppermute | solution.py:23
  389.3 101.1 %collective-permute-start.54 = (bf16[128,1536]{1,0:T(8,128)(2,1)}, bf16[128,1536]{1,0:T(8,128)(2,1)}, u32[]{:S(2)}, u32[]{:S(2)}) collective-permute-start(bf16[128,1536]{1,0:T(8,128)(2,1)} %copy-done.76), channel_id=1, source_target_pairs={{0,8},{8,0},{16,24},{24,16},{1,9},{9,1},{17,25},{25,17},{2,10},{10... | collective-permute-start | bytes 1179656 | tf_op jit(solution)/shard_map/ppermute | solution.py:23
  407.9 29.0 %collective-permute-start.28 = (bf16[128,1536]{1,0:T(8,128)(2,1)}, bf16[128,1536]{1,0:T(8,128)(2,1)}, u32[]{:S(2)}, u32[]{:S(2)}) collective-permute-start(bf16[128,1536]{1,0:T(8,128)(2,1)} %fusion.69), channel_id=1, source_target_pairs={{0,16},{8,24},{16,0},{24,8},{1,17},{9,25},{17,1},{25,9},{2,18},{10... | collective-permute-start | bytes 1179656 | tf_op jit(solution)/shard_map/ppermute | solution.py:23
  430.5 54.3 %collective-permute-start.35 = (bf16[2,384,512]{2,1,0:T(8,128)(2,1)}, bf16[2,384,512]{2,1,0:T(8,128)(2,1)}, u32[]{:S(2)}, u32[]{:S(2)}) collective-permute-start(bf16[2,384,512]{2,1,0:T(8,128)(2,1)} %pad_maximum_fusion.18), channel_id=1, source_target_pairs={{0,1},{1,2},{2,3},{3,4},{4,5},{5,6},{6,7},{8,9},{9,10},{10,11},{11... | collective-permute-start | bytes 2359304 | tf_op jit(solution)/shard_map/ppermute | solution.py:29
  450.3 34.6 %collective-permute-start.34 = (bf16[2,384,512]{2,1,0:T(8,128)(2,1)}, bf16[2,384,512]{2,1,0:T(8,128)(2,1)}, u32[]{:S(2)}, u32[]{:S(2)}) collective-permute-start(bf16[2,384,512]{2,1,0:T(8,128)(2,1)} %pad_maximum_fusion.17), channel_id=1, source_target_pairs={{1,0},{2,1},{3,2},{4,3},{5,4},{6,5},{7,6},{9,8},{10,9},{11,10},{12... | collective-permute-start | bytes 2359304 | tf_op jit(solution)/shard_map/ppermute | solution.py:29
  470.1 40.0 %collective-permute-start.73 = (bf16[192,1536]{1,0:T(8,128)(2,1)}, bf16[192,1536]{1,0:T(8,128)(2,1)S(1)}, u32[]{:S(2)}, u32[]{:S(2)}) collective-permute-start(bf16[192,1536]{1,0:T(8,128)(2,1)} %get-tuple-element.211), channel_id=1, source_target_pairs={{0,2},{1,3},{8,10},{9,11},{16,18},{17,19},{24,26},{25,27}} | collective-permute-start | bytes 1769480 | tf_op jit(solution)/shard_map/ppermute | solution.py:120
  477.6 32.6 %collective-permute-start.74 = (bf16[192,1536]{1,0:T(8,128)(2,1)S(1)}, bf16[192,1536]{1,0:T(8,128)(2,1)S(1)}, u32[]{:S(2)}, u32[]{:S(2)}) collective-permute-start(bf16[192,1536]{1,0:T(8,128)(2,1)S(1)} %copy-done.106), channel_id=1, source_target_pairs={{6,4},{7,5},{14,12},{15,13},{22,20},{23,21},{30,28},{31,29}} | collective-permute-start | bytes 1769480 | tf_op jit(solution)/shard_map/ppermute | solution.py:121
  484.9 19.3 %collective-permute-start.30 = (bf16[256,384]{1,0:T(8,128)(2,1)S(1)}, bf16[256,384]{1,0:T(8,128)(2,1)S(1)}, u32[]{:S(2)}, u32[]{:S(2)}) collective-permute-start(bf16[256,384]{1,0:T(8,128)(2,1)S(1)} %copy-done.119), channel_id=1, source_target_pairs={{0,8},{8,0},{16,24},{24,16},{1,9},{9,1},{17,25},{25,17},{2,10},{10... | collective-permute-start | bytes 589832 | tf_op jit(solution)/shard_map/ppermute | solution.py:23
  490.4 22.2 %collective-permute-start.80 = (bf16[192,1536]{1,0:T(8,128)(2,1)S(1)}, bf16[192,1536]{1,0:T(8,128)(2,1)S(1)}, u32[]{:S(2)}, u32[]{:S(2)}) collective-permute-start(bf16[192,1536]{1,0:T(8,128)(2,1)S(1)} %get-tuple-element.225), channel_id=1, source_target_pairs={{0,2},{1,3},{8,10},{9,11},{16,18},{17,19},{24,26},{25,27}} | collective-permute-start | bytes 1769480 | tf_op jit(solution)/shard_map/ppermute | solution.py:120
  491.7 21.3 %collective-permute-start.81 = (bf16[192,1536]{1,0:T(8,128)(2,1)S(1)}, bf16[192,1536]{1,0:T(8,128)(2,1)S(1)}, u32[]{:S(2)}, u32[]{:S(2)}) collective-permute-start(bf16[192,1536]{1,0:T(8,128)(2,1)S(1)} %get-tuple-element.226), channel_id=1, source_target_pairs={{6,4},{7,5},{14,12},{15,13},{22,20},{23,21},{30,28},{31,29}} | collective-permute-start | bytes 1769480 | tf_op jit(solution)/shard_map/ppermute | solution.py:121
  510.1 20.3 %collective-permute-start.36 = (bf16[2,512,384]{2,1,0:T(8,128)(2,1)S(1)}, bf16[2,512,384]{2,1,0:T(8,128)(2,1)S(1)}, u32[]{:S(2)}, u32[]{:S(2)}) collective-permute-start(bf16[2,512,384]{2,1,0:T(8,128)(2,1)S(1)} %pad_maximum_fusion.19), channel_id=1, source_target_pairs={{0,8},{8,0},{16,24},{24,16},{1,9},{9,1},{17,25},{25,17},{2,10},{10... | collective-permute-start | bytes 2359304 | tf_op jit(solution)/shard_map/ppermute | solution.py:23
  510.4 14.8 %collective-permute-start.75 = (bf16[192,1536]{1,0:T(8,128)(2,1)S(1)}, bf16[192,1536]{1,0:T(8,128)(2,1)S(1)}, u32[]{:S(2)}, u32[]{:S(2)}) collective-permute-start(bf16[192,1536]{1,0:T(8,128)(2,1)S(1)} %get-tuple-element.215), channel_id=1, source_target_pairs={{0,2},{1,3},{2,4},{3,5},{8,10},{9,11},{10,12},{11,13},{16,18},{17,... | collective-permute-start | bytes 1769480 | tf_op jit(solution)/shard_map/ppermute | solution.py:120
  511.8 17.9 %collective-permute-start.76 = (bf16[192,1536]{1,0:T(8,128)(2,1)S(1)}, bf16[192,1536]{1,0:T(8,128)(2,1)S(1)}, u32[]{:S(2)}, u32[]{:S(2)}) collective-permute-start(bf16[192,1536]{1,0:T(8,128)(2,1)S(1)} %get-tuple-element.216), channel_id=1, source_target_pairs={{6,4},{7,5},{4,2},{5,3},{14,12},{15,13},{12,10},{13,11},{22,20},{2... | collective-permute-start | bytes 1769480 | tf_op jit(solution)/shard_map/ppermute | solution.py:121
  512.5 41.0 %collective-permute-start.44 = (bf16[1152,512]{1,0:T(8,128)(2,1)S(1)}, bf16[1152,512]{1,0:T(8,128)(2,1)S(1)}, u32[]{:S(2)}, u32[]{:S(2)}) collective-permute-start(bf16[1152,512]{1,0:T(8,128)(2,1)S(1)} %pad_maximum_fusion.9), channel_id=1, source_target_pairs={{0,1},{1,0},{2,3},{3,2},{4,5},{5,4},{6,7},{7,6},{8,9},{9,8},{10,11... | collective-permute-start | bytes 3538952 | tf_op jit(solution)/shard_map/ppermute | solution.py:23
  513.0 82.7 %collective-permute-start.64 = (bf16[4,192,1536]{2,1,0:T(8,128)(2,1)}, bf16[4,192,1536]{2,1,0:T(8,128)(2,1)}, u32[]{:S(2)}, u32[]{:S(2)}) collective-permute-start(bf16[4,192,1536]{2,1,0:T(8,128)(2,1)} %dynamic-slice_bitcast_fusion), channel_id=1, source_target_pairs={{0,1},{1,0},{2,3},{3,2},{4,5},{5,4},{6,7},{7,6},{8,9},{9,8},{10,11... | collective-permute-start | bytes 7077896 | tf_op jit(solution)/shard_map/ppermute | solution.py:23
  525.2 17.0 %collective-permute-start.82 = (bf16[192,1536]{1,0:T(8,128)(2,1)S(1)}, bf16[192,1536]{1,0:T(8,128)(2,1)S(1)}, u32[]{:S(2)}, u32[]{:S(2)}) collective-permute-start(bf16[192,1536]{1,0:T(8,128)(2,1)S(1)} %get-tuple-element.229), channel_id=1, source_target_pairs={{0,2},{1,3},{2,4},{3,5},{8,10},{9,11},{10,12},{11,13},{16,18},{17,... | collective-permute-start | bytes 1769480 | tf_op jit(solution)/shard_map/ppermute | solution.py:120
  529.7 17.8 %collective-permute-start.83 = (bf16[192,1536]{1,0:T(8,128)(2,1)S(1)}, bf16[192,1536]{1,0:T(8,128)(2,1)S(1)}, u32[]{:S(2)}, u32[]{:S(2)}) collective-permute-start(bf16[192,1536]{1,0:T(8,128)(2,1)S(1)} %get-tuple-element.230), channel_id=1, source_target_pairs={{6,4},{7,5},{4,2},{5,3},{14,12},{15,13},{12,10},{13,11},{22,20},{2... | collective-permute-start | bytes 1769480 | tf_op jit(solution)/shard_map/ppermute | solution.py:121
  530.6 18.3 %collective-permute-start.37 = (bf16[512,384]{1,0:T(8,128)(2,1)S(1)}, bf16[512,384]{1,0:T(8,128)(2,1)S(1)}, u32[]{:S(2)}, u32[]{:S(2)}) collective-permute-start(bf16[512,384]{1,0:T(8,128)(2,1)S(1)} %fusion.70), channel_id=1, source_target_pairs={{0,16},{8,24},{16,0},{24,8},{1,17},{9,25},{17,1},{25,9},{2,18},{10... | collective-permute-start | bytes 1179656 | tf_op jit(solution)/shard_map/ppermute | solution.py:23
  542.3 50.7 %collective-permute-start.77 = (bf16[192,1536]{1,0:T(8,128)(2,1)}, bf16[192,1536]{1,0:T(8,128)(2,1)}, u32[]{:S(2)}, u32[]{:S(2)}) collective-permute-start(bf16[192,1536]{1,0:T(8,128)(2,1)} %get-tuple-element.219), channel_id=1, source_target_pairs={{0,2},{1,3},{2,4},{3,5},{4,6},{5,7},{8,10},{9,11},{10,12},{11,13},... | collective-permute-start | bytes 1769480 | tf_op jit(solution)/shard_map/ppermute | solution.py:120
  547.5 46.9 %collective-permute-start.78 = (bf16[192,1536]{1,0:T(8,128)(2,1)}, bf16[192,1536]{1,0:T(8,128)(2,1)}, u32[]{:S(2)}, u32[]{:S(2)}) collective-permute-start(bf16[192,1536]{1,0:T(8,128)(2,1)} %get-tuple-element.220), channel_id=1, source_target_pairs={{6,4},{7,5},{4,2},{5,3},{2,0},{3,1},{14,12},{15,13},{12,10},{13,11... | collective-permute-start | bytes 1769480 | tf_op jit(solution)/shard_map/ppermute | solution.py:121
  569.3 26.4 %collective-permute-start.46 = (bf16[192,1152]{1,0:T(8,128)(2,1)S(1)}, bf16[192,1152]{1,0:T(8,128)(2,1)S(1)}, u32[]{:S(2)}, u32[]{:S(2)}) collective-permute-start(bf16[192,1152]{1,0:T(8,128)(2,1)S(1)} %get-tuple-element.167), channel_id=1, source_target_pairs={{0,2},{1,3},{8,10},{9,11},{16,18},{17,19},{24,26},{25,27}} | collective-permute-start | bytes 1327112 | tf_op jit(solution)/shard_map/ppermute | solution.py:120
  592.9 15.1 %collective-permute-start.84 = (bf16[192,1536]{1,0:T(8,128)(2,1)S(1)}, bf16[192,1536]{1,0:T(8,128)(2,1)S(1)}, u32[]{:S(2)}, u32[]{:S(2)}) collective-permute-start(bf16[192,1536]{1,0:T(8,128)(2,1)S(1)} %copy-done.108), channel_id=1, source_target_pairs={{0,2},{1,3},{2,4},{3,5},{4,6},{5,7},{8,10},{9,11},{10,12},{11,13},... | collective-permute-start | bytes 1769480 | tf_op jit(solution)/shard_map/ppermute | solution.py:120
  594.4 17.2 %collective-permute-start.85 = (bf16[192,1536]{1,0:T(8,128)(2,1)S(1)}, bf16[192,1536]{1,0:T(8,128)(2,1)S(1)}, u32[]{:S(2)}, u32[]{:S(2)}) collective-permute-start(bf16[192,1536]{1,0:T(8,128)(2,1)S(1)} %copy-done.107), channel_id=1, source_target_pairs={{6,4},{7,5},{4,2},{5,3},{2,0},{3,1},{14,12},{15,13},{12,10},{13,11... | collective-permute-start | bytes 1769480 | tf_op jit(solution)/shard_map/ppermute | solution.py:121
  598.8 30.3 %collective-permute-start.65 = (bf16[192,1536]{1,0:T(8,128)(2,1)S(1)}, bf16[192,1536]{1,0:T(8,128)(2,1)S(1)}, u32[]{:S(2)}, u32[]{:S(2)}) collective-permute-start(bf16[192,1536]{1,0:T(8,128)(2,1)S(1)} %get-tuple-element.195), channel_id=1, source_target_pairs={{0,2},{1,3},{8,10},{9,11},{16,18},{17,19},{24,26},{25,27}} | collective-permute-start | bytes 1769480 | tf_op jit(solution)/shard_map/ppermute | solution.py:120
  604.5 24.6 %collective-permute-start.66 = (bf16[192,1536]{1,0:T(8,128)(2,1)S(1)}, bf16[192,1536]{1,0:T(8,128)(2,1)S(1)}, u32[]{:S(2)}, u32[]{:S(2)}) collective-permute-start(bf16[192,1536]{1,0:T(8,128)(2,1)S(1)} %get-tuple-element.196), channel_id=1, source_target_pairs={{6,4},{7,5},{14,12},{15,13},{22,20},{23,21},{30,28},{31,29}} | collective-permute-start | bytes 1769480 | tf_op jit(solution)/shard_map/ppermute | solution.py:121
  605.4 23.7 %collective-permute-start.48 = (bf16[192,1152]{1,0:T(8,128)(2,1)S(1)}, bf16[192,1152]{1,0:T(8,128)(2,1)S(1)}, u32[]{:S(2)}, u32[]{:S(2)}) collective-permute-start(bf16[192,1152]{1,0:T(8,128)(2,1)S(1)} %get-tuple-element.171), channel_id=1, source_target_pairs={{0,2},{1,3},{2,4},{3,5},{8,10},{9,11},{10,12},{11,13},{16,18},{17,... | collective-permute-start | bytes 1327112 | tf_op jit(solution)/shard_map/ppermute | solution.py:120
  608.0 21.1 %collective-permute-start.49 = (bf16[192,1152]{1,0:T(8,128)(2,1)S(1)}, bf16[192,1152]{1,0:T(8,128)(2,1)S(1)}, u32[]{:S(2)}, u32[]{:S(2)}) collective-permute-start(bf16[192,1152]{1,0:T(8,128)(2,1)S(1)} %get-tuple-element.172), channel_id=1, source_target_pairs={{6,4},{7,5},{4,2},{5,3},{14,12},{15,13},{12,10},{13,11},{22,20},{2... | collective-permute-start | bytes 1327112 | tf_op jit(solution)/shard_map/ppermute | solution.py:121
  629.4 29.8 %collective-permute-start.67 = (bf16[192,1536]{1,0:T(8,128)(2,1)S(1)}, bf16[192,1536]{1,0:T(8,128)(2,1)S(1)}, u32[]{:S(2)}, u32[]{:S(2)}) collective-permute-start(bf16[192,1536]{1,0:T(8,128)(2,1)S(1)} %get-tuple-element.199), channel_id=1, source_target_pairs={{0,2},{1,3},{2,4},{3,5},{8,10},{9,11},{10,12},{11,13},{16,18},{17,... | collective-permute-start | bytes 1769480 | tf_op jit(solution)/shard_map/ppermute | solution.py:120
  633.9 25.4 %collective-permute-start.68 = (bf16[192,1536]{1,0:T(8,128)(2,1)S(1)}, bf16[192,1536]{1,0:T(8,128)(2,1)S(1)}, u32[]{:S(2)}, u32[]{:S(2)}) collective-permute-start(bf16[192,1536]{1,0:T(8,128)(2,1)S(1)} %get-tuple-element.200), channel_id=1, source_target_pairs={{6,4},{7,5},{4,2},{5,3},{14,12},{15,13},{12,10},{13,11},{22,20},{2... | collective-permute-start | bytes 1769480 | tf_op jit(solution)/shard_map/ppermute | solution.py:121
  634.8 20.3 %collective-permute-start.50 = (bf16[192,1152]{1,0:T(8,128)(2,1)S(1)}, bf16[192,1152]{1,0:T(8,128)(2,1)S(1)}, u32[]{:S(2)}, u32[]{:S(2)}) collective-permute-start(bf16[192,1152]{1,0:T(8,128)(2,1)S(1)} %get-tuple-element.175), channel_id=1, source_target_pairs={{0,2},{1,3},{2,4},{3,5},{4,6},{5,7},{8,10},{9,11},{10,12},{11,13},... | collective-permute-start | bytes 1327112 | tf_op jit(solution)/shard_map/ppermute | solution.py:120
  659.6 20.5 %collective-permute-start.69 = (bf16[192,1536]{1,0:T(8,128)(2,1)S(1)}, bf16[192,1536]{1,0:T(8,128)(2,1)S(1)}, u32[]{:S(2)}, u32[]{:S(2)}) collective-permute-start(bf16[192,1536]{1,0:T(8,128)(2,1)S(1)} %get-tuple-element.203), channel_id=1, source_target_pairs={{0,2},{1,3},{2,4},{3,5},{4,6},{5,7},{8,10},{9,11},{10,12},{11,13},... | collective-permute-start | bytes 1769480 | tf_op jit(solution)/shard_map/ppermute | solution.py:120
  670.3 13.8 %collective-permute-start.70 = (bf16[192,1536]{1,0:T(8,128)(2,1)S(1)}, bf16[192,1536]{1,0:T(8,128)(2,1)S(1)}, u32[]{:S(2)}, u32[]{:S(2)}) collective-permute-start(bf16[192,1536]{1,0:T(8,128)(2,1)S(1)} %get-tuple-element.204), channel_id=1, source_target_pairs={{6,4},{7,5},{4,2},{5,3},{2,0},{3,1},{14,12},{15,13},{12,10},{13,11... | collective-permute-start | bytes 1769480 | tf_op jit(solution)/shard_map/ppermute | solution.py:121
  (194 other events, 1361.7 us)

commit v2 on v1

v2 whole, which is shorter than its diff:
```python
import functools
import math

import jax
import jax.numpy as jnp
from jax import lax
from jax.experimental import pallas as pl
from jax.experimental.pallas import tpu as pltpu
from jax.sharding import PartitionSpec as P

HEAD_SIZE = 64
ROW_MIN = 2048
TILE = 256
GROUP = 3
BF16 = jnp.bfloat16
F32 = jnp.float32


def after(value, token):
    return lax.optimization_barrier((value, token))[0]


def swap(value, axis, by):
    return lax.ppermute(value, axis, [(i, i ^ by) for i in range(lax.axis_size(axis))])


def shift(value, axis, by):
    peers = lax.axis_size(axis)
    pairs = [(i, i + by) for i in range(peers) if 0 <= i + by < peers]
    return lax.ppermute(value, axis, pairs)


def tensor_place():
    place = lax.axis_index("tensor")
    return place // 2, place % 2


def ordered(own, far, mate, far_mate, axis):
    side, core = tensor_place()
    near = (jnp.where(core == 0, own, mate), jnp.where(core == 0, mate, own))
    away = (jnp.where(core == 0, far, far_mate), jnp.where(core == 0, far_mate, far))
    low = [jnp.where(side == 0, n, a) for n, a in zip(near, away)]
    high = [jnp.where(side == 0, a, n) for n, a in zip(near, away)]
    return jnp.concatenate(low + high, axis)


def gather_near(own):
    far = swap(own, "tensor", 2)
    return own, swap(own, "tensor", 1), far, swap(far, "tensor", 1)


def gather_staged(own, first, second):
    far = swap(after(own, first), "tensor", 2)
    far, late = after((far, own), second)
    return own, swap(late, "tensor", 1), far, swap(far, "tensor", 1)


def gather(own, axis):
    own, mate, far, far_mate = gather_near(own)
    return ordered(own, far, mate, far_mate, axis)


def scatter_near(away, near):
    got = swap(away.astype(BF16), "tensor", 1)
    size = away.shape[0] // 2
    low = (near[size:] + got[size:].astype(F32)).astype(BF16)
    return near[:size] + got[:size].astype(F32), swap(low, "tensor", 2), low


def rows_to_cols(own, mate, far, far_mate, later):
    width = own.shape[1]
    got = after(swap(jnp.concatenate([far, far_mate], 1), "tensor", 2), later)
    other = swap(jnp.concatenate([mate, got[:, width:]], 0), "tensor", 1)
    size = own.shape[0]
    return jnp.concatenate([own, other[:size], got[:, :width], other[size:]], 0)


def quarters(value, axis):
    return jnp.split(value, 4, axis)


def own_blocks(near):
    return jnp.concatenate([quarters(value, 1)[r] for r, value in enumerate(near)], 0)


def trade(value, start, done):
    return after(swap(after(value, start), "seq", 1), done)


def halve(blocks, bit, start, done):
    count, rows, cols = blocks.shape
    side = (lax.axis_index("seq") >> bit) % 2
    parts = blocks.reshape(count // 2, 2, rows, cols)
    send = lax.dynamic_index_in_dim(parts, 1 - side, 1, False)
    keep = lax.dynamic_index_in_dim(parts, side, 1, False)
    got = after(swap(after(send, start), "seq", 1 << bit), done)
    return keep.astype(F32) + got.astype(F32)


def halve_all(blocks, bit, *tokens):
    while blocks.shape[0] > 1:
        blocks = halve(blocks.astype(BF16), bit, tokens[0], tokens[1])
        tokens, bit = tokens[2:] or tokens, bit + 1
    return blocks[0]


def reduce_small(vectors):
    count = lax.axis_size("seq")
    kinds, width = vectors.shape
    parts = vectors.reshape(kinds, count, width // count).transpose(1, 0, 2)
    bit = 0
    while parts.shape[0] > 1:
        parts = halve(parts, bit, parts, parts)
        bit += 1
    return parts[0]


def frame_clip_labels(segment, row_length):
    frame_index = jnp.arange(segment.shape[0], dtype=jnp.int32)
    border = (frame_index % row_length == 0) | (segment != jnp.roll(segment, 1))
    clip_starts = lax.cummax(jnp.where(border, frame_index, 0), axis=0)
    return (clip_starts, (frame_index - clip_starts + 1).astype(jnp.float32))


def tile_ranges(q_labels, key_labels):
    q = q_labels.reshape(-1, TILE)
    k = key_labels.reshape(-1, TILE)
    meets = (k[None, :, 0] <= q[:, None, -1]) & (k[None, :, -1] >= q[:, None, 0])
    index = jnp.arange(k.shape[0], dtype=jnp.int32)[None]
    low = jnp.min(jnp.where(meets, index, k.shape[0]), 1)
    high = jnp.max(jnp.where(meets, index + 1, 0), 1)
    return jnp.stack([low, high], 1).reshape(-1)

def head_rows(g):
    return slice(g * HEAD_SIZE, (g + 1) * HEAD_SIZE)

def fill_natural(dest, refs):
    size = refs[0].shape[1]
    for part, ref in enumerate(refs):
        dest[part * size : (part + 1) * size, :] = ref[...].T

def sums_over(left, right):
    return lax.dot_general(left, right, (((1,), (0,)), ((), ())), preferred_element_type=F32)

def across(left, right):
    return lax.dot_general(left, right, (((1,), (1,)), ((), ())), preferred_element_type=F32)

def forward_body(span, q, k0, k1, k2, v0, v1, v2, tk, tv, qlab, klab, out, lse, keys, vals):
    rows, size = q.shape
    group = rows // HEAD_SIZE
    fill_natural(keys, (k0, k1, k2))
    for part, ref in enumerate((v0, v1, v2)):
        for piece in range(size // TILE):
            vals[part * (size // TILE) + piece] = ref[:, piece * TILE : (piece + 1) * TILE]
    for tile in range(size // TILE):
        cols = slice(tile * TILE, (tile + 1) * TILE)
        lab = qlab[:, cols]
        state = []
        for g in range(group):
            part = q[head_rows(g), cols].astype(F32)
            top = jnp.sum(part * tk[head_rows(g), :], 0, keepdims=True)
            state += [
                top,
                jnp.ones_like(top),
                jnp.broadcast_to(tv[head_rows(g), :], (HEAD_SIZE, TILE)),
            ]

        def step(j, state):
            start = pl.multiple_of(j * TILE, TILE)
            seen = klab[pl.ds(start, TILE), :] == lab
            fresh = []
            for g in range(group):
                top, total, acc = state[3 * g : 3 * g + 3]
                s = sums_over(keys[pl.ds(start, TILE), head_rows(g)], q[head_rows(g), cols])
                s = jnp.where(seen, s, -1e30)
                new = jnp.maximum(top, jnp.max(s, 0, keepdims=True))
                fade = jnp.exp(top - new)
                p = jnp.exp(s - new)
                total = total * fade + jnp.sum(p, 0, keepdims=True)
                acc = acc * fade + sums_over(vals[j, head_rows(g), :], p.astype(BF16))
                fresh += [new, total, acc]
            return tuple(fresh)

        state = lax.fori_loop(span[2 * tile], span[2 * tile + 1], step, tuple(state))
        for g in range(group):
            top, total, acc = state[3 * g : 3 * g + 3]
            out[head_rows(g), cols] = (acc / total).astype(BF16)
            lse[0, g : g + 1, cols] = top + jnp.log(total)

def backward_body(span, q, k0, k1, k2, v0, v1, v2, tk, tv, qlab, klab, out, lse, og,
                  dq, dk0, dk1, dk2, dv0, dv1, dv2, dtk, dtv, keys, vals, tkeys, ak, av):
    rows, size = q.shape
    group = rows // HEAD_SIZE
    pieces = size // TILE
    fill_natural(keys, (k0, k1, k2))
    fill_natural(vals, (v0, v1, v2))
    for part, ref in enumerate((k0, k1, k2)):
        for piece in range(pieces):
            tkeys[part * pieces + piece] = ref[:, piece * TILE : (piece + 1) * TILE]
    ak[...] = jnp.zeros_like(ak)
    av[...] = jnp.zeros_like(av)
    for tile in range(pieces):
        cols = slice(tile * TILE, (tile + 1) * TILE)
        lab = qlab[:, cols]
        state, norms, deltas = [], [], []
        for g in range(group):
            hr = head_rows(g)
            qf = q[hr, cols].astype(F32)
            gf = og[hr, cols].astype(F32)
            norm = lse[0, g : g + 1, cols]
            delta = jnp.sum(gf * out[hr, cols].astype(F32), 0, keepdims=True)
            pt = jnp.exp(jnp.sum(qf * tk[hr, :], 0, keepdims=True) - norm)
            st = pt * (jnp.sum(gf * tv[hr, :], 0, keepdims=True) - delta)
            gk = jnp.sum(qf * st, 1, keepdims=True)
            gv = jnp.sum(gf * pt, 1, keepdims=True)
            if tile == 0:
                dtk[hr, :] = gk
                dtv[hr, :] = gv
            else:
                dtk[hr, :] += gk
                dtv[hr, :] += gv
            state.append(tk[hr, :] * st)
            norms.append(norm)
            deltas.append(delta)

        def step(j, state):
            start = pl.multiple_of(j * TILE, TILE)
            seen = klab[pl.ds(start, TILE), :] == lab
            fresh = []
            for g in range(group):
                hr = head_rows(g)
                s = sums_over(keys[pl.ds(start, TILE), hr], q[hr, cols])
                p = jnp.exp(jnp.where(seen, s, -1e30) - norms[g])
                m = sums_over(vals[pl.ds(start, TILE), hr], og[hr, cols])
                ds = (p * (m - deltas[g])).astype(BF16)
                av[j, hr, :] += across(og[hr, cols], p.astype(BF16))
                ak[j, hr, :] += across(q[hr, cols], ds)
                fresh.append(state[g] + sums_over(tkeys[j, hr, :], ds))
            return tuple(fresh)

        state = lax.fori_loop(span[2 * tile], span[2 * tile + 1], step, tuple(state))
        for g in range(group):
            dq[head_rows(g), cols] = state[g]
    for part, (dk, dv) in enumerate(((dk0, dv0), (dk1, dv1), (dk2, dv2))):
        for piece in range(pieces):
            at = slice(piece * TILE, (piece + 1) * TILE)
            dk[:, at] = ak[part * pieces + piece].astype(dk.dtype)
            dv[:, at] = av[part * pieces + piece].astype(dv.dtype)

def attend(span, q, ks, vs, tk, tv, qlab, klab):
    cols, size = q.shape
    gr = GROUP * HEAD_SIZE
    steps = cols // gr
    block = pl.BlockSpec((gr, size), lambda i, s: (i, 0))
    column = pl.BlockSpec((gr, 1), lambda i, s: (i, 0))
    return pl.pallas_call(
        forward_body,
        grid_spec=pltpu.PrefetchScalarGridSpec(
            num_scalar_prefetch=1,
            grid=(steps,),
            in_specs=[block] * 7 + [column] * 2
            + [pl.BlockSpec((1, size), lambda i, s: (0, 0)), pl.BlockSpec((3 * size, 1), lambda i, s: (0, 0))],
            out_specs=[block, pl.BlockSpec((1, GROUP, size), lambda i, s: (i, 0, 0))],
            scratch_shapes=[pltpu.VMEM((3 * size, gr), BF16), pltpu.VMEM((3 * size // TILE, gr, TILE), BF16)],
        ),
        out_shape=[jax.ShapeDtypeStruct((cols, size), BF16), jax.ShapeDtypeStruct((steps, GROUP, size), F32)],
        name="attend", cost_estimate=FREE,
    )(span, q, *ks, *vs, tk, tv, qlab, klab)

def attend_back(span, q, ks, vs, tk, tv, qlab, klab, out, lse, og):
    cols, size = q.shape
    gr = GROUP * HEAD_SIZE
    steps = cols // gr
    tiles = 3 * size // TILE
    block = pl.BlockSpec((gr, size), lambda i, s: (i, 0))
    column = pl.BlockSpec((gr, 1), lambda i, s: (i, 0))
    small = jax.ShapeDtypeStruct((cols, 1), F32)
    wide = jax.ShapeDtypeStruct((cols, size), F32)
    low = jax.ShapeDtypeStruct((cols, size), BF16)
    return pl.pallas_call(
        backward_body,
        grid_spec=pltpu.PrefetchScalarGridSpec(
            num_scalar_prefetch=1,
            grid=(steps,),
            in_specs=[block] * 7 + [column] * 2
            + [pl.BlockSpec((1, size), lambda i, s: (0, 0)), pl.BlockSpec((3 * size, 1), lambda i, s: (0, 0)),
               block, pl.BlockSpec((1, GROUP, size), lambda i, s: (i, 0, 0)), block],
            out_specs=[block] * 7 + [column] * 2,
            scratch_shapes=[pltpu.VMEM((3 * size, gr), BF16), pltpu.VMEM((3 * size, gr), BF16),
                            pltpu.VMEM((tiles, gr, TILE), BF16),
                            pltpu.VMEM((tiles, gr, TILE), F32), pltpu.VMEM((tiles, gr, TILE), F32)],
        ),
        out_shape=[wide, low, wide, low, low, wide, low, small, small],
        name="attend_back", cost_estimate=FREE,
    )(span, q, *ks, *vs, tk, tv, qlab, klab, out, lse, og)


def rotary_tables(frame_positions):
    half_dim = HEAD_SIZE // 2
    frequency = jnp.exp(jnp.arange(half_dim, dtype=jnp.float32) * (-math.log(10000.0) / half_dim))
    angles = frequency[:, None] * frame_positions[None, :]
    return (jnp.cos(angles), jnp.sin(angles))


def rotate(rows, tables, sign=1.0):
    count, size = rows.shape
    halves = rows.reshape(count // HEAD_SIZE, 2, HEAD_SIZE // 2, size)
    cosine, sine = tables[0][None], tables[1][None] * sign
    first = halves[:, 0] * cosine - halves[:, 1] * sine
    second = halves[:, 1] * cosine + halves[:, 0] * sine
    return jnp.stack([first, second], 1).reshape(count, size)


def product(left, right):
    return jnp.dot(left, right, preferred_element_type=jnp.float32)


def inner_rows(left, right):
    return jnp.einsum("nd,nf->df", left, right, preferred_element_type=jnp.float32)


def back_project(gradient, weight):
    return jnp.einsum("nf,df->nd", gradient, weight, preferred_element_type=jnp.float32)


def by_feature(left, right):
    return jnp.einsum("nd,df->fn", left, right, preferred_element_type=jnp.float32)


def columns(weight, start, size):
    return lax.dynamic_slice_in_dim(weight, start, size, 1)


def rows_of(weight, start, size):
    return lax.dynamic_slice_in_dim(weight, start, size, 0)


def normalize(value_rows):
    means = jnp.mean(value_rows, -1, keepdims=True)
    centred = value_rows - means
    inverse = lax.rsqrt(jnp.mean(centred * centred, -1, keepdims=True) + 1e-05)
    return centred * inverse, inverse


def norm_backward(gradient, scaled, inverse, norm_gain):
    scaled_grad = gradient * norm_gain
    plain = jnp.mean(scaled_grad, -1, keepdims=True)
    cross = jnp.mean(scaled_grad * scaled, -1, keepdims=True)
    return inverse * (scaled_grad - plain - scaled * cross)


FREE = pl.CostEstimate(flops=1, transcendentals=0, bytes_accessed=1)


def dot_nn(left, right):
    return lax.dot_general(left, right, (((1,), (0,)), ((), ())), preferred_element_type=F32)


def dot_nt(left, right):
    return lax.dot_general(left, right, (((1,), (1,)), ((), ())), preferred_element_type=F32)


def dot_tn(left, right):
    return lax.dot_general(left, right, (((0,), (0,)), ((), ())), preferred_element_type=F32)


def head_weights(query, key, lanes, which):
    mine = jnp.where(lanes == which, query, jnp.zeros_like(query))
    scores = dot_nt(mine, key) * (1.0 / math.sqrt(HEAD_SIZE))
    weights = jnp.exp(scores - jnp.max(scores, -1, keepdims=True))
    return weights / jnp.sum(weights, -1, keepdims=True)


def cross_forward_body(rows, own, far, norms, q0, q1, q2, q3, kv, o0, o1, o2, o3,
                       normed_two, queries, crossed, first, second, normed_three):
    width = rows.shape[1]
    context_rows = kv.shape[0] // 2
    lanes = lax.broadcasted_iota(jnp.int32, (rows.shape[0], 2 * HEAD_SIZE), 1) // HEAD_SIZE
    residual = rows[...].astype(F32) + own[...] + far[...].astype(F32)
    first[...] = residual
    scaled, _ = normalize(residual)
    low = (scaled * norms[2:3, :] + norms[3:4, :]).astype(BF16)
    normed_two[...] = low
    part = width // 4
    for b, ref in enumerate((q0, q1, q2, q3)):
        queries[:, b * part : (b + 1) * part] = dot_nn(low, ref[...]).astype(BF16)
    for p in range(width // (2 * HEAD_SIZE)):
        cols = slice(p * 2 * HEAD_SIZE, (p + 1) * 2 * HEAD_SIZE)
        q, k, v = queries[:, cols], kv[:context_rows, cols], kv[context_rows:, cols]
        mixed = [dot_nn(head_weights(q, k, lanes, g).astype(BF16), v) for g in (0, 1)]
        crossed[:, cols] = jnp.where(lanes == 0, mixed[0], mixed[1]).astype(BF16)
    for b, ref in enumerate((o0, o1, o2, o3)):
        residual = residual + dot_nn(crossed[:, b * part : (b + 1) * part], ref[...])
    second[...] = residual
    scaled, _ = normalize(residual)
    normed_three[...] = (scaled * norms[4:5, :] + norms[5:6, :]).astype(BF16)


def cross_forward(rows, own, far, norms, query_parts, kv, out_parts):
    low = jax.ShapeDtypeStruct(rows.shape, BF16)
    wide = jax.ShapeDtypeStruct(rows.shape, F32)
    return pl.pallas_call(
        cross_forward_body, out_shape=[low, low, low, wide, wide, low],
        cost_estimate=FREE, name="cross",
    )(rows, own, far, norms, *query_parts, kv, *out_parts)


def deal_rows(rows, size, column, own, away):
    for b in range(rows.shape[0] // (2 * size)):
        at = slice(b * size, (b + 1) * size)
        even = rows[2 * b * size : (2 * b + 1) * size, :]
        odd = rows[(2 * b + 1) * size : (2 * b + 2) * size, :]

        @pl.when(column == 0)
        def _():
            own[at, :] = even
            away[at, :] = odd

        @pl.when(column != 0)
        def _():
            own[at, :] = odd
            away[at, :] = even


def ffn_body(width_block, unit_block, place, n0, n1, n2, n3, grad, gate_w, up_w, down_w,
             hidden, hid_own, hid_away, gate_grad, lifted_grad, nrm_own, nrm_away, away, near,
             normed, total):
    step = pl.program_id(0)
    share = n0.shape[0]
    column = place[0]

    @pl.when(step == 0)
    def _():
        for b, ref in enumerate((n0, n1, n2, n3)):
            normed[b * share : (b + 1) * share, :] = ref[...]
        total[...] = jnp.zeros_like(total)
        deal_rows(normed[...].T, width_block, column, nrm_own, nrm_away)

    gate = dot_nn(normed[...], gate_w[...])
    lifted = dot_nn(normed[...], up_w[...])
    back = dot_nt(grad[...], down_w[...]).astype(BF16).astype(F32)
    sig = jax.nn.sigmoid(gate)
    swish = gate * sig
    low = (swish * lifted).astype(BF16)
    hidden[...] = low
    deal_rows(low.T, unit_block, column, hid_own, hid_away)
    gg = (back * lifted * sig * (1.0 + gate * (1.0 - sig))).astype(BF16)
    lg = (back * swish).astype(BF16)
    gate_grad[...] = gg
    lifted_grad[...] = lg
    total[...] += dot_nt(gg, gate_w[...]) + dot_nt(lg, up_w[...])

    @pl.when(step == pl.num_programs(0) - 1)
    def _():
        for b in (0, 1):
            near[b * share : (b + 1) * share, :] = total[2 * b * share : (2 * b + 1) * share, :]
            away[b * share : (b + 1) * share, :] = total[
                (2 * b + 1) * share : (2 * b + 2) * share, :
            ].astype(BF16)


def ffn(devices, place, parts, grad, gate_w, up_w, down_w):
    share, width = parts[0].shape
    size, units = 4 * share, gate_w.shape[1]
    tile = units // 2
    whole = lambda r, c: pl.BlockSpec((r, c), lambda i, s: (0, 0))
    cols = lambda r: pl.BlockSpec((r, tile), lambda i, s: (0, i))
    rows = lambda c: pl.BlockSpec((tile, c), lambda i, s: (i, 0))
    halves = pl.BlockSpec((tile // 2, size), lambda i, s: (i, 0))
    low = lambda r, c: jax.ShapeDtypeStruct((r, c), BF16)
    return pl.pallas_call(
        functools.partial(ffn_body, width // devices, units // devices),
        grid_spec=pltpu.PrefetchScalarGridSpec(
            num_scalar_prefetch=1,
            grid=(2,),
            in_specs=[whole(share, width)] * 4
            + [whole(size, width), cols(width), cols(width), rows(width)],
            out_specs=[cols(size), halves, halves, cols(size), cols(size),
                       whole(width // 2, size), whole(width // 2, size),
                       whole(2 * share, width), whole(2 * share, width)],
            scratch_shapes=[pltpu.VMEM((size, width), BF16), pltpu.VMEM((size, width), F32)],
        ),
        out_shape=[low(size, units), low(units // 2, size), low(units // 2, size),
                   low(size, units), low(size, units), low(width // 2, size),
                   low(width // 2, size), low(2 * share, width),
                   jax.ShapeDtypeStruct((2 * share, width), F32)],
        cost_estimate=FREE, name="ffn",
    )(place, *parts, grad, gate_w, up_w, down_w)


def cross_backward_body(own, far, grad, first, second, norms, q0, q1, q2, q3, kv,
                        o0, o1, o2, o3, queries, grad_two, query_grad, kv_grad, vectors, grad_one,
                        crossed_grad):
    width = grad.shape[1]
    context_rows = kv.shape[0] // 2
    part = width // 4
    lanes = lax.broadcasted_iota(jnp.int32, (grad.shape[0], 2 * HEAD_SIZE), 1) // HEAD_SIZE
    lane_k = lax.broadcasted_iota(jnp.int32, (context_rows, 2 * HEAD_SIZE), 1) // HEAD_SIZE
    scale = 1.0 / math.sqrt(HEAD_SIZE)
    arrived = own[...] + far[...].astype(F32)
    scaled, inverse = normalize(second[...])
    vectors[0:1, :] = jnp.sum(arrived * scaled, 0, keepdims=True)
    vectors[1:2, :] = jnp.sum(arrived, 0, keepdims=True)
    two = grad[...].astype(F32) + norm_backward(arrived, scaled, inverse, norms[4:5, :])
    low = two.astype(BF16)
    grad_two[...] = low
    for b, ref in enumerate((o0, o1, o2, o3)):
        crossed_grad[:, b * part : (b + 1) * part] = dot_nt(low, ref[...]).astype(BF16)
    for p in range(width // (2 * HEAD_SIZE)):
        cols = slice(p * 2 * HEAD_SIZE, (p + 1) * 2 * HEAD_SIZE)
        q, k, v = queries[:, cols], kv[:context_rows, cols], kv[context_rows:, cols]
        g_rows = crossed_grad[:, cols]
        found = []
        for g in (0, 1):
            probs = head_weights(q, k, lanes, g)
            change = dot_nt(jnp.where(lanes == g, g_rows, jnp.zeros_like(g_rows)), v)
            delta = jnp.sum(change * probs, -1, keepdims=True)
            ds = (probs * (change - delta)).astype(BF16)
            found.append((dot_nn(ds, k), dot_tn(ds, q), dot_tn(probs.astype(BF16), g_rows)))
        query_grad[:, cols] = (
            jnp.where(lanes == 0, found[0][0], found[1][0]) * scale
        ).astype(BF16)
        kv_grad[:context_rows, cols] = (
            jnp.where(lane_k == 0, found[0][1], found[1][1]) * scale
        ).astype(BF16)
        kv_grad[context_rows:, cols] = jnp.where(lane_k == 0, found[0][2], found[1][2]).astype(
            BF16
        )
    back = jnp.zeros(grad.shape, F32)
    for b, ref in enumerate((q0, q1, q2, q3)):
        back = back + dot_nt(query_grad[:, b * part : (b + 1) * part], ref[...])
    scaled, inverse = normalize(first[...])
    vectors[2:3, :] = jnp.sum(back * scaled, 0, keepdims=True)
    vectors[3:4, :] = jnp.sum(back, 0, keepdims=True)
    grad_one[...] = (two + norm_backward(back, scaled, inverse, norms[2:3, :])).astype(BF16)


def cross_backward(own, far, grad, first, second, norms, query_parts, kv, out_parts, queries):
    rows, width = own.shape
    low = lambda r: jax.ShapeDtypeStruct((r, width), BF16)
    return pl.pallas_call(
        cross_backward_body,
        out_shape=[low(rows), low(rows), low(kv.shape[0]),
                   jax.ShapeDtypeStruct((4, width), F32), low(rows)],
        in_specs=[pl.BlockSpec((rows, width), lambda: (0, 0)), pl.BlockSpec((rows, width), lambda: (0, 0)),
                  pl.BlockSpec((rows, width), lambda: (0, 0))]
        + [pl.BlockSpec(memory_space=pltpu.VMEM)] * 13,
        scratch_shapes=[pltpu.VMEM((rows, width), BF16)],
        cost_estimate=FREE, name="cross_back",
    )(own, far, grad, first, second, norms, *query_parts, kv, *out_parts, queries)


def front_body(width_block, place, x0, x1, x2, x3, g0, g1, g2, g3, cosine, sine, wq, wk, wv,
               queries, pair, rows, low, nrm_own, nrm_away, norms, means, inverses, wide):
    size, part = x0.shape
    for r, (x, g) in enumerate(((x0, g0), (x1, g1), (x2, g2), (x3, g3))):
        start = pl.multiple_of((place[0] ^ r) * part, 128)
        wide[:, pl.ds(start, part)] = x[...]
        norms[:, pl.ds(start, part)] = g[...]
    share = size // 4
    rows[...] = wide[pl.ds(pl.multiple_of(place[0] * share, share), share), :]
    values = wide[...].astype(F32)
    mean = jnp.mean(values, -1, keepdims=True)
    centred = values - mean
    inverse = lax.rsqrt(jnp.mean(centred * centred, -1, keepdims=True) + 1e-05)
    means[...] = mean
    inverses[...] = inverse
    normed = (centred * inverse * norms[0:1, :] + norms[1:2, :]).astype(BF16)
    low[...] = normed
    half = HEAD_SIZE // 2

    def turned(weight):
        return dot_nn(normed, weight[...]).T

    def rotated(block, dest, scale):
        for h in range(part // HEAD_SIZE):
            a = block[h * HEAD_SIZE : h * HEAD_SIZE + half, :]
            b = block[h * HEAD_SIZE + half : (h + 1) * HEAD_SIZE, :]
            dest[h * HEAD_SIZE : h * HEAD_SIZE + half, :] = (
                (a * cosine[...] - b * sine[...]) * scale
            ).astype(BF16)
            dest[h * HEAD_SIZE + half : (h + 1) * HEAD_SIZE, :] = (
                (b * cosine[...] + a * sine[...]) * scale
            ).astype(BF16)

    rotated(turned(wk), pair.at[0], 1.0)
    pair[1] = turned(wv).astype(BF16)
    rotated(turned(wq), queries, 1.0 / math.sqrt(HEAD_SIZE))
    deal_rows(normed.T, width_block, place[1], nrm_own, nrm_away)


def front(devices, place, parts, norm_parts, tables, wq, wk, wv):
    size, part = parts[0].shape
    width = 4 * part
    low = lambda *s: jax.ShapeDtypeStruct(s, BF16)
    wide = lambda *s: jax.ShapeDtypeStruct(s, F32)
    vmem = pl.BlockSpec(memory_space=pltpu.VMEM)
    return pl.pallas_call(
        functools.partial(front_body, width // devices),
        in_specs=[pl.BlockSpec(memory_space=pltpu.SMEM)] + [vmem] * 13,
        out_specs=[vmem] * 9,
        out_shape=[low(part, size), low(2, part, size), low(size // 4, width), low(size, width),
                   low(width // 2, size), low(width // 2, size), wide(6, width),
                   wide(size, 1), wide(size, 1)],
        scratch_shapes=[pltpu.VMEM((size, width), BF16)],
        cost_estimate=FREE, name="front",
    )(place, *parts, *norm_parts, *tables, wq, wk, wv)


def per_device(
    frames,
    segment,
    time_token,
    context,
    gain_attn,
    bias_attn,
    gain_cross,
    bias_cross,
    gain_ffn,
    bias_ffn,
    w_query,
    w_key,
    w_value,
    w_out,
    c_query,
    c_key,
    c_value,
    c_out,
    w_gate,
    w_up,
    w_down,
    out_grad,
):
    local_rows = frames.shape[0]
    local_width = frames.shape[1]
    model_width = w_query.shape[0]
    head_cols = w_query.shape[1]
    heads = head_cols // HEAD_SIZE
    number_of_frames = lax.axis_size("seq") * local_rows
    row_length = min(max(ROW_MIN, 64 * lax.axis_size("seq")), number_of_frames)
    first_frame = lax.axis_index("seq") * local_rows
    own_start = lax.axis_index("tensor") * local_width

    def own_cols(value):
        return lax.dynamic_slice_in_dim(value, own_start, local_width, value.ndim - 1)

    place = lax.axis_index("tensor")
    share = local_rows // 4

    def own_rows(value):
        return rows_of(value, place * share, share)

    def row_block(value, index):
        return rows_of(value, index * share, share)

    place = lax.axis_index("tensor")
    share = local_rows // 4

    def own_rows(value):
        return rows_of(value, place * share, share)

    def row_block(value, index):
        return rows_of(value, index * share, share)

    column = lax.axis_index("seq") % 2
    frame_parts_near = gather_near(frames)
    norm_parts = gather_near(
        jnp.stack([gain_attn, bias_attn, gain_cross, bias_cross, gain_ffn, bias_ffn])
    )
    clip_starts, frame_positions = frame_clip_labels(segment, row_length)
    own_labels = lax.dynamic_slice_in_dim(clip_starts, first_frame, local_rows)
    own_positions = lax.dynamic_slice_in_dim(frame_positions, first_frame, local_rows)
    blanks = jnp.full((local_rows,), -1, jnp.int32)
    key_labels = lax.dynamic_slice_in_dim(
        jnp.concatenate([blanks, clip_starts, blanks]), first_frame, 3 * local_rows
    )
    spans = tile_ranges(own_labels, key_labels)
    label_row, label_column = own_labels[None, :], key_labels[:, None]
    row_index = first_frame // row_length
    time_row = lax.dynamic_slice_in_dim(time_token, row_index, 1, 0).astype(F32)
    row_context = lax.dynamic_slice_in_dim(context, row_index, 1, 0)[0]
    context_rows = row_context.shape[0]
    tables = rotary_tables(own_positions)
    score_scale = 1.0 / math.sqrt(HEAD_SIZE)
    all_heads = model_width // HEAD_SIZE

    (
        queries, both, frame_rows, frame_normed, one_own_half, one_away_half, norms, means_one,
        inverse_one,
    ) = front(
        lax.axis_size("seq"), jnp.stack([place, column]).astype(jnp.int32), frame_parts_near, norm_parts, tables,
        w_query, w_key, w_value,
    )
    own_keys, own_values = both[0], both[1]
    gain_one, bias_one = norms[0:1], norms[1:2]
    behind, ahead = shift(both, "seq", 1), shift(both, "seq", -1)
    query_far = swap(after(c_query, frame_parts_near[3]), "tensor", 2)
    out_far = swap(after(c_out, frame_parts_near[3]), "tensor", 2)
    time_late = after(time_row, both)
    scaled_time, _ = normalize(time_late)
    time_normed = (scaled_time * gain_one + bias_one).astype(BF16)
    time_keys = by_feature(time_normed, w_key).astype(BF16).astype(F32)
    time_values = by_feature(time_normed, w_value).astype(BF16).astype(F32)
    context_late = after(row_context, both)
    context_kv = jnp.concatenate(
        [product(context_late, c_key), product(context_late, c_value)], 0
    ).astype(BF16)
    kv_far = swap(context_kv, "tensor", 2)

    behind, ahead, query_far, out_far, kv_far = lax.optimization_barrier(
        (behind, ahead, query_far, out_far, kv_far)
    )
    keys = (behind[0], own_keys, ahead[0])
    values = (behind[1], own_values, ahead[1])
    attended, log_totals = attend(
        spans, queries, keys, values, time_keys, time_values, label_row, label_column
    )
    query_parts = (
        c_query, swap(after(c_query, both), "tensor", 1), query_far, swap(query_far, "tensor", 1)
    )
    out_parts = (c_out, swap(after(c_out, both), "tensor", 1), out_far, swap(out_far, "tensor", 1))
    kv_rows = jnp.concatenate([context_kv, kv_far], 0)
    kv_other = swap(kv_rows, "tensor", 1)
    count = context_kv.shape[0]
    cross_kv = jnp.concatenate([context_kv, kv_other[:count], kv_far, kv_other[count:]], 1)

    def out_rows(*relative):
        return jnp.concatenate(
            [
                jnp.einsum(
                    "fn,fd->nd",
                    lax.dynamic_slice_in_dim(attended, (place ^ r) * share, share, 1),
                    w_out,
                    preferred_element_type=F32,
                )
                for r in relative
            ],
            0,
        )

    one_own, one_far, one_near = scatter_near(out_rows(1, 3), out_rows(0, 2))
    normed_two, cross_queries, crossed, residual_one, residual_two, normed_share = cross_forward(
        frame_rows, one_own, one_far, norms, query_parts, cross_kv, out_parts
    )
    three_parts = gather_near(normed_share)
    own, mate, far, far_mate = gather_staged(out_grad, one_far, normed_share)
    grad_low = ordered(own, far, mate, far_mate, 1)
    grad_near = jnp.concatenate([row_block(grad_low, place ^ r) for r in range(4)], 0)
    (
        hidden, hidden_own, hidden_away, gate_grad, lifted_grad, three_own, three_away,
        normed_away, normed_near,
    ) = ffn(lax.axis_size("seq"), column.reshape(1), three_parts, grad_near, w_gate, w_up, w_down)
    three_sum, three_far, three_near = scatter_near(normed_away, normed_near)
    cross_full, cross_query_grad, kv_grad, norm_vectors, grad_one = cross_backward(
        three_sum, three_far, grad_near[:share], residual_one, residual_two, norms,
        query_parts, cross_kv, out_parts, cross_queries,
    )
    attend_full = gather(grad_one, 0)
    grad_heads = jnp.einsum(
        "nd,fd->fn", attend_full, w_out, preferred_element_type=F32
    ).astype(BF16)
    back = attend_back(
        spans, queries, keys, values, time_keys, time_values, label_row, label_column,
        attended, log_totals, grad_heads,
    )
    query_grad, key_prev, key_own, key_next, value_prev, value_own, value_next = back[:7]
    time_key_grad, time_value_grad = back[7], back[8]
    from_next = shift(jnp.stack([key_prev, value_prev]), "seq", -1)
    from_prev = shift(jnp.stack([key_next, value_next]), "seq", 1)
    query_raw = (rotate(query_grad, tables, -1.0) * score_scale).astype(BF16)
    key_raw = rotate(
        key_own + from_next[0].astype(F32) + from_prev[0].astype(F32), tables, -1.0
    ).astype(BF16)
    value_raw = (value_own + from_next[1].astype(F32) + from_prev[1].astype(F32)).astype(BF16)

    def to_frames(rows, weight):
        return jnp.einsum("fn,df->nd", rows, weight, preferred_element_type=F32)

    def frame_parts(*relative):
        return jnp.concatenate(
            [
                sum(
                    to_frames(rows, rows_of(weight, (place ^ r) * local_width, local_width))
                    for rows, weight in (
                        (query_raw, w_query), (key_raw, w_key), (value_raw, w_value)
                    )
                )
                for r in relative
            ],
            0,
        )

    last_own, last_far, last_near = scatter_near(frame_parts(1, 3), frame_parts(0, 2))
    frame_grad = last_own + last_far.astype(F32)
    time_grad = to_frames(time_key_grad.astype(BF16), w_key) + to_frames(
        time_value_grad.astype(BF16), w_value
    )
    own_scaled = (frames.astype(F32) - means_one) * inverse_one
    scaled_grad = frame_grad * gain_attn[None]
    sums = jnp.concatenate(
        [
            jnp.sum(scaled_grad, -1),
            jnp.sum(scaled_grad * own_scaled, -1),
            time_grad[0],
            norm_vectors.reshape(-1),
        ]
    )[None]
    sums = sums + swap(sums, "tensor", 1)
    sums = sums + swap(sums, "tensor", 2)
    plain = sums[0, :local_rows, None] / model_width
    cross = sums[0, local_rows : 2 * local_rows, None] / model_width
    vectors = own_cols(sums[0, 2 * local_rows :].reshape(5, model_width))
    d_frames = own_cols(attend_full).astype(F32) + inverse_one * (
        scaled_grad - plain - own_scaled * cross
    )
    d_gain_attn = jnp.sum(frame_grad * own_scaled, 0) + vectors[0] * own_cols(scaled_time)[0]
    d_bias_attn = jnp.sum(frame_grad, 0) + vectors[0]
    small = reduce_small(
        jnp.stack([d_gain_attn, d_bias_attn, vectors[3], vectors[4], vectors[1], vectors[2]])
    )

    def down_rows(*relative):
        late = after(hidden, three_sum)
        return jnp.concatenate([product(row_block(late, r), w_down) for r in relative], 0)

    down_own, down_far, _ = scatter_near(down_rows(1, 3), down_rows(0, 2))
    block_rows = (residual_two + (down_own + down_far.astype(F32))).astype(BF16)
    block_cols = rows_to_cols(
        *[
            lax.dynamic_slice_in_dim(block_rows, (place ^ r) * local_width, local_width, 1)
            for r in range(4)
        ],
        attend_full,
    )
    block_out = jnp.concatenate([row_block(block_cols, place ^ b) for b in range(4)], 0)

    kv_parts = quarters(after(kv_grad, attend_full), 1)
    kv_own, kv_away, _ = scatter_near(
        jnp.concatenate([kv_parts[1], kv_parts[3]], 0),
        jnp.concatenate([kv_parts[0], kv_parts[2]], 0).astype(F32),
    )
    context_own = kv_own + after(kv_away, query_grad).astype(F32)
    forward_near = gather_staged(jnp.concatenate([normed_two, crossed], 1), three_far, grad_one)
    two_full = jnp.concatenate([value[:, :model_width] for value in forward_near], 0)
    crossed_own = own_blocks([value[:, model_width:] for value in forward_near])
    back_near = gather_staged(
        jnp.concatenate([cross_full, cross_query_grad], 1), attend_full, query_grad
    )
    cross_grad_full = jnp.concatenate([value[:, :model_width] for value in back_near], 0)
    cross_query_own = own_blocks([value[:, model_width:] for value in back_near])
    time_column = time_normed.astype(F32).T

    def context_grads(kv):
        left = row_context.T
        both_grads = jnp.concatenate([kv[:context_rows], kv[context_rows:]], 1)
        return product(left, both_grads.astype(BF16))

    count = lax.axis_size("seq")

    def meet(rows, cols, spec):
        blocks = sum(
            jnp.einsum(spec, r, c, preferred_element_type=F32) for r, c in zip(rows, cols)
        )
        return blocks.reshape(count // 2, 2 * blocks.shape[0] // count, blocks.shape[1])

    normed_pair = (one_own_half, trade(one_away_half, attended, normed_share))
    grad_pair = (grad_near, trade(grad_near, normed_share, grad_one))
    hidden_pair = (hidden_own, trade(hidden_away, hidden, grad_one))
    three_pair = (three_own, trade(three_away, three_sum, query_grad))
    gate_pair = (gate_grad, trade(gate_grad, three_sum, query_grad))
    lifted_pair = (lifted_grad, trade(lifted_grad, grad_heads, from_next))

    down_blocks = meet(hidden_pair, grad_pair, "dn,nf->df").astype(BF16)
    grad_down = halve_all(down_blocks, 1, grad_one, query_grad, query_grad, from_next)
    gate_blocks = meet(three_pair, gate_pair, "dn,nf->df").astype(BF16)
    grad_gate_w = halve_all(gate_blocks, 1, query_grad, last_near, last_near, last_far)
    up_blocks = meet(three_pair, lifted_pair, "dn,nf->df").astype(BF16)
    grad_up_w = halve_all(up_blocks, 1, last_near, last_far, last_far, last_far)

    late = after((crossed_own, cross_grad_full), query_grad)
    grad_c_out = inner_rows(*late).astype(BF16)
    late = after((two_full, cross_query_own), query_grad)
    grad_c_query = inner_rows(*late).astype(BF16)
    grad_c_kv = context_grads(context_own).astype(BF16)
    late = after((attended, attend_full), query_grad)
    grad_w_out = product(*late).astype(BF16)
    part = head_cols // count
    bundle = jnp.concatenate(
        [
            value.reshape(count, part, model_width)
            for value in (grad_c_out, grad_c_query, grad_c_kv, grad_w_out)
        ],
        1,
    )
    middle = halve_all(
        bundle, 0, from_next, last_near, last_near, last_far, last_far, last_far
    )
    grad_c_out = middle[:part]
    grad_c_query = middle[part : 2 * part].reshape(model_width // count, head_cols)
    grad_c_kv = middle[2 * part : 3 * part].reshape(-1, 2 * head_cols)
    grad_w_out = middle[3 * part :]

    raw = jnp.concatenate([query_raw, key_raw, value_raw], 0)
    raw_pair = (raw, trade(raw, key_raw, last_near))
    time_both = jnp.concatenate([time_key_grad, time_value_grad], 0)
    time_both = time_both + trade(time_both, from_next, key_raw)
    own_time_rows = lax.dynamic_index_in_dim(
        time_column.reshape(count // 2, 2, -1), column, 1, False
    ).reshape(-1, 1)
    outer = own_time_rows * jnp.concatenate([jnp.zeros((head_cols, 1), F32), time_both], 0).T
    blocks = meet(normed_pair, raw_pair, "dn,fn->df")
    blocks = (blocks + outer.reshape(blocks.shape)).astype(BF16)
    heads_sum = halve_all(blocks, 1, last_far, last_far, last_far, last_far)
    grad_w_query, grad_w_key, grad_w_value = (
        heads_sum[:, i * head_cols : (i + 1) * head_cols] for i in range(3)
    )
    return (
        block_out,
        d_frames,
        small[0],
        small[1],
        small[2],
        small[3],
        small[4],
        small[5],
        grad_w_query,
        grad_w_key,
        grad_w_value,
        grad_w_out,
        grad_c_query,
        grad_c_kv[:, :head_cols],
        grad_c_kv[:, head_cols:],
        grad_c_out,
        grad_gate_w,
        grad_up_w,
        grad_down,
    )


def solution(mesh):
    return jax.shard_map(
        per_device,
        mesh=mesh,
        in_specs=(
            P("seq", "tensor"),
            P(),
            P(),
            P(),
            P("tensor"),
            P("tensor"),
            P("tensor"),
            P("tensor"),
            P("tensor"),
            P("tensor"),
            P(None, "tensor"),
            P(None, "tensor"),
            P(None, "tensor"),
            P("tensor", None),
            P(None, "tensor"),
            P(None, "tensor"),
            P(None, "tensor"),
            P("tensor", None),
            P(None, "tensor"),
            P(None, "tensor"),
            P("tensor", None),
            P("seq", "tensor"),
        ),
        out_specs=(
            P("seq", "tensor"),
            P("seq", "tensor"),
            P(("tensor", "seq")),
            P(("tensor", "seq")),
            P(("tensor", "seq")),
            P(("tensor", "seq")),
            P(("tensor", "seq")),
            P(("tensor", "seq")),
            P("seq", "tensor"),
            P("seq", "tensor"),
            P("seq", "tensor"),
            P(("tensor", "seq"), None),
            P("seq", "tensor"),
            P("seq", "tensor"),
            P("seq", "tensor"),
            P(("tensor", "seq"), None),
            P("seq", "tensor"),
            P("seq", "tensor"),
            P(("tensor", "seq"), None),
        ),
        check_vma=False,
    )
```

time: 698 us -> 611 us (0.88)
  Pallas kernels: 30.4 us -> 99.8 us
  matrix products: 119 us -> 58.1 us
  starting transfers between devices: 149 us -> 96.4 us
  other arithmetic: 93.3 us -> 51.2 us
  waiting for transfers between devices: 217 us -> 237 us
  local copies, waits for them, and re-layouts: 73.2 us -> 60.1 us
    ppermute x60 -> x65, waiting for transfers between devices: 117 us -> 210 us  [swap(): lax.ppermute(value, axis, [(i, i ^ by) for i in range(lax.axis_size(axis))])]
    ppermute x30 -> x0, starting transfers between devices: 84.2 us -> none  [the longest x12 52.7 us: line_sum(): up = lax.ppermute(rise, 'seq', climbs)]
    ppermute x30 -> x0, waiting for transfers between devices: 70.8 us -> none  [the longest x12 50 us: line_sum(): up = lax.ppermute(rise, 'seq', climbs)]
    pallas_call x0 -> x4, Pallas kernels: none -> 69.9 us  [the longest x1 25.9 us: ffn(): pl.pallas_call(functools.partial(ffn_body, width // devices, units // dev...]
    dot_general x22 -> x4, matrix products: 54.3 us -> 7.14 us  [out_rows(): jnp.einsum('fn,fd->nd', lax.dynamic_slice_in_dim(attended, (place ^ r) *...]
    ppermute x60 -> x65, starting transfers between devices: 51.9 us -> 87 us  [swap(): lax.ppermute(value, axis, [(i, i ^ by) for i in range(lax.axis_size(axis))])]
    convert_element_type x24 -> x12, other arithmetic: 23.3 us -> 10.7 us  [the longest x6 6.61 us: halve_all(): blocks = halve(blocks.astype(BF16), bit, tokens[0], tokens[1])]
    add x14 -> x6, other arithmetic: 14 us -> 1.42 us  [the longest x1 0.64 us: per_device(): d_bias_attn = jnp.sum(frame_grad, 0) + vectors[0]]
  transfers between devices with their start and end apart: 94 -> 69, of which waited for: 29 -> 17; matrix products, arithmetic and copies ran while one was open for 36% -> 24% of each run, Pallas kernels for 2% -> 13%
where the time goes in v2:
time: 611 us; the launch traced here: 607 us
  waiting for transfers between devices  237 us (39%)
  Pallas kernels  99.8 us (16%)
  starting transfers between devices  96.4 us (16%)
  local copies, waits for them, and re-layouts  60.1 us (10%)
  matrix products  58.1 us (10%)
  other arithmetic  51.2 us (8%)
    ppermute x65, waiting for transfers between devices, swap(): lax.ppermute(value, axis, [(i, i ^ by) for i in range(lax.axis_size(axis))])  210 us
    ppermute x65, starting transfers between devices, swap(): lax.ppermute(value, axis, [(i, i ^ by) for i in range(lax.axis_size(axis))])  87 us
    ppermute x4, waiting for transfers between devices, shift(): return lax.ppermute(value, axis, pairs)  26.9 us
    pallas_call x1, Pallas kernels, ffn(): pl.pallas_call(functools.partial(ffn_body, width // devices, units // dev...  25.9 us
    pallas_call x1, Pallas kernels, cross_backward(): pl.pallas_call(cross_backward_body, out_shape=[low(rows), low(rows), low(...  20.3 us
    dot_general x8, matrix products, meet(): jnp.einsum(spec, r, c, preferred_element_type=F32)  20.2 us
    pallas_call x1, Pallas kernels, attend_back(): pl.pallas_call(backward_body, grid_spec=pltpu.PrefetchScalarGridSpec(num_...  16.4 us
    pallas_call x1, Pallas kernels, cross_forward(): pl.pallas_call(cross_forward_body, out_shape=[low, low, low, wide, wide,...  15 us
  transfers between devices with their start and end apart: 69, of which 17 were waited for; matrix products, arithmetic and copies ran while one was open for 24% of the time, Pallas kernels for 13%

profile of v2, /device:TPU:0, one launch (start us, length us, event | category | flops | bytes accessed | tf_op | source)
XLA Modules:
  0.0 606.8 jit_solution(13602530761707319700)
XLA Ops:
  4.9 3.0 collective-permute-start.4
  14.1 5.6 collective-permute-done.1.x2
  24.8 8.7 %front.1 = (bf16[384,512]{1,0:T(8,128)(2,1)}, bf16[2,384,512]{2,1,0:T(8,128)(2,1)}, bf16[128,1536]{1,0:T(8,128)(2,1)}, bf16[512,1536]{1,0:T(8,128)(2,1)}, bf16[7...) custom-call(s32[2]{0:T(128)} %pad_add_fusion.1.place, ...), custom_call_target="tpu_custom_call" | custom-call | flops 1 | bytes 1 | tf_op jit(solution)/shard_map/front/pallas_call | solution.py:598
  33.5 4.4 collective-permute-start.6
  51.8 45.1 %collective-permute-done.10 = bf16[256,384]{1,0:T(8,128)(2,1)} collective-permute-done((bf16[256,384]{1,0:T(8,128)(2,1)}, bf16[256,384]{1,0:T(8,128)(2,1)}, u32[]{:S(2)}, u32[]{:S(2)}) %collective-permute-start.10) | collective-permute-done | bytes 196640 | tf_op jit(solution)/shard_map/ppermute | solution.py:24
  96.9 2.5 slice_bitcast_fusion.4
  99.5 13.6 %attend.1 = (bf16[384,512]{1,0:T(8,128)(2,1)}, f32[2,3,512]{2,1,0:T(4,128)}) custom-call(s32[4]{0:T(128)} %reshape.353.span, bf16[384,512]{1,0:T(8,128)(2,1)} %get-tuple-element.133.q, bf16[384,512]{1,0:T(8,128)(2,1)} %get-tuple-element.337.k0, bf16[384,512]{1,0:T(8,128)(2,1)} %get-tuple-element.296.k1, bf16[384,512]{1,0:T(8,128)(2,1)} %get-tuple-element.294.k2, ...), custom_call_target="tpu_custom_call" | custom-call | flops 1 | bytes 1 | tf_op jit(solution)/shard_map/attend/pallas_call | solution.py:256
  119.9 2.2 add_convert_fusion.7
  123.6 9.8 %collective-permute-done.12.far = bf16[128,1536]{1,0:T(8,128)(2,1)} collective-permute-done((bf16[128,1536]{1,0:T(8,128)(2,1)}, bf16[128,1536]{1,0:T(8,128)(2,1)}, u32[]{:S(2)}, u32[]{:S(2)}) %collective-permute-start.12) | collective-permute-done | bytes 393248 | tf_op jit(solution)/shard_map/ppermute | solution.py:24
  133.9 2.0 pad_maximum_fusion.8.kv
  135.9 2.3 convert_add_fusion.13.own
  139.3 15.0 %cross.1 = (bf16[128,1536]{1,0:T(8,128)(2,1)}, bf16[128,1536]{1,0:T(8,128)(2,1)}, bf16[128,1536]{1,0:T(8,128)(2,1)}, f32[128,1536]{1,0:T(8,128)}, f32[128,1536]{1,0:T(8,128)}, /*index=5*/bf16[128,1536]{1,0:T(8,128)(2,1)}) custom-call(bf16[128,1536]{1,0:T(8,128)(2,1)} %get-tuple-element.132.rows, f32[128,1536]{1,0:T(8,128)} %convert_add_fusion.13.own, ...), custom_call_target="tpu_custom_call" | custom-call | flops 1 | bytes 1 | tf_op jit(solution)/shard_map/cross/pallas_call | solution.py:402
  156.3 4.2 collective-permute-start.42
  160.4 4.0 collective-permute-done.19.n2
  168.5 25.9 %ffn.1 = (bf16[512,1536]{1,0:T(8,128)(2,1)}, bf16[768,512]{1,0:T(8,128)(2,1)}, bf16[768,512]{1,0:T(8,128)(2,1)}, bf16[512,1536]{1,0:T(8,128)(2,1)}, bf16[512,153...) custom-call(s32[1]{0:T(128)} %bitcast.1.place, ...), custom_call_target="tpu_custom_call" | custom-call | flops 1 | bytes 1 | tf_op jit(solution)/shard_map/ffn/pallas_call | solution.py:471
  200.5 1.9 constant_dynamic-update-slice_fusion.4
  202.4 4.2 collective-permute-start.66
  206.6 2.4 add_convert_fusion.4
  209.0 3.1 convolution_convert_fusion.3
  214.5 2.0 collective-permute-start.58
  217.5 1.8 fusion.21
  219.3 4.6 collective-permute-done.28.far
  224.6 20.3 %cross_back.1 = (bf16[128,1536]{1,0:T(8,128)(2,1)}, bf16[128,1536]{1,0:T(8,128)(2,1)}, bf16[256,1536]{1,0:T(8,128)(2,1)}, f32[4,1536]{1,0:T(4,128)}, bf16[128,1536]{1,0:T(8,128)(2,1)}) custom-call(f32[128,1536]{1,0:T(8,128)} %get-tuple-element.263.own, bf16[128,1536]{1,0:T(8,128)(2,1)} %copy-done.72, bf16[128,1536]{1,0:T(8,128)(2,1)} %copy-done.16, ...), custom_call_target="tpu_custom_call" | custom-call | flops 1 | bytes 1 | tf_op jit(solution)/shard_map/cross_back/pallas_call | solution.py:541
  245.0 14.0 %collective-permute-done.65 = bf16[768,512]{1,0:T(8,128)(2,1)} collective-permute-done((bf16[768,512]{1,0:T(8,128)(2,1)}, bf16[768,512]{1,0:T(8,128)(2,1)}, u32[]{:S(2)}, u32[]{:S(2)}) %collective-permute-start.65) | collective-permute-done | bytes 786464 | tf_op jit(solution)/shard_map/ppermute | solution.py:24
  266.8 3.0 fusion.104
  269.9 3.6 add_convert_fusion.6
  277.8 16.7 %collective-permute-done.26 = bf16[128,1536]{1,0:T(8,128)(2,1)S(1)} collective-permute-done((bf16[128,1536]{1,0:T(8,128)(2,1)S(1)}, bf16[128,1536]{1,0:T(8,128)(2,1)S(1)}, u32[]{:S(2)}, u32[]{:S(2)}) %collective-permute-start.26) | collective-permute-done | bytes 393248 | tf_op jit(solution)/shard_map/ppermute | solution.py:24
  294.8 3.4 collective-permute-start.67
  299.7 1.8 slice.318
  306.2 16.4 %attend_back.1 = (f32[384,512]{1,0:T(8,128)}, bf16[384,512]{1,0:T(8,128)(2,1)}, f32[384,512]{1,0:T(8,128)}, bf16[384,512]{1,0:T(8,128)(2,1)}, bf16[384,512]{1,0:...) custom-call(s32[4]{0:T(128)} %reshape.353.span, ...), custom_call_target="tpu_custom_call" | custom-call | flops 1 | bytes 1 | tf_op jit(solution)/shard_map/attend_back/pallas_call | solution.py:280
  334.5 1.8 convolution_convert_fusion
  338.1 3.0 fusion.102
  341.1 2.8 add_convert_fusion.2
  348.9 4.5 collective-permute-done.54
  353.4 3.0 collective-permute-start.62
  358.3 2.3 collective-permute-start.34
  360.6 1.9 fusion.2
  366.2 3.5 collective-permute-start.60
  372.6 18.9 %collective-permute-start.68 = (bf16[1,192,1536]{2,1,0:T(8,128)(2,1)S(1)}, bf16[1,192,1536]{2,1,0:T(8,128)(2,1)S(1)}, u32[]{:S(2)}, u32[]{:S(2)}) collective-permute-start(bf16[1,192,1536]{2,1,0:T(8,128)(2,1)S(1)} %constant_dynamic-slice_fusion.1), channel_id=1, source_target_pairs={{0,4},{1,5},{2,6},{3,7},{4,0},{5,1},{6,2},{7,3},{8,12},{9,13},{10,... | collective-permute-start | bytes 1769480 | tf_op jit(solution)/shard_map/ppermute | solution.py:24
  391.5 26.9 %collective-permute-done.34 = bf16[2,384,512]{2,1,0:T(8,128)(2,1)S(1)} collective-permute-done((bf16[2,384,512]{2,1,0:T(8,128)(2,1)}, bf16[2,384,512]{2,1,0:T(8,128)(2,1)S(1)}, u32[]{:S(2)}, u32[]{:S(2)}) %collective-permute-start.34) | collective-permute-done | bytes 786464 | tf_op jit(solution)/shard_map/ppermute | solution.py:30
  424.6 2.4 collective-permute-start.44
  432.5 3.1 fusion.103
  435.6 2.8 add_convert_fusion.1
  444.6 5.3 collective-permute-start.61
  450.0 2.1 convolution_convert_fusion.1
  454.4 3.3 concatenate.130
  457.7 2.5 convolution_convert_fusion.2
  460.7 1.8 dynamic-slice_bitcast_fusion
  463.7 2.0 collective-permute-start.55
  465.7 2.7 fusion.101
  468.5 3.3 multiply_reduce_fusion
  474.7 2.5 collective-permute-done.38
  478.8 2.1 collective-permute-start.45
  480.9 36.0 %collective-permute-done.39 = f32[4,6,48]{2,0,1:T(4,128)S(1)} collective-permute-done((f32[4,6,48]{2,0,1:T(4,128)S(1)}, f32[4,6,48]{2,0,1:T(4,128)S(1)}, u32[]{:S(2)}, u32[]{:S(2)}) %collective-permute-start.39) | collective-permute-done | bytes 4640 | tf_op jit(solution)/shard_map/ppermute | solution.py:24
  517.0 1.8 collective-permute-start.40
  518.8 1.9 collective-permute-done.40
  521.7 2.6 multiply_add_fusion
  525.8 2.2 add_bitcast_fusion.2
  529.5 2.3 fusion
  531.9 1.8 collective-permute-start.56
  535.3 1.9 collective-permute-start.64
  537.2 11.2 %collective-permute-done.46 = bf16[1,192,1152]{2,1,0:T(8,128)(2,1)S(1)} collective-permute-done((bf16[1,192,1152]{2,1,0:T(8,128)(2,1)S(1)}, bf16[1,192,1152]{2,1,0:T(8,128)(2,1)S(1)}, u32[]{:S(2)}, u32[]{:S(2)}) %collective-permute-start.46) | collective-permute-done | bytes 442400 | tf_op jit(solution)/shard_map/ppermute | solution.py:24
  548.5 30.3 %collective-permute-done.56 = bf16[2,192,1536]{2,1,0:T(8,128)(2,1)S(1)} collective-permute-done((bf16[2,192,1536]{2,1,0:T(8,128)(2,1)S(1)}, bf16[2,192,1536]{2,1,0:T(8,128)(2,1)S(1)}, u32[]{:S(2)}, u32[]{:S(2)}) %collective-permute-start.56) | collective-permute-done | bytes 1179680 | tf_op jit(solution)/shard_map/ppermute | solution.py:24
  581.9 21.9 %collective-permute-done.57 = bf16[1,192,1536]{2,1,0:T(8,128)(2,1)S(1)} collective-permute-done((bf16[1,192,1536]{2,1,0:T(8,128)(2,1)S(1)}, bf16[1,192,1536]{2,1,0:T(8,128)(2,1)S(1)}, u32[]{:S(2)}, u32[]{:S(2)}) %collective-permute-start.57) | collective-permute-done | bytes 589856 | tf_op jit(solution)/shard_map/ppermute | solution.py:24
  (491 shorter events, 136.6 us)
Async XLA Ops:
  4.9 16.0 %collective-permute-start.4 = (f32[6,384]{1,0:T(8,128)S(1)}, f32[6,384]{1,0:T(8,128)S(1)}, u32[]{:S(2)}, u32[]{:S(2)}) collective-permute-start(f32[6,384]{1,0:T(8,128)S(1)} %stack.91.g0), channel_id=1, source_target_pairs={{0,16},{8,24},{16,0},{24,8},{1,17},{9,25},{17,1},{25,9},{2,18},{10... | collective-permute-start | bytes 27656 | tf_op jit(solution)/shard_map/ppermute | solution.py:24
  7.9 16.0 %collective-permute-start.3 = (f32[6,384]{1,0:T(8,128)S(1)}, f32[6,384]{1,0:T(8,128)S(1)}, u32[]{:S(2)}, u32[]{:S(2)}) collective-permute-start(f32[6,384]{1,0:T(8,128)S(1)} %stack.91.g0), channel_id=1, source_target_pairs={{0,8},{8,0},{16,24},{24,16},{1,9},{9,1},{17,25},{25,17},{2,10},{10... | collective-permute-start | bytes 27656 | tf_op jit(solution)/shard_map/ppermute | solution.py:24
  7.9 11.7 %collective-permute-start.1 = (bf16[512,384]{1,0:T(8,128)(2,1)}, bf16[512,384]{1,0:T(8,128)(2,1)S(1)}, u32[]{:S(2)}, u32[]{:S(2)}) collective-permute-start(bf16[512,384]{1,0:T(8,128)(2,1)} %x0.1), channel_id=1, source_target_pairs={{0,16},{8,24},{16,0},{24,8},{1,17},{9,25},{17,1},{25,9},{2,18},{10... | collective-permute-start | bytes 1179656 | tf_op jit(solution)/shard_map/ppermute | solution.py:24
  8.1 15.8 %collective-permute-start = (bf16[512,384]{1,0:T(8,128)(2,1)}, bf16[512,384]{1,0:T(8,128)(2,1)S(1)}, u32[]{:S(2)}, u32[]{:S(2)}) collective-permute-start(bf16[512,384]{1,0:T(8,128)(2,1)} %x0.1), channel_id=1, source_target_pairs={{0,8},{8,0},{16,24},{24,16},{1,9},{9,1},{17,25},{25,17},{2,10},{10... | collective-permute-start | bytes 1179656 | tf_op jit(solution)/shard_map/ppermute | solution.py:24
  19.7 4.3 collective-permute-start.2
  33.5 63.4 %collective-permute-start.6 = (bf16[2,384,512]{2,1,0:T(8,128)(2,1)}, bf16[2,384,512]{2,1,0:T(8,128)(2,1)}, u32[]{:S(2)}, u32[]{:S(2)}) collective-permute-start(bf16[2,384,512]{2,1,0:T(8,128)(2,1)} %get-tuple-element.134), channel_id=1, source_target_pairs={{0,1},{1,2},{2,3},{3,4},{4,5},{5,6},{6,7},{8,9},{9,10},{10,11},{11... | collective-permute-start | bytes 2359304 | tf_op jit(solution)/shard_map/ppermute | solution.py:30
  38.0 58.9 %collective-permute-start.7 = (bf16[2,384,512]{2,1,0:T(8,128)(2,1)}, bf16[2,384,512]{2,1,0:T(8,128)(2,1)}, u32[]{:S(2)}, u32[]{:S(2)}) collective-permute-start(bf16[2,384,512]{2,1,0:T(8,128)(2,1)} %get-tuple-element.134), channel_id=1, source_target_pairs={{1,0},{2,1},{3,2},{4,3},{5,4},{6,5},{7,6},{9,8},{10,9},{11,10},{12... | collective-permute-start | bytes 2359304 | tf_op jit(solution)/shard_map/ppermute | solution.py:30
  39.4 57.5 %collective-permute-start.8 = (bf16[1536,384]{1,0:T(8,128)(2,1)}, bf16[1536,384]{1,0:T(8,128)(2,1)}, u32[]{:S(2)}, u32[]{:S(2)}) collective-permute-start(bf16[1536,384]{1,0:T(8,128)(2,1)} %q0.3), channel_id=1, source_target_pairs={{0,16},{8,24},{16,0},{24,8},{1,17},{9,25},{17,1},{25,9},{2,18},{10... | collective-permute-start | bytes 3538952 | tf_op jit(solution)/shard_map/ppermute | solution.py:24
  40.0 56.9 %collective-permute-start.9 = (bf16[384,1536]{1,0:T(8,128)(2,1)}, bf16[384,1536]{1,0:T(8,128)(2,1)}, u32[]{:S(2)}, u32[]{:S(2)}) collective-permute-start(bf16[384,1536]{1,0:T(8,128)(2,1)} %o0.3), channel_id=1, source_target_pairs={{0,16},{8,24},{16,0},{24,8},{1,17},{9,25},{17,1},{25,9},{2,18},{10... | collective-permute-start | bytes 3538952 | tf_op jit(solution)/shard_map/ppermute | solution.py:24
  44.1 52.8 %collective-permute-start.10 = (bf16[256,384]{1,0:T(8,128)(2,1)}, bf16[256,384]{1,0:T(8,128)(2,1)}, u32[]{:S(2)}, u32[]{:S(2)}) collective-permute-start(bf16[256,384]{1,0:T(8,128)(2,1)} %pad_maximum_fusion.20), channel_id=1, source_target_pairs={{0,16},{8,24},{16,0},{24,8},{1,17},{9,25},{17,1},{25,9},{2,18},{10... | collective-permute-start | bytes 589832 | tf_op jit(solution)/shard_map/ppermute | solution.py:24
  118.8 19.4 %collective-permute-start.13 = (bf16[1536,384]{1,0:T(8,128)(2,1)}, bf16[1536,384]{1,0:T(8,128)(2,1)S(1)}, u32[]{:S(2)}, u32[]{:S(2)}) collective-permute-start(bf16[1536,384]{1,0:T(8,128)(2,1)} %q0.3), channel_id=1, source_target_pairs={{0,8},{8,0},{16,24},{24,16},{1,9},{9,1},{17,25},{25,17},{2,10},{10... | collective-permute-start | bytes 3538952 | tf_op jit(solution)/shard_map/ppermute | solution.py:24
  118.8 19.4 %collective-permute-start.16 = (bf16[384,1536]{1,0:T(8,128)(2,1)}, bf16[384,1536]{1,0:T(8,128)(2,1)}, u32[]{:S(2)}, u32[]{:S(2)}) collective-permute-start(bf16[384,1536]{1,0:T(8,128)(2,1)} %o0.3), channel_id=1, source_target_pairs={{0,8},{8,0},{16,24},{24,16},{1,9},{9,1},{17,25},{25,17},{2,10},{10... | collective-permute-start | bytes 3538952 | tf_op jit(solution)/shard_map/ppermute | solution.py:24
  119.3 18.9 %collective-permute-start.14 = (bf16[1536,384]{1,0:T(8,128)(2,1)}, bf16[1536,384]{1,0:T(8,128)(2,1)}, u32[]{:S(2)}, u32[]{:S(2)}) collective-permute-start(bf16[1536,384]{1,0:T(8,128)(2,1)} %collective-permute-done.8.q2), channel_id=1, source_target_pairs={{0,8},{8,0},{16,24},{24,16},{1,9},{9,1},{17,25},{25,17},{2,10},{10... | collective-permute-start | bytes 3538952 | tf_op jit(solution)/shard_map/ppermute | solution.py:24
  119.4 18.9 %collective-permute-start.17 = (bf16[384,1536]{1,0:T(8,128)(2,1)}, bf16[384,1536]{1,0:T(8,128)(2,1)}, u32[]{:S(2)}, u32[]{:S(2)}) collective-permute-start(bf16[384,1536]{1,0:T(8,128)(2,1)} %collective-permute-done.9.o2), channel_id=1, source_target_pairs={{0,8},{8,0},{16,24},{24,16},{1,9},{9,1},{17,25},{25,17},{2,10},{10... | collective-permute-start | bytes 3538952 | tf_op jit(solution)/shard_map/ppermute | solution.py:24
  122.1 11.3 %collective-permute-start.12 = (bf16[128,1536]{1,0:T(8,128)(2,1)}, bf16[128,1536]{1,0:T(8,128)(2,1)}, u32[]{:S(2)}, u32[]{:S(2)}) collective-permute-start(bf16[128,1536]{1,0:T(8,128)(2,1)} %add_convert_fusion.7), channel_id=1, source_target_pairs={{0,16},{8,24},{16,0},{24,8},{1,17},{9,25},{17,1},{25,9},{2,18},{10... | collective-permute-start | bytes 1179656 | tf_op jit(solution)/shard_map/ppermute | solution.py:24
  133.4 22.4 %collective-permute-start.21 = (bf16[512,384]{1,0:T(8,128)(2,1)}, bf16[512,384]{1,0:T(8,128)(2,1)}, u32[]{:S(2)}, u32[]{:S(2)}) collective-permute-start(bf16[512,384]{1,0:T(8,128)(2,1)} %param.43), channel_id=1, source_target_pairs={{0,16},{8,24},{16,0},{24,8},{1,17},{9,25},{17,1},{25,9},{2,18},{10... | collective-permute-start | bytes 1179656 | tf_op jit(solution)/shard_map/ppermute | solution.py:24
  154.2 10.2 %collective-permute-start.19 = (bf16[128,1536]{1,0:T(8,128)(2,1)}, bf16[128,1536]{1,0:T(8,128)(2,1)}, u32[]{:S(2)}, u32[]{:S(2)}) collective-permute-start(bf16[128,1536]{1,0:T(8,128)(2,1)} %get-tuple-element.149.n0), channel_id=1, source_target_pairs={{0,16},{8,24},{16,0},{24,8},{1,17},{9,25},{17,1},{25,9},{2,18},{10... | collective-permute-start | bytes 1179656 | tf_op jit(solution)/shard_map/ppermute | solution.py:24
  155.8 8.7 %collective-permute-start.22 = (bf16[512,384]{1,0:T(8,128)(2,1)}, bf16[512,384]{1,0:T(8,128)(2,1)S(1)}, u32[]{:S(2)}, u32[]{:S(2)}) collective-permute-start(bf16[512,384]{1,0:T(8,128)(2,1)} %param.43), channel_id=1, source_target_pairs={{0,8},{8,0},{16,24},{24,16},{1,9},{9,1},{17,25},{25,17},{2,10},{10... | collective-permute-start | bytes 1179656 | tf_op jit(solution)/shard_map/ppermute | solution.py:24
  155.8 8.7 %collective-permute-start.23 = (bf16[512,384]{1,0:T(8,128)(2,1)}, bf16[512,384]{1,0:T(8,128)(2,1)S(1)}, u32[]{:S(2)}, u32[]{:S(2)}) collective-permute-start(bf16[512,384]{1,0:T(8,128)(2,1)} %collective-permute-done.21), channel_id=1, source_target_pairs={{0,8},{8,0},{16,24},{24,16},{1,9},{9,1},{17,25},{25,17},{2,10},{10... | collective-permute-start | bytes 1179656 | tf_op jit(solution)/shard_map/ppermute | solution.py:24
  156.3 43.4 %collective-permute-start.42 = (bf16[768,512]{1,0:T(8,128)(2,1)}, bf16[768,512]{1,0:T(8,128)(2,1)}, u32[]{:S(2)}, u32[]{:S(2)}) collective-permute-start(bf16[768,512]{1,0:T(8,128)(2,1)} %get-tuple-element.182), channel_id=1, source_target_pairs={{0,1},{1,0},{2,3},{3,2},{4,5},{5,4},{6,7},{7,6},{8,9},{9,8},{10,11... | collective-permute-start | bytes 2359304 | tf_op jit(solution)/shard_map/ppermute | solution.py:24
  160.4 7.3 %collective-permute-start.18 = (bf16[128,1536]{1,0:T(8,128)(2,1)}, bf16[128,1536]{1,0:T(8,128)(2,1)S(1)}, u32[]{:S(2)}, u32[]{:S(2)}) collective-permute-start(bf16[128,1536]{1,0:T(8,128)(2,1)} %get-tuple-element.149.n0), channel_id=1, source_target_pairs={{0,8},{8,0},{16,24},{24,16},{1,9},{9,1},{17,25},{25,17},{2,10},{10... | collective-permute-start | bytes 1179656 | tf_op jit(solution)/shard_map/ppermute | solution.py:24
  164.4 4.0 collective-permute-start.20
  194.3 12.3 %collective-permute-start.24 = (bf16[256,1536]{1,0:T(8,128)(2,1)}, bf16[256,1536]{1,0:T(8,128)(2,1)}, u32[]{:S(2)}, u32[]{:S(2)}) collective-permute-start(bf16[256,1536]{1,0:T(8,128)(2,1)} %get-tuple-element.155), channel_id=1, source_target_pairs={{0,8},{8,0},{16,24},{24,16},{1,9},{9,1},{17,25},{25,17},{2,10},{10... | collective-permute-start | bytes 2359304 | tf_op jit(solution)/shard_map/ppermute | solution.py:24
  202.4 63.0 %collective-permute-start.66 = (bf16[512,1536]{1,0:T(8,128)(2,1)}, bf16[512,1536]{1,0:T(8,128)(2,1)}, u32[]{:S(2)}, u32[]{:S(2)}) collective-permute-start(bf16[512,1536]{1,0:T(8,128)(2,1)} %pad_maximum_fusion.2.grad), channel_id=1, source_target_pairs={{0,1},{1,0},{2,3},{3,2},{4,5},{5,4},{6,7},{7,6},{8,9},{9,8},{10,11... | collective-permute-start | bytes 4718600 | tf_op jit(solution)/shard_map/ppermute | solution.py:24
  206.6 52.4 %collective-permute-start.65 = (bf16[768,512]{1,0:T(8,128)(2,1)}, bf16[768,512]{1,0:T(8,128)(2,1)}, u32[]{:S(2)}, u32[]{:S(2)}) collective-permute-start(bf16[768,512]{1,0:T(8,128)(2,1)} %get-tuple-element.237), channel_id=1, source_target_pairs={{0,1},{1,0},{2,3},{3,2},{4,5},{5,4},{6,7},{7,6},{8,9},{9,8},{10,11... | collective-permute-start | bytes 2359304 | tf_op jit(solution)/shard_map/ppermute | solution.py:24
  212.9 10.9 %collective-permute-start.28 = (bf16[128,1536]{1,0:T(8,128)(2,1)S(1)}, bf16[128,1536]{1,0:T(8,128)(2,1)S(1)}, u32[]{:S(2)}, u32[]{:S(2)}) collective-permute-start(bf16[128,1536]{1,0:T(8,128)(2,1)S(1)} %get-tuple-element.262), channel_id=1, source_target_pairs={{0,16},{8,24},{16,0},{24,8},{1,17},{9,25},{17,1},{25,9},{2,18},{10... | collective-permute-start | bytes 1179656 | tf_op jit(solution)/shard_map/ppermute | solution.py:24
  214.5 115.6 %collective-permute-start.58 = (bf16[768,512]{1,0:T(8,128)(2,1)}, bf16[768,512]{1,0:T(8,128)(2,1)}, u32[]{:S(2)}, u32[]{:S(2)}) collective-permute-start(bf16[768,512]{1,0:T(8,128)(2,1)} %get-tuple-element.220), channel_id=1, source_target_pairs={{0,1},{1,0},{2,3},{3,2},{4,5},{5,4},{6,7},{7,6},{8,9},{9,8},{10,11... | collective-permute-start | bytes 2359304 | tf_op jit(solution)/shard_map/ppermute | solution.py:24
  216.5 121.0 %collective-permute-start.59 = (bf16[512,1536]{1,0:T(8,128)(2,1)}, bf16[512,1536]{1,0:T(8,128)(2,1)}, u32[]{:S(2)}, u32[]{:S(2)}) collective-permute-start(bf16[512,1536]{1,0:T(8,128)(2,1)} %get-tuple-element.222), channel_id=1, source_target_pairs={{0,1},{1,0},{2,3},{3,2},{4,5},{5,4},{6,7},{7,6},{8,9},{9,8},{10,11... | collective-permute-start | bytes 4718600 | tf_op jit(solution)/shard_map/ppermute | solution.py:24
  223.9 46.0 %collective-permute-start.25 = (bf16[256,1536]{1,0:T(8,128)(2,1)}, bf16[256,1536]{1,0:T(8,128)(2,1)S(1)}, u32[]{:S(2)}, u32[]{:S(2)}) collective-permute-start(bf16[256,1536]{1,0:T(8,128)(2,1)} %pad_maximum_fusion.9), channel_id=1, source_target_pairs={{0,8},{8,0},{16,24},{24,16},{1,9},{9,1},{17,25},{25,17},{2,10},{10... | collective-permute-start | bytes 2359304 | tf_op jit(solution)/shard_map/ppermute | solution.py:24
  258.9 18.7 %collective-permute-start.30 = (bf16[128,1536]{1,0:T(8,128)(2,1)}, bf16[128,1536]{1,0:T(8,128)(2,1)S(1)}, u32[]{:S(2)}, u32[]{:S(2)}) collective-permute-start(bf16[128,1536]{1,0:T(8,128)(2,1)} %get-tuple-element.159), channel_id=1, source_target_pairs={{0,16},{8,24},{16,0},{24,8},{1,17},{9,25},{17,1},{25,9},{2,18},{10... | collective-permute-start | bytes 1179656 | tf_op jit(solution)/shard_map/ppermute | solution.py:24
  266.3 28.4 %collective-permute-start.47 = (bf16[128,3072]{1,0:T(8,128)(2,1)}, bf16[128,3072]{1,0:T(8,128)(2,1)}, u32[]{:S(2)}, u32[]{:S(2)}) collective-permute-start(bf16[128,3072]{1,0:T(8,128)(2,1)} %constant_dynamic-update-slice_fusion.4), channel_id=1, source_target_pairs={{0,16},{8,24},{16,0},{24,8},{1,17},{9,25},{17,1},{25,9},{2,18},{10... | collective-permute-start | bytes 2359304 | tf_op jit(solution)/shard_map/ppermute | solution.py:24
  273.5 21.0 %collective-permute-start.26 = (bf16[128,1536]{1,0:T(8,128)(2,1)S(1)}, bf16[128,1536]{1,0:T(8,128)(2,1)S(1)}, u32[]{:S(2)}, u32[]{:S(2)}) collective-permute-start(bf16[128,1536]{1,0:T(8,128)(2,1)S(1)} %add_convert_fusion.6), channel_id=1, source_target_pairs={{0,16},{8,24},{16,0},{24,8},{1,17},{9,25},{17,1},{25,9},{2,18},{10... | collective-permute-start | bytes 1179656 | tf_op jit(solution)/shard_map/ppermute | solution.py:24
  277.8 25.2 %collective-permute-start.29 = (bf16[128,1536]{1,0:T(8,128)(2,1)S(1)}, bf16[128,1536]{1,0:T(8,128)(2,1)S(1)}, u32[]{:S(2)}, u32[]{:S(2)}) collective-permute-start(bf16[128,1536]{1,0:T(8,128)(2,1)S(1)} %copy-done.66), channel_id=1, source_target_pairs={{0,8},{8,0},{16,24},{24,16},{1,9},{9,1},{17,25},{25,17},{2,10},{10... | collective-permute-start | bytes 1179656 | tf_op jit(solution)/shard_map/ppermute | solution.py:24
  294.5 8.7 %collective-permute-start.31 = (bf16[128,1536]{1,0:T(8,128)(2,1)S(1)}, bf16[128,1536]{1,0:T(8,128)(2,1)S(1)}, u32[]{:S(2)}, u32[]{:S(2)}) collective-permute-start(bf16[128,1536]{1,0:T(8,128)(2,1)S(1)} %collective-permute-done.30), channel_id=1, source_target_pairs={{0,8},{8,0},{16,24},{24,16},{1,9},{9,1},{17,25},{25,17},{2,10},{10... | collective-permute-start | bytes 1179656 | tf_op jit(solution)/shard_map/ppermute | solution.py:24
  294.8 63.6 %collective-permute-start.67 = (bf16[2,192,1536]{2,1,0:T(8,128)(2,1)}, bf16[2,192,1536]{2,1,0:T(8,128)(2,1)}, u32[]{:S(2)}, u32[]{:S(2)}) collective-permute-start(bf16[2,192,1536]{2,1,0:T(8,128)(2,1)} %dynamic-slice_bitcast_fusion.1), channel_id=1, source_target_pairs={{0,2},{1,3},{2,0},{3,1},{4,6},{5,7},{6,4},{7,5},{8,10},{9,11},{10,... | collective-permute-start | bytes 3538952 | tf_op jit(solution)/shard_map/ppermute | solution.py:24
  303.0 63.2 %collective-permute-start.49 = (bf16[128,3072]{1,0:T(8,128)(2,1)}, bf16[128,3072]{1,0:T(8,128)(2,1)}, u32[]{:S(2)}, u32[]{:S(2)}) collective-permute-start(bf16[128,3072]{1,0:T(8,128)(2,1)} %collective-permute-done.47), channel_id=1, source_target_pairs={{0,8},{8,0},{16,24},{24,16},{1,9},{9,1},{17,25},{25,17},{2,10},{10... | collective-permute-start | bytes 2359304 | tf_op jit(solution)/shard_map/ppermute | solution.py:24
  303.2 59.5 %collective-permute-start.48 = (bf16[128,3072]{1,0:T(8,128)(2,1)}, bf16[128,3072]{1,0:T(8,128)(2,1)}, u32[]{:S(2)}, u32[]{:S(2)}) collective-permute-start(bf16[128,3072]{1,0:T(8,128)(2,1)} %constant_dynamic-update-slice_fusion.4), channel_id=1, source_target_pairs={{0,8},{8,0},{16,24},{24,16},{1,9},{9,1},{17,25},{25,17},{2,10},{10... | collective-permute-start | bytes 2359304 | tf_op jit(solution)/shard_map/ppermute | solution.py:24
  330.2 7.2 %collective-permute-start.27 = (bf16[128,768]{1,0:T(8,128)(2,1)}, bf16[128,768]{1,0:T(8,128)(2,1)S(1)}, u32[]{:S(2)}, u32[]{:S(2)}) collective-permute-start(bf16[128,768]{1,0:T(8,128)(2,1)} %pad_maximum_fusion.21), channel_id=1, source_target_pairs={{0,16},{8,24},{16,0},{24,8},{1,17},{9,25},{17,1},{25,9},{2,18},{10... | collective-permute-start | bytes 589832 | tf_op jit(solution)/shard_map/ppermute | solution.py:24
  337.4 9.1 %collective-permute-start.53 = (bf16[512,384]{1,0:T(8,128)(2,1)S(1)}, bf16[512,384]{1,0:T(8,128)(2,1)S(1)}, u32[]{:S(2)}, u32[]{:S(2)}) collective-permute-start(bf16[512,384]{1,0:T(8,128)(2,1)S(1)} %pad_maximum_fusion.19), channel_id=1, source_target_pairs={{0,8},{8,0},{16,24},{24,16},{1,9},{9,1},{17,25},{25,17},{2,10},{10... | collective-permute-start | bytes 1179656 | tf_op jit(solution)/shard_map/ppermute | solution.py:24
  337.5 7.6 %collective-permute-start.32 = (bf16[256,384]{1,0:T(8,128)(2,1)S(1)}, bf16[256,384]{1,0:T(8,128)(2,1)S(1)}, u32[]{:S(2)}, u32[]{:S(2)}) collective-permute-start(bf16[256,384]{1,0:T(8,128)(2,1)S(1)} %pad_maximum_fusion.22), channel_id=1, source_target_pairs={{0,8},{8,0},{16,24},{24,16},{1,9},{9,1},{17,25},{25,17},{2,10},{10... | collective-permute-start | bytes 589832 | tf_op jit(solution)/shard_map/ppermute | solution.py:24
  345.1 27.5 %collective-permute-start.33 = (bf16[2,384,512]{2,1,0:T(8,128)(2,1)}, bf16[2,384,512]{2,1,0:T(8,128)(2,1)}, u32[]{:S(2)}, u32[]{:S(2)}) collective-permute-start(bf16[2,384,512]{2,1,0:T(8,128)(2,1)} %pad_maximum_fusion.10), channel_id=1, source_target_pairs={{1,0},{2,1},{3,2},{4,3},{5,4},{6,5},{7,6},{9,8},{10,9},{11,10},{12... | collective-permute-start | bytes 2359304 | tf_op jit(solution)/shard_map/ppermute | solution.py:30
  346.5 6.9 %collective-permute-start.54 = (bf16[256,384]{1,0:T(8,128)(2,1)S(1)}, bf16[256,384]{1,0:T(8,128)(2,1)S(1)}, u32[]{:S(2)}, u32[]{:S(2)}) collective-permute-start(bf16[256,384]{1,0:T(8,128)(2,1)S(1)} %fusion.12), channel_id=1, source_target_pairs={{0,16},{8,24},{16,0},{24,8},{1,17},{9,25},{17,1},{25,9},{2,18},{10... | collective-permute-start | bytes 589832 | tf_op jit(solution)/shard_map/ppermute | solution.py:24
  353.4 79.0 %collective-permute-start.62 = (bf16[512,1536]{1,0:T(8,128)(2,1)}, bf16[512,1536]{1,0:T(8,128)(2,1)}, u32[]{:S(2)}, u32[]{:S(2)}) collective-permute-start(bf16[512,1536]{1,0:T(8,128)(2,1)} %get-tuple-element.229), channel_id=1, source_target_pairs={{0,1},{1,0},{2,3},{3,2},{4,5},{5,4},{6,7},{7,6},{8,9},{9,8},{10,11... | collective-permute-start | bytes 4718600 | tf_op jit(solution)/shard_map/ppermute | solution.py:24
  358.3 60.1 %collective-permute-start.34 = (bf16[2,384,512]{2,1,0:T(8,128)(2,1)}, bf16[2,384,512]{2,1,0:T(8,128)(2,1)S(1)}, u32[]{:S(2)}, u32[]{:S(2)}) collective-permute-start(bf16[2,384,512]{2,1,0:T(8,128)(2,1)} %pad_maximum_fusion.11), channel_id=1, source_target_pairs={{0,1},{1,2},{2,3},{3,4},{4,5},{5,6},{6,7},{8,9},{9,10},{10,11},{11... | collective-permute-start | bytes 2359304 | tf_op jit(solution)/shard_map/ppermute | solution.py:30
  362.7 61.9 %collective-permute-start.50 = (bf16[128,3072]{1,0:T(8,128)(2,1)S(1)}, bf16[128,3072]{1,0:T(8,128)(2,1)S(1)}, u32[]{:S(2)}, u32[]{:S(2)}) collective-permute-start(bf16[128,3072]{1,0:T(8,128)(2,1)S(1)} %copy-done.78), channel_id=1, source_target_pairs={{0,16},{8,24},{16,0},{24,8},{1,17},{9,25},{17,1},{25,9},{2,18},{10... | collective-permute-start | bytes 2359304 | tf_op jit(solution)/shard_map/ppermute | solution.py:24
  366.2 76.1 %collective-permute-start.60 = (bf16[2,192,1536]{2,1,0:T(8,128)(2,1)S(1)}, bf16[2,192,1536]{2,1,0:T(8,128)(2,1)S(1)}, u32[]{:S(2)}, u32[]{:S(2)}) collective-permute-start(bf16[2,192,1536]{2,1,0:T(8,128)(2,1)S(1)} %copy-done.48), channel_id=1, source_target_pairs={{0,2},{1,3},{2,0},{3,1},{4,6},{5,7},{6,4},{7,5},{8,10},{9,11},{10,... | collective-permute-start | bytes 3538952 | tf_op jit(solution)/shard_map/ppermute | solution.py:24
  372.6 58.2 %collective-permute-start.68 = (bf16[1,192,1536]{2,1,0:T(8,128)(2,1)S(1)}, bf16[1,192,1536]{2,1,0:T(8,128)(2,1)S(1)}, u32[]{:S(2)}, u32[]{:S(2)}) collective-permute-start(bf16[1,192,1536]{2,1,0:T(8,128)(2,1)S(1)} %constant_dynamic-slice_fusion.1), channel_id=1, source_target_pairs={{0,4},{1,5},{2,6},{3,7},{4,0},{5,1},{6,2},{7,3},{8,12},{9,13},{10,... | collective-permute-start | bytes 1769480 | tf_op jit(solution)/shard_map/ppermute | solution.py:24
  424.5 25.4 %collective-permute-start.52 = (bf16[128,3072]{1,0:T(8,128)(2,1)S(1)}, bf16[128,3072]{1,0:T(8,128)(2,1)S(1)}, u32[]{:S(2)}, u32[]{:S(2)}) collective-permute-start(bf16[128,3072]{1,0:T(8,128)(2,1)S(1)} %collective-permute-done.50), channel_id=1, source_target_pairs={{0,8},{8,0},{16,24},{24,16},{1,9},{9,1},{17,25},{25,17},{2,10},{10... | collective-permute-start | bytes 2359304 | tf_op jit(solution)/shard_map/ppermute | solution.py:24
  424.6 5.9 collective-permute-start.44
  430.6 9.0 %collective-permute-start.35 = (bf16[1024,384]{1,0:T(8,128)(2,1)S(1)}, bf16[1024,384]{1,0:T(8,128)(2,1)S(1)}, u32[]{:S(2)}, u32[]{:S(2)}) collective-permute-start(bf16[1024,384]{1,0:T(8,128)(2,1)S(1)} %pad_maximum_fusion.12), channel_id=1, source_target_pairs={{0,8},{8,0},{16,24},{24,16},{1,9},{9,1},{17,25},{25,17},{2,10},{10... | collective-permute-start | bytes 2359304 | tf_op jit(solution)/shard_map/ppermute | solution.py:24
  430.8 13.8 %collective-permute-start.51 = (bf16[128,3072]{1,0:T(8,128)(2,1)S(1)}, bf16[128,3072]{1,0:T(8,128)(2,1)S(1)}, u32[]{:S(2)}, u32[]{:S(2)}) collective-permute-start(bf16[128,3072]{1,0:T(8,128)(2,1)S(1)} %copy-done.78), channel_id=1, source_target_pairs={{0,8},{8,0},{16,24},{24,16},{1,9},{9,1},{17,25},{25,17},{2,10},{10... | collective-permute-start | bytes 2359304 | tf_op jit(solution)/shard_map/ppermute | solution.py:24
  432.4 33.2 %collective-permute-start.43 = (bf16[1152,512]{1,0:T(8,128)(2,1)}, bf16[1152,512]{1,0:T(8,128)(2,1)}, u32[]{:S(2)}, u32[]{:S(2)}) collective-permute-start(bf16[1152,512]{1,0:T(8,128)(2,1)} %pad_maximum_fusion.6), channel_id=1, source_target_pairs={{0,1},{1,0},{2,3},{3,2},{4,5},{5,4},{6,7},{7,6},{8,9},{9,8},{10,11... | collective-permute-start | bytes 3538952 | tf_op jit(solution)/shard_map/ppermute | solution.py:24
  440.8 27.7 %collective-permute-start.36 = (bf16[512,384]{1,0:T(8,128)(2,1)}, bf16[512,384]{1,0:T(8,128)(2,1)}, u32[]{:S(2)}, u32[]{:S(2)}) collective-permute-start(bf16[512,384]{1,0:T(8,128)(2,1)} %add_convert_fusion.3), channel_id=1, source_target_pairs={{0,16},{8,24},{16,0},{24,8},{1,17},{9,25},{17,1},{25,9},{2,18},{10... | collective-permute-start | bytes 1179656 | tf_op jit(solution)/shard_map/ppermute | solution.py:24
  442.3 85.8 %collective-permute-start.63 = (bf16[2,192,1536]{2,1,0:T(8,128)(2,1)}, bf16[2,192,1536]{2,1,0:T(8,128)(2,1)}, u32[]{:S(2)}, u32[]{:S(2)}) collective-permute-start(bf16[2,192,1536]{2,1,0:T(8,128)(2,1)} %dynamic-slice_bitcast_fusion.2), channel_id=1, source_target_pairs={{0,2},{1,3},{2,0},{3,1},{4,6},{5,7},{6,4},{7,5},{8,10},{9,11},{10,... | collective-permute-start | bytes 3538952 | tf_op jit(solution)/shard_map/ppermute | solution.py:24
  444.6 81.2 %collective-permute-start.61 = (bf16[1,192,1536]{2,1,0:T(8,128)(2,1)}, bf16[1,192,1536]{2,1,0:T(8,128)(2,1)}, u32[]{:S(2)}, u32[]{:S(2)}) collective-permute-start(bf16[1,192,1536]{2,1,0:T(8,128)(2,1)} %constant_dynamic-slice_fusion.3), channel_id=1, source_target_pairs={{0,4},{1,5},{2,6},{3,7},{4,0},{5,1},{6,2},{7,3},{8,12},{9,13},{10,... | collective-permute-start | bytes 1769480 | tf_op jit(solution)/shard_map/ppermute | solution.py:24
  463.7 65.8 %collective-permute-start.55 = (bf16[4,192,1536]{2,1,0:T(8,128)(2,1)}, bf16[4,192,1536]{2,1,0:T(8,128)(2,1)}, u32[]{:S(2)}, u32[]{:S(2)}) collective-permute-start(bf16[4,192,1536]{2,1,0:T(8,128)(2,1)} %dynamic-slice_bitcast_fusion), channel_id=1, source_target_pairs={{0,1},{1,0},{2,3},{3,2},{4,5},{5,4},{6,7},{7,6},{8,9},{9,8},{10,11... | collective-permute-start | bytes 7077896 | tf_op jit(solution)/shard_map/ppermute | solution.py:24
  473.2 4.0 collective-permute-start.38
  478.5 38.5 %collective-permute-start.39 = (f32[4,6,48]{2,0,1:T(4,128)S(1)}, f32[4,6,48]{2,0,1:T(4,128)S(1)}, u32[]{:S(2)}, u32[]{:S(2)}) collective-permute-start(f32[4,6,48]{2,0,1:T(4,128)S(1)} %bitcast.236), channel_id=1, source_target_pairs={{0,1},{1,0},{2,3},{3,2},{4,5},{5,4},{6,7},{7,6},{8,9},{9,8},{10,11... | collective-permute-start | bytes 13832 | tf_op jit(solution)/shard_map/ppermute | solution.py:24
  478.8 49.2 %collective-permute-start.45 = (bf16[2,192,1152]{2,1,0:T(8,128)(2,1)S(1)}, bf16[2,192,1152]{2,1,0:T(8,128)(2,1)S(1)}, u32[]{:S(2)}, u32[]{:S(2)}) collective-permute-start(bf16[2,192,1152]{2,1,0:T(8,128)(2,1)S(1)} %dynamic-slice_bitcast_fusion.5), channel_id=1, source_target_pairs={{0,2},{1,3},{2,0},{3,1},{4,6},{5,7},{6,4},{7,5},{8,10},{9,11},{10,... | collective-permute-start | bytes 2654216 | tf_op jit(solution)/shard_map/ppermute | solution.py:24
  520.7 4.6 collective-permute-start.41
  528.3 20.1 %collective-permute-start.46 = (bf16[1,192,1152]{2,1,0:T(8,128)(2,1)S(1)}, bf16[1,192,1152]{2,1,0:T(8,128)(2,1)S(1)}, u32[]{:S(2)}, u32[]{:S(2)}) collective-permute-start(bf16[1,192,1152]{2,1,0:T(8,128)(2,1)S(1)} %constant_dynamic-slice_fusion.5), channel_id=1, source_target_pairs={{0,4},{1,5},{2,6},{3,7},{4,0},{5,1},{6,2},{7,3},{8,12},{9,13},{10,... | collective-permute-start | bytes 1327112 | tf_op jit(solution)/shard_map/ppermute | solution.py:24
  531.9 46.9 %collective-permute-start.56 = (bf16[2,192,1536]{2,1,0:T(8,128)(2,1)S(1)}, bf16[2,192,1536]{2,1,0:T(8,128)(2,1)S(1)}, u32[]{:S(2)}, u32[]{:S(2)}) collective-permute-start(bf16[2,192,1536]{2,1,0:T(8,128)(2,1)S(1)} %dynamic-slice_bitcast_fusion.4), channel_id=1, source_target_pairs={{0,2},{1,3},{2,0},{3,1},{4,6},{5,7},{6,4},{7,5},{8,10},{9,11},{10,... | collective-permute-start | bytes 3538952 | tf_op jit(solution)/shard_map/ppermute | solution.py:24
  535.3 45.5 %collective-permute-start.64 = (bf16[1,192,1536]{2,1,0:T(8,128)(2,1)S(1)}, bf16[1,192,1536]{2,1,0:T(8,128)(2,1)S(1)}, u32[]{:S(2)}, u32[]{:S(2)}) collective-permute-start(bf16[1,192,1536]{2,1,0:T(8,128)(2,1)S(1)} %constant_dynamic-slice_fusion.2), channel_id=1, source_target_pairs={{0,4},{1,5},{2,6},{3,7},{4,0},{5,1},{6,2},{7,3},{8,12},{9,13},{10,... | collective-permute-start | bytes 1769480 | tf_op jit(solution)/shard_map/ppermute | solution.py:24
  579.2 24.7 %collective-permute-start.57 = (bf16[1,192,1536]{2,1,0:T(8,128)(2,1)S(1)}, bf16[1,192,1536]{2,1,0:T(8,128)(2,1)S(1)}, u32[]{:S(2)}, u32[]{:S(2)}) collective-permute-start(bf16[1,192,1536]{2,1,0:T(8,128)(2,1)S(1)} %constant_dynamic-slice_fusion.4), channel_id=1, source_target_pairs={{0,4},{1,5},{2,6},{3,7},{4,0},{5,1},{6,2},{7,3},{8,12},{9,13},{10,... | collective-permute-start | bytes 1769480 | tf_op jit(solution)/shard_map/ppermute | solution.py:24
  (105 other events, 924.9 us)

commit v3 on v2

v3 whole, which is shorter than its diff:
```python
import functools
import math

import jax
import jax.numpy as jnp
from jax import lax
from jax.experimental import pallas as pl
from jax.experimental.pallas import tpu as pltpu
from jax.sharding import PartitionSpec as P

HEAD_SIZE = 64
ROW_MIN = 2048
TILE = 256
BF16 = jnp.bfloat16
F32 = jnp.float32


def meeting(*values):
    return lax.optimization_barrier(values)


def after(value, token):
    return lax.optimization_barrier((value, token))[0]


def swap(value, axis, by):
    return lax.ppermute(value, axis, [(i, i ^ by) for i in range(lax.axis_size(axis))])


def shift(value, axis, by):
    peers = lax.axis_size(axis)
    pairs = [(i, i + by) for i in range(peers) if 0 <= i + by < peers]
    return lax.ppermute(value, axis, pairs)


def tensor_place():
    place = lax.axis_index("tensor")
    return place // 2, place % 2


def ordered(own, far, mate, far_mate, axis):
    side, core = tensor_place()
    near = (jnp.where(core == 0, own, mate), jnp.where(core == 0, mate, own))
    away = (jnp.where(core == 0, far, far_mate), jnp.where(core == 0, far_mate, far))
    low = [jnp.where(side == 0, n, a) for n, a in zip(near, away)]
    high = [jnp.where(side == 0, a, n) for n, a in zip(near, away)]
    return jnp.concatenate(low + high, axis)


def gather_near(own):
    far = swap(own, "tensor", 2)
    return own, swap(own, "tensor", 1), far, swap(far, "tensor", 1)


def gather_staged(own, first, second):
    far = swap(after(own, first), "tensor", 2)
    far, late = after((far, own), second)
    return own, swap(late, "tensor", 1), far, swap(far, "tensor", 1)


def gather(own, axis):
    own, mate, far, far_mate = gather_near(own)
    return ordered(own, far, mate, far_mate, axis)


def scatter_near(away, low):
    got = swap(away, "tensor", 1)
    total = (low.astype(F32) + got[low.shape[0] :].astype(F32)).astype(BF16)
    return got, total, swap(total, "tensor", 2)


def rows_to_cols(own, mate, far, far_mate, later):
    width = own.shape[1]
    got = after(swap(jnp.concatenate([far, far_mate], 1), "tensor", 2), later)
    other = swap(jnp.concatenate([mate, got[:, width:]], 0), "tensor", 1)
    size = own.shape[0]
    return jnp.concatenate([own, other[:size], got[:, :width], other[size:]], 0)


def quarters(value, axis):
    return jnp.split(value, 4, axis)


def own_blocks(near):
    return jnp.concatenate([quarters(value, 1)[r] for r, value in enumerate(near)], 0)


def trade(value, start, done):
    return after(swap(after(value, start), "seq", 1), done)


def halve(blocks, bit):
    count, rows, cols = blocks.shape
    side = (lax.axis_index("seq") >> bit) % 2
    parts = blocks.reshape(count // 2, 2, rows, cols)
    send = lax.dynamic_index_in_dim(parts, 1 - side, 1, False)
    keep = lax.dynamic_index_in_dim(parts, side, 1, False)
    return keep, swap(send, "seq", 1 << bit)


def added(keep, got):
    return keep.astype(F32) + got.astype(F32)


def halve_all(blocks, bit):
    while blocks.shape[0] > 1:
        blocks = added(*halve(blocks.astype(BF16), bit))
        bit += 1
    return blocks[0].astype(F32)


def halve_end(keep, got, bit):
    return halve_all(added(keep, got), bit)


def reduce_small(vectors):
    count = lax.axis_size("seq")
    kinds, width = vectors.shape
    parts = vectors.reshape(kinds, count, width // count).transpose(1, 0, 2)
    bit = 0
    while parts.shape[0] > 1:
        parts = added(*halve(parts, bit))
        bit += 1
    return parts[0]


def frame_clip_labels(segment, row_length):
    frame_index = jnp.arange(segment.shape[0], dtype=jnp.int32)
    border = (frame_index % row_length == 0) | (segment != jnp.roll(segment, 1))
    clip_starts = lax.cummax(jnp.where(border, frame_index, 0), axis=0)
    return (clip_starts, (frame_index - clip_starts + 1).astype(jnp.float32))


def tile_ranges(q_labels, key_labels):
    q = q_labels.reshape(-1, TILE)
    k = key_labels.reshape(-1, TILE)
    meets = (k[None, :, 0] <= q[:, None, -1]) & (k[None, :, -1] >= q[:, None, 0])
    index = jnp.arange(k.shape[0], dtype=jnp.int32)[None]
    low = jnp.min(jnp.where(meets, index, k.shape[0]), 1)
    high = jnp.max(jnp.where(meets, index + 1, 0), 1)
    return jnp.stack([low, high], 1).reshape(-1)

def head_rows(g):
    return slice(g * HEAD_SIZE, (g + 1) * HEAD_SIZE)

def fill_natural(dest, refs):
    size = refs[0].shape[1]
    for part, ref in enumerate(refs):
        dest[part * size : (part + 1) * size, :] = ref[...].T

def relative(place, r, size):
    return pl.ds(pl.multiple_of((place ^ r) * size, size), size)


def forward_body(span, q, k0, k1, k2, v0, v1, v2, tk, tv, qlab, klab, w_out,
                 out, lse, away, own, low, keys, vals):
    rows, size = q.shape
    group = rows // HEAD_SIZE
    pieces = size // TILE
    fill_natural(keys, (k0, k1, k2))
    for part, ref in enumerate((v0, v1, v2)):
        for piece in range(pieces):
            vals[part * pieces + piece] = ref[:, piece * TILE : (piece + 1) * TILE]
    for tile in range(pieces):
        cols = slice(tile * TILE, (tile + 1) * TILE)
        lab = qlab[:, cols]
        state = []
        for g in range(group):
            part = q[head_rows(g), cols].astype(F32)
            top = jnp.sum(part * tk[head_rows(g), :], 0, keepdims=True)
            state += [
                top,
                jnp.ones_like(top),
                jnp.broadcast_to(tv[head_rows(g), :], (HEAD_SIZE, TILE)),
            ]

        def step(j, state):
            start = pl.multiple_of(j * TILE, TILE)
            seen = klab[pl.ds(start, TILE), :] == lab
            fresh = []
            for g in range(group):
                top, total, acc = state[3 * g : 3 * g + 3]
                s = dot_nn(keys[pl.ds(start, TILE), head_rows(g)], q[head_rows(g), cols])
                s = jnp.where(seen, s, -1e30)
                new = jnp.maximum(top, jnp.max(s, 0, keepdims=True))
                fade = jnp.exp(top - new)
                p = jnp.exp(s - new)
                total = total * fade + jnp.sum(p, 0, keepdims=True)
                acc = acc * fade + dot_nn(vals[j, head_rows(g), :], p.astype(BF16))
                fresh += [new, total, acc]
            return tuple(fresh)

        state = lax.fori_loop(span[2 * tile], span[2 * tile + 1], step, tuple(state))
        for g in range(group):
            top, total, acc = state[3 * g : 3 * g + 3]
            out[head_rows(g), cols] = (acc / total).astype(BF16)
            lse[g : g + 1, cols] = top + jnp.log(total)
    place = span[2 * pieces]
    share = own.shape[0]

    def sent(r):
        return dot_tn(out[:, relative(place, r, share)], w_out[...])

    away[:share, :] = sent(1).astype(BF16)
    away[share:, :] = sent(3).astype(BF16)
    low[...] = sent(2).astype(BF16)
    own[...] = sent(0)


def backward_body(span, q, k0, k1, k2, v0, v1, v2, tk, tv, qlab, klab, w_out, out, lse,
                  g0, g1, g2, g3, dq, to_prev, kept, to_next, dtk, dtv,
                  og, keys, vals, tkeys, ak, av):
    rows, size = q.shape
    group = rows // HEAD_SIZE
    pieces = size // TILE
    share = g0.shape[0]
    for r, ref in enumerate((g0, g1, g2, g3)):
        og[:, relative(span[2 * pieces], r, share)] = dot_nt(w_out[...], ref[...]).astype(BF16)
    fill_natural(keys, (k0, k1, k2))
    fill_natural(vals, (v0, v1, v2))
    for part, ref in enumerate((k0, k1, k2)):
        for piece in range(pieces):
            tkeys[part * pieces + piece] = ref[:, piece * TILE : (piece + 1) * TILE]
    ak[...] = jnp.zeros_like(ak)
    av[...] = jnp.zeros_like(av)
    for tile in range(pieces):
        cols = slice(tile * TILE, (tile + 1) * TILE)
        lab = qlab[:, cols]
        state, norms, deltas = [], [], []
        for g in range(group):
            hr = head_rows(g)
            qf = q[hr, cols].astype(F32)
            gf = og[hr, cols].astype(F32)
            norm = lse[g : g + 1, cols]
            delta = jnp.sum(gf * out[hr, cols].astype(F32), 0, keepdims=True)
            pt = jnp.exp(jnp.sum(qf * tk[hr, :], 0, keepdims=True) - norm)
            st = pt * (jnp.sum(gf * tv[hr, :], 0, keepdims=True) - delta)
            gk = jnp.sum(qf * st, 1, keepdims=True)
            gv = jnp.sum(gf * pt, 1, keepdims=True)
            if tile == 0:
                dtk[hr, :] = gk
                dtv[hr, :] = gv
            else:
                dtk[hr, :] += gk
                dtv[hr, :] += gv
            state.append(tk[hr, :] * st)
            norms.append(norm)
            deltas.append(delta)

        def step(j, state):
            start = pl.multiple_of(j * TILE, TILE)
            seen = klab[pl.ds(start, TILE), :] == lab
            fresh = []
            for g in range(group):
                hr = head_rows(g)
                s = dot_nn(keys[pl.ds(start, TILE), hr], q[hr, cols])
                p = jnp.exp(jnp.where(seen, s, -1e30) - norms[g])
                m = dot_nn(vals[pl.ds(start, TILE), hr], og[hr, cols])
                ds = (p * (m - deltas[g])).astype(BF16)
                av[j, hr, :] += dot_nt(og[hr, cols], p.astype(BF16))
                ak[j, hr, :] += dot_nt(q[hr, cols], ds)
                fresh.append(state[g] + dot_nn(tkeys[j, hr, :], ds))
            return tuple(fresh)

        state = lax.fori_loop(span[2 * tile], span[2 * tile + 1], step, tuple(state))
        for g in range(group):
            dq[head_rows(g), cols] = state[g]
    for part, dest in enumerate((to_prev, kept, to_next)):
        for piece in range(pieces):
            at = slice(piece * TILE, (piece + 1) * TILE)
            dest[0, :, at] = ak[part * pieces + piece].astype(dest.dtype)
            dest[1, :, at] = av[part * pieces + piece].astype(dest.dtype)


def attend(span, q, ks, vs, tk, tv, qlab, klab, w_out):
    cols, size = q.shape
    share, width = size // 4, w_out.shape[1]
    tiles = 3 * size // TILE
    low = lambda *dims: jax.ShapeDtypeStruct(dims, BF16)
    wide = lambda *dims: jax.ShapeDtypeStruct(dims, F32)
    vmem = pl.BlockSpec(memory_space=pltpu.VMEM)
    return pl.pallas_call(
        forward_body,
        in_specs=[pl.BlockSpec(memory_space=pltpu.SMEM)] + [vmem] * 12,
        out_specs=[vmem] * 5,
        out_shape=[low(cols, size), wide(cols // HEAD_SIZE, size), low(2 * share, width),
                   wide(share, width), low(share, width)],
        scratch_shapes=[pltpu.VMEM((3 * size, cols), BF16), pltpu.VMEM((tiles, cols, TILE), BF16)],
        name="attend", cost_estimate=FREE,
    )(span, q, *ks, *vs, tk, tv, qlab, klab, w_out)


def attend_back(span, q, ks, vs, tk, tv, qlab, klab, w_out, out, lse, grads):
    cols, size = q.shape
    tiles = 3 * size // TILE
    low = lambda *dims: jax.ShapeDtypeStruct(dims, BF16)
    wide = lambda *dims: jax.ShapeDtypeStruct(dims, F32)
    vmem = pl.BlockSpec(memory_space=pltpu.VMEM)
    return pl.pallas_call(
        backward_body,
        in_specs=[pl.BlockSpec(memory_space=pltpu.SMEM)] + [vmem] * 18,
        out_specs=[vmem] * 6,
        out_shape=[wide(cols, size), low(2, cols, size), wide(2, cols, size), low(2, cols, size),
                   wide(cols, 1), wide(cols, 1)],
        scratch_shapes=[pltpu.VMEM((cols, size), BF16), pltpu.VMEM((3 * size, cols), BF16),
                        pltpu.VMEM((3 * size, cols), BF16), pltpu.VMEM((tiles, cols, TILE), BF16),
                        pltpu.VMEM((tiles, cols, TILE), F32), pltpu.VMEM((tiles, cols, TILE), F32)],
        name="attend_back", cost_estimate=FREE,
    )(span, q, *ks, *vs, tk, tv, qlab, klab, w_out, out, lse, *grads)


def tail_body(place, dq, kept, ahead, behind, cosine, sine, wq, wk, wv, raw, away, own, low, flipped):
    part, size = dq.shape
    half = HEAD_SIZE // 2

    def returned(block, base, scale):
        for h in range(part // HEAD_SIZE):
            a = block[h * HEAD_SIZE : h * HEAD_SIZE + half, :]
            b = block[h * HEAD_SIZE + half : (h + 1) * HEAD_SIZE, :]
            at = base + h * HEAD_SIZE
            raw[at : at + half, :] = ((a * cosine[...] + b * sine[...]) * scale).astype(BF16)
            raw[at + half : at + HEAD_SIZE, :] = (
                (b * cosine[...] - a * sine[...]) * scale
            ).astype(BF16)

    def whole(index):
        return kept[index] + ahead[index].astype(F32) + behind[index].astype(F32)

    returned(dq[...], 0, 1.0 / math.sqrt(HEAD_SIZE))
    returned(whole(0), part, 1.0)
    raw[2 * part :, :] = whole(1).astype(BF16)
    flipped[...] = raw[...].T

    def sent(r):
        at = relative(place[0], r, part)
        return sum(
            dot_nt(flipped[:, i * part : (i + 1) * part], weight[at, :])
            for i, weight in enumerate((wq, wk, wv))
        )

    away[:size, :] = sent(1).astype(BF16)
    away[size:, :] = sent(3).astype(BF16)
    low[...] = sent(2).astype(BF16)
    own[...] = sent(0)


def tail(place, dq, kept, ahead, behind, tables, wq, wk, wv):
    part, size = dq.shape
    low = lambda *dims: jax.ShapeDtypeStruct(dims, BF16)
    vmem = pl.BlockSpec(memory_space=pltpu.VMEM)
    return pl.pallas_call(
        tail_body,
        in_specs=[pl.BlockSpec(memory_space=pltpu.SMEM)] + [vmem] * 9,
        out_specs=[vmem] * 4,
        out_shape=[low(3 * part, size), low(2 * size, part), jax.ShapeDtypeStruct((size, part), F32),
                   low(size, part)],
        scratch_shapes=[pltpu.VMEM((size, 3 * part), BF16)],
        name="tail", cost_estimate=FREE,
    )(place, dq, kept, ahead, behind, *tables, wq, wk, wv)


def rotary_tables(frame_positions):
    half_dim = HEAD_SIZE // 2
    frequency = jnp.exp(jnp.arange(half_dim, dtype=jnp.float32) * (-math.log(10000.0) / half_dim))
    angles = frequency[:, None] * frame_positions[None, :]
    return (jnp.cos(angles), jnp.sin(angles))


def rotate(rows, tables, sign=1.0):
    count, size = rows.shape
    halves = rows.reshape(count // HEAD_SIZE, 2, HEAD_SIZE // 2, size)
    cosine, sine = tables[0][None], tables[1][None] * sign
    first = halves[:, 0] * cosine - halves[:, 1] * sine
    second = halves[:, 1] * cosine + halves[:, 0] * sine
    return jnp.stack([first, second], 1).reshape(count, size)


def product(left, right):
    return jnp.dot(left, right, preferred_element_type=jnp.float32)


def inner_rows(left, right):
    return jnp.einsum("nd,nf->df", left, right, preferred_element_type=jnp.float32)


def back_project(gradient, weight):
    return jnp.einsum("nf,df->nd", gradient, weight, preferred_element_type=jnp.float32)


def by_feature(left, right):
    return jnp.einsum("nd,df->fn", left, right, preferred_element_type=jnp.float32)


def columns(weight, start, size):
    return lax.dynamic_slice_in_dim(weight, start, size, 1)


def rows_of(weight, start, size):
    return lax.dynamic_slice_in_dim(weight, start, size, 0)


def normalize(value_rows):
    means = jnp.mean(value_rows, -1, keepdims=True)
    centred = value_rows - means
    inverse = lax.rsqrt(jnp.mean(centred * centred, -1, keepdims=True) + 1e-05)
    return centred * inverse, inverse


def norm_backward(gradient, scaled, inverse, norm_gain):
    scaled_grad = gradient * norm_gain
    plain = jnp.mean(scaled_grad, -1, keepdims=True)
    cross = jnp.mean(scaled_grad * scaled, -1, keepdims=True)
    return inverse * (scaled_grad - plain - scaled * cross)


FREE = pl.CostEstimate(flops=1, transcendentals=0, bytes_accessed=1)


def dot_nn(left, right):
    return lax.dot_general(left, right, (((1,), (0,)), ((), ())), preferred_element_type=F32)


def dot_nt(left, right):
    return lax.dot_general(left, right, (((1,), (1,)), ((), ())), preferred_element_type=F32)


def dot_tn(left, right):
    return lax.dot_general(left, right, (((0,), (0,)), ((), ())), preferred_element_type=F32)


def head_weights(query, key, lanes, which):
    mine = jnp.where(lanes == which, query, jnp.zeros_like(query))
    scores = dot_nt(mine, key) * (1.0 / math.sqrt(HEAD_SIZE))
    weights = jnp.exp(scores - jnp.max(scores, -1, keepdims=True))
    return weights / jnp.sum(weights, -1, keepdims=True)


def pair_cols(refs, p, rows):
    ref = refs[p * 2 * HEAD_SIZE // refs[0].shape[1]]
    start = p * 2 * HEAD_SIZE % refs[0].shape[1]
    return ref[rows, start : start + 2 * HEAD_SIZE]


def cross_forward_body(width_block, place, rows, own, got, far, norms, q0, q1, q2, q3,
                       c0, c1, c2, c3, o0, o1, o2, o3,
                       normed_two, queries, crossed, first, second, normed_three,
                       flip_own, flip_away):
    width = rows.shape[1]
    kv = (c0, c1, c2, c3)
    context_rows = c0.shape[0] // 2
    key_rows, value_rows = slice(0, context_rows), slice(context_rows, 2 * context_rows)
    lanes = lax.broadcasted_iota(jnp.int32, (rows.shape[0], 2 * HEAD_SIZE), 1) // HEAD_SIZE
    residual = (
        rows[...].astype(F32) + own[...] + got[...].astype(F32) + far[...].astype(F32)
    )
    first[...] = residual
    scaled, _ = normalize(residual)
    low = (scaled * norms[2:3, :] + norms[3:4, :]).astype(BF16)
    normed_two[...] = low
    part = width // 4
    for b, ref in enumerate((q0, q1, q2, q3)):
        queries[:, b * part : (b + 1) * part] = dot_nn(low, ref[...]).astype(BF16)
    for p in range(width // (2 * HEAD_SIZE)):
        cols = slice(p * 2 * HEAD_SIZE, (p + 1) * 2 * HEAD_SIZE)
        q, k, v = queries[:, cols], pair_cols(kv, p, key_rows), pair_cols(kv, p, value_rows)
        mixed = [dot_nn(head_weights(q, k, lanes, g).astype(BF16), v) for g in (0, 1)]
        crossed[:, cols] = jnp.where(lanes == 0, mixed[0], mixed[1]).astype(BF16)
    for b, ref in enumerate((o0, o1, o2, o3)):
        residual = residual + dot_nn(crossed[:, b * part : (b + 1) * part], ref[...])
    second[...] = residual
    scaled, _ = normalize(residual)
    low = (scaled * norms[4:5, :] + norms[5:6, :]).astype(BF16)
    normed_three[...] = low
    deal_rows(low.T, width_block, place[0], flip_own, flip_away)


def cross_forward(devices, place, rows, own, got, far, norms, query_parts, kv_parts, out_parts):
    size, width = rows.shape
    low = jax.ShapeDtypeStruct(rows.shape, BF16)
    wide = jax.ShapeDtypeStruct(rows.shape, F32)
    flip = jax.ShapeDtypeStruct((width // 2, size), BF16)
    vmem = pl.BlockSpec(memory_space=pltpu.VMEM)
    block = pl.BlockSpec((size, width), lambda i: (0, 0))
    return pl.pallas_call(
        functools.partial(cross_forward_body, width // devices),
        grid=(1,),
        in_specs=[pl.BlockSpec(memory_space=pltpu.SMEM)] + [block] * 4 + [vmem] * 13,
        out_shape=[low, low, low, wide, wide, low, flip, flip],
        cost_estimate=FREE, name="cross",
    )(place, rows, own, got, far, norms, *query_parts, *kv_parts, *out_parts)


def deal_rows(rows, size, column, own, away):
    for b in range(rows.shape[0] // (2 * size)):
        at = slice(b * size, (b + 1) * size)
        even = rows[2 * b * size : (2 * b + 1) * size, :]
        odd = rows[(2 * b + 1) * size : (2 * b + 2) * size, :]

        @pl.when(column == 0)
        def _():
            own[at, :] = even
            away[at, :] = odd

        @pl.when(column != 0)
        def _():
            own[at, :] = odd
            away[at, :] = even


def ffn_body(unit_block, place, n0, n1, n2, n3, g0, g1, g2, g3, gate_w, up_w, down_w,
             hidden, hid_own, hid_away, gate_grad, lifted_grad, away, own, low, grad, grad_pair,
             normed, total):
    step = pl.program_id(0)
    share = n0.shape[0]
    part = g0.shape[2]

    @pl.when(step == 0)
    def _():
        for b, ref in enumerate((n0, n1, n2, n3)):
            normed[b * share : (b + 1) * share, :] = ref[...]
        total[...] = jnp.zeros_like(total)
        for c, ref in enumerate((g0, g1, g2, g3)):
            for b in range(4):
                rows, cols = relative(place[1], b, share), relative(place[1], c, part)
                grad[b * share : (b + 1) * share, cols] = ref[0, rows, :]
                grad_pair[b * share : (b + 1) * share, cols] = ref[1, rows, :]

    gate = dot_nn(normed[...], gate_w[...])
    lifted = dot_nn(normed[...], up_w[...])
    back = dot_nt(grad[...], down_w[...]).astype(BF16).astype(F32)
    sig = jax.nn.sigmoid(gate)
    swish = gate * sig
    made = (swish * lifted).astype(BF16)
    hidden[...] = made
    deal_rows(made.T, unit_block, place[0], hid_own, hid_away)
    gg = (back * lifted * sig * (1.0 + gate * (1.0 - sig))).astype(BF16)
    lg = (back * swish).astype(BF16)
    gate_grad[...] = gg
    lifted_grad[...] = lg
    total[...] += dot_nt(gg, gate_w[...]) + dot_nt(lg, up_w[...])

    @pl.when(step == pl.num_programs(0) - 1)
    def _():
        own[...] = total[:share, :]
        low[...] = total[2 * share : 3 * share, :].astype(BF16)
        away[:share, :] = total[share : 2 * share, :].astype(BF16)
        away[share:, :] = total[3 * share :, :].astype(BF16)


def ffn(devices, place, parts, grads, gate_w, up_w, down_w):
    share, width = parts[0].shape
    size, units = 4 * share, gate_w.shape[1]
    tile = units // 2
    whole = lambda *dims: pl.BlockSpec(dims, lambda i, s: (0,) * len(dims))
    cols = lambda r: pl.BlockSpec((r, tile), lambda i, s: (0, i))
    rows = lambda c: pl.BlockSpec((tile, c), lambda i, s: (i, 0))
    halves = pl.BlockSpec((tile // 2, size), lambda i, s: (i, 0))
    low = lambda *dims: jax.ShapeDtypeStruct(dims, BF16)
    return pl.pallas_call(
        functools.partial(ffn_body, units // devices),
        grid_spec=pltpu.PrefetchScalarGridSpec(
            num_scalar_prefetch=1,
            grid=(2,),
            in_specs=[whole(share, width)] * 4 + [whole(2, size, width // 4)] * 4
            + [cols(width), cols(width), rows(width)],
            out_specs=[cols(size), halves, halves, cols(size), cols(size),
                       whole(2 * share, width), whole(share, width), whole(share, width),
                       whole(size, width), whole(size, width)],
            scratch_shapes=[pltpu.VMEM((size, width), BF16), pltpu.VMEM((size, width), F32)],
        ),
        out_shape=[low(size, units), low(units // 2, size), low(units // 2, size),
                   low(size, units), low(size, units), low(2 * share, width),
                   jax.ShapeDtypeStruct((share, width), F32), low(share, width),
                   low(size, width), low(size, width)],
        cost_estimate=FREE, name="ffn",
    )(place, *parts, *grads, gate_w, up_w, down_w)


def cross_backward_body(own, got, far, grad, first, second, norms, q0, q1, q2, q3,
                        c0, c1, c2, c3, o0, o1, o2, o3, queries,
                        grad_two, query_grad, kv_grad, vectors, grad_one, crossed_grad):
    width = grad.shape[1]
    kv = (c0, c1, c2, c3)
    context_rows = c0.shape[0] // 2
    key_rows, value_rows = slice(0, context_rows), slice(context_rows, 2 * context_rows)
    part = width // 4
    lanes = lax.broadcasted_iota(jnp.int32, (grad.shape[0], 2 * HEAD_SIZE), 1) // HEAD_SIZE
    lane_k = lax.broadcasted_iota(jnp.int32, (context_rows, 2 * HEAD_SIZE), 1) // HEAD_SIZE
    scale = 1.0 / math.sqrt(HEAD_SIZE)
    arrived = own[...] + got[...].astype(F32) + far[...].astype(F32)
    scaled, inverse = normalize(second[...])
    vectors[0:1, :] = jnp.sum(arrived * scaled, 0, keepdims=True)
    vectors[1:2, :] = jnp.sum(arrived, 0, keepdims=True)
    two = grad[...].astype(F32) + norm_backward(arrived, scaled, inverse, norms[4:5, :])
    low = two.astype(BF16)
    grad_two[...] = low
    for b, ref in enumerate((o0, o1, o2, o3)):
        crossed_grad[:, b * part : (b + 1) * part] = dot_nt(low, ref[...]).astype(BF16)
    for p in range(width // (2 * HEAD_SIZE)):
        cols = slice(p * 2 * HEAD_SIZE, (p + 1) * 2 * HEAD_SIZE)
        q, k, v = queries[:, cols], pair_cols(kv, p, key_rows), pair_cols(kv, p, value_rows)
        g_rows = crossed_grad[:, cols]
        found = []
        for g in (0, 1):
            probs = head_weights(q, k, lanes, g)
            change = dot_nt(jnp.where(lanes == g, g_rows, jnp.zeros_like(g_rows)), v)
            delta = jnp.sum(change * probs, -1, keepdims=True)
            ds = (probs * (change - delta)).astype(BF16)
            found.append((dot_nn(ds, k), dot_tn(ds, q), dot_tn(probs.astype(BF16), g_rows)))
        query_grad[:, cols] = (
            jnp.where(lanes == 0, found[0][0], found[1][0]) * scale
        ).astype(BF16)
        kv_grad[:context_rows, cols] = (
            jnp.where(lane_k == 0, found[0][1], found[1][1]) * scale
        ).astype(BF16)
        kv_grad[context_rows:, cols] = jnp.where(lane_k == 0, found[0][2], found[1][2]).astype(
            BF16
        )
    back = jnp.zeros(grad.shape, F32)
    for b, ref in enumerate((q0, q1, q2, q3)):
        back = back + dot_nt(query_grad[:, b * part : (b + 1) * part], ref[...])
    scaled, inverse = normalize(first[...])
    vectors[2:3, :] = jnp.sum(back * scaled, 0, keepdims=True)
    vectors[3:4, :] = jnp.sum(back, 0, keepdims=True)
    grad_one[...] = (two + norm_backward(back, scaled, inverse, norms[2:3, :])).astype(BF16)


def cross_backward(own, got, far, grad, first, second, norms, query_parts, kv_parts, out_parts,
                   queries):
    rows, width = own.shape
    low = lambda r: jax.ShapeDtypeStruct((r, width), BF16)
    block = pl.BlockSpec((rows, width), lambda i: (0, 0))
    return pl.pallas_call(
        cross_backward_body,
        grid=(1,),
        out_shape=[low(rows), low(rows), low(kv_parts[0].shape[0]),
                   jax.ShapeDtypeStruct((4, width), F32), low(rows)],
        in_specs=[block] * 6 + [pl.BlockSpec(memory_space=pltpu.VMEM)] * 14,
        scratch_shapes=[pltpu.VMEM((rows, width), BF16)],
        cost_estimate=FREE, name="cross_back",
    )(own, got, far, grad, first, second, norms, *query_parts, *kv_parts, *out_parts, queries)


def meet_body(left, left_pair, right, right_pair, out):
    out[...] = (
        dot_nn(left[...], right[...]) + dot_nn(left_pair[...], right_pair[...])
    ).astype(BF16)


def meet(rows, cols):
    count, size = rows[0].shape
    width = cols[0].shape[1]
    tile = width // 3
    left = pl.BlockSpec((count, size), lambda i: (0, 0))
    right = pl.BlockSpec((size, tile), lambda i: (0, i))
    return pl.pallas_call(
        meet_body,
        grid=(3,),
        in_specs=[left, left, right, right],
        out_specs=pl.BlockSpec((count, tile), lambda i: (0, i)),
        out_shape=jax.ShapeDtypeStruct((count, width), BF16),
        name="meet", cost_estimate=FREE,
    )(*rows, *cols)


def down_body(hidden, down_w, away, own, low):
    share = own.shape[0]

    def sent(r):
        return dot_nn(hidden[r * share : (r + 1) * share, :], down_w[...])

    away[:share, :] = sent(1).astype(BF16)
    away[share:, :] = sent(3).astype(BF16)
    low[...] = sent(2).astype(BF16)
    own[...] = sent(0)


def down_parts(hidden, down_w):
    share, width = hidden.shape[0] // 4, down_w.shape[1]
    low = lambda *dims: jax.ShapeDtypeStruct(dims, BF16)
    return pl.pallas_call(
        down_body,
        out_shape=[low(2 * share, width), jax.ShapeDtypeStruct((share, width), F32),
                   low(share, width)],
        name="down", cost_estimate=FREE,
    )(hidden, down_w)


def bundle_body(devices, place, f0, f1, f2, f3, b0, b1, b2, b3, a0, a1, a2, a3, attended,
                context, kv, out):
    width = a0.shape[1]
    part, share = width // 4, a0.shape[0]
    own = lambda refs: jnp.concatenate(
        [ref[:, width + r * part : width + (r + 1) * part] for r, ref in enumerate(refs)], 0
    )
    full = lambda refs: jnp.concatenate([ref[:, :width] for ref in refs], 0)
    fronts, backs = (f0, f1, f2, f3), (b0, b1, b2, b3)
    rows = width // devices
    small = part // devices
    half = width // 2

    def put(block, base, left):
        for d in range(devices):
            at = slice(base, base + block.shape[0] // devices)
            piece = block[d * block.shape[0] // devices : (d + 1) * block.shape[0] // devices, :]
            out[d, at, left : left + block.shape[1]] = piece.astype(BF16)

    put(dot_tn(full(fronts), own(backs)), 0, 0)
    count = context.shape[0]
    put(dot_tn(context[...], kv[:count, :]), 0, part)
    put(dot_tn(context[...], kv[count:, :]), rows // 2, part)
    grads = dot_tn(own(fronts), full(backs))
    put(grads[:, :half], 0, half)
    put(grads[:, half:], small, half)
    grads = sum(
        dot_nn(attended[:, relative(place[0], r, share)], ref[...])
        for r, ref in enumerate((a0, a1, a2, a3))
    )
    put(grads[:, :half], 2 * small, half)
    put(grads[:, half:], 3 * small, half)


def bundle_grads(devices, place, fronts, backs, ones, attended, context, kv):
    width = ones[0].shape[1]
    vmem = pl.BlockSpec(memory_space=pltpu.VMEM)
    return pl.pallas_call(
        functools.partial(bundle_body, devices),
        in_specs=[pl.BlockSpec(memory_space=pltpu.SMEM)] + [vmem] * 15,
        out_specs=vmem,
        out_shape=jax.ShapeDtypeStruct((devices, width // devices, width), BF16),
        name="bundle", cost_estimate=FREE,
    )(place, *fronts, *backs, *ones, attended, context, kv)


def front_body(width_block, place, x0, x1, x2, x3, g0, g1, g2, g3, cosine, sine, wq, wk, wv,
               queries, pair, rows, low, nrm_own, nrm_away, norms, means, inverses, wide):
    size, part = x0.shape
    for r, (x, g) in enumerate(((x0, g0), (x1, g1), (x2, g2), (x3, g3))):
        start = pl.multiple_of((place[0] ^ r) * part, 128)
        wide[:, pl.ds(start, part)] = x[...]
        norms[:, pl.ds(start, part)] = g[...]
    share = size // 4
    rows[...] = wide[pl.ds(pl.multiple_of(place[0] * share, share), share), :]
    values = wide[...].astype(F32)
    mean = jnp.mean(values, -1, keepdims=True)
    centred = values - mean
    inverse = lax.rsqrt(jnp.mean(centred * centred, -1, keepdims=True) + 1e-05)
    means[...] = mean
    inverses[...] = inverse
    normed = (centred * inverse * norms[0:1, :] + norms[1:2, :]).astype(BF16)
    low[...] = normed
    half = HEAD_SIZE // 2

    def turned(weight):
        return dot_nn(normed, weight[...]).T

    def rotated(block, dest, scale):
        for h in range(part // HEAD_SIZE):
            a = block[h * HEAD_SIZE : h * HEAD_SIZE + half, :]
            b = block[h * HEAD_SIZE + half : (h + 1) * HEAD_SIZE, :]
            dest[h * HEAD_SIZE : h * HEAD_SIZE + half, :] = (
                (a * cosine[...] - b * sine[...]) * scale
            ).astype(BF16)
            dest[h * HEAD_SIZE + half : (h + 1) * HEAD_SIZE, :] = (
                (b * cosine[...] + a * sine[...]) * scale
            ).astype(BF16)

    rotated(turned(wk), pair.at[0], 1.0)
    pair[1] = turned(wv).astype(BF16)
    rotated(turned(wq), queries, 1.0 / math.sqrt(HEAD_SIZE))
    deal_rows(normed.T, width_block, place[1], nrm_own, nrm_away)


def front(devices, place, parts, norm_parts, tables, wq, wk, wv):
    size, part = parts[0].shape
    width = 4 * part
    low = lambda *s: jax.ShapeDtypeStruct(s, BF16)
    wide = lambda *s: jax.ShapeDtypeStruct(s, F32)
    vmem = pl.BlockSpec(memory_space=pltpu.VMEM)
    return pl.pallas_call(
        functools.partial(front_body, width // devices),
        in_specs=[pl.BlockSpec(memory_space=pltpu.SMEM)] + [vmem] * 13,
        out_specs=[vmem] * 9,
        out_shape=[low(part, size), low(2, part, size), low(size // 4, width), low(size, width),
                   low(width // 2, size), low(width // 2, size), wide(6, width),
                   wide(size, 1), wide(size, 1)],
        scratch_shapes=[pltpu.VMEM((size, width), BF16)],
        cost_estimate=FREE, name="front",
    )(place, *parts, *norm_parts, *tables, wq, wk, wv)


def per_device(
    frames,
    segment,
    time_token,
    context,
    gain_attn,
    bias_attn,
    gain_cross,
    bias_cross,
    gain_ffn,
    bias_ffn,
    w_query,
    w_key,
    w_value,
    w_out,
    c_query,
    c_key,
    c_value,
    c_out,
    w_gate,
    w_up,
    w_down,
    out_grad,
):
    local_rows = frames.shape[0]
    local_width = frames.shape[1]
    model_width = w_query.shape[0]
    head_cols = w_query.shape[1]
    heads = head_cols // HEAD_SIZE
    number_of_frames = lax.axis_size("seq") * local_rows
    row_length = min(max(ROW_MIN, 64 * lax.axis_size("seq")), number_of_frames)
    first_frame = lax.axis_index("seq") * local_rows
    own_start = lax.axis_index("tensor") * local_width

    def own_cols(value):
        return lax.dynamic_slice_in_dim(value, own_start, local_width, value.ndim - 1)

    place = lax.axis_index("tensor")
    share = local_rows // 4

    def row_block(value, index):
        return rows_of(value, index * share, share)

    column = lax.axis_index("seq") % 2
    frame_parts_near = gather_near(frames)
    norm_parts = gather_near(
        jnp.stack([gain_attn, bias_attn, gain_cross, bias_cross, gain_ffn, bias_ffn])
    )
    clip_starts, frame_positions = frame_clip_labels(segment, row_length)
    own_labels = lax.dynamic_slice_in_dim(clip_starts, first_frame, local_rows)
    own_positions = lax.dynamic_slice_in_dim(frame_positions, first_frame, local_rows)
    blanks = jnp.full((local_rows,), -1, jnp.int32)
    key_labels = lax.dynamic_slice_in_dim(
        jnp.concatenate([blanks, clip_starts, blanks]), first_frame, 3 * local_rows
    )
    spans = jnp.concatenate(
        [tile_ranges(own_labels, key_labels), place.astype(jnp.int32).reshape(1)]
    )
    places = jnp.stack([column, place]).astype(jnp.int32)
    label_row, label_column = own_labels[None, :], key_labels[:, None]
    row_index = first_frame // row_length
    time_row = lax.dynamic_slice_in_dim(time_token, row_index, 1, 0).astype(F32)
    row_context = lax.dynamic_slice_in_dim(context, row_index, 1, 0)[0]
    context_rows = row_context.shape[0]
    tables = rotary_tables(own_positions)
    score_scale = 1.0 / math.sqrt(HEAD_SIZE)
    all_heads = model_width // HEAD_SIZE

    (
        queries, both, frame_rows, frame_normed, one_own_half, one_away_half, norms, means_one,
        inverse_one,
    ) = front(
        lax.axis_size("seq"), jnp.flip(places), frame_parts_near, norm_parts, tables, w_query,
        w_key, w_value,
    )
    own_keys, own_values = both[0], both[1]
    gain_one, bias_one = norms[0:1], norms[1:2]
    behind, ahead = shift(both, "seq", 1), shift(both, "seq", -1)
    out_pair = trade(out_grad, frame_parts_near[2], both)
    query_far = swap(after(c_query, frame_parts_near[3]), "tensor", 2)
    out_far = swap(after(c_out, frame_parts_near[3]), "tensor", 2)
    time_late = after(time_row, both)
    scaled_time, _ = normalize(time_late)
    time_normed = (scaled_time * gain_one + bias_one).astype(BF16)
    time_keys = by_feature(time_normed, w_key).astype(BF16).astype(F32)
    time_values = by_feature(time_normed, w_value).astype(BF16).astype(F32)
    context_late = after(row_context, both)
    context_kv = jnp.concatenate(
        [product(context_late, c_key), product(context_late, c_value)], 0
    ).astype(BF16)
    behind, ahead, query_far, out_far = lax.optimization_barrier(
        (behind, ahead, query_far, out_far)
    )
    keys = (behind[0], own_keys, ahead[0])
    values = (behind[1], own_values, ahead[1])
    attended, log_totals, one_away, one_own, one_low = attend(
        spans, queries, keys, values, time_keys, time_values, label_row, label_column, w_out
    )
    kv_parts = gather_staged(context_kv, both, attended)
    query_parts = (
        c_query, swap(after(c_query, both), "tensor", 1), query_far, swap(query_far, "tensor", 1)
    )
    out_parts = (c_out, swap(after(c_out, both), "tensor", 1), out_far, swap(out_far, "tensor", 1))
    one_got, _, one_far = scatter_near(one_away, one_low)
    (
        normed_two, cross_queries, crossed, residual_one, residual_two, normed_share, flip_own,
        flip_away,
    ) = cross_forward(
        lax.axis_size("seq"), places, frame_rows, one_own, one_got, one_far, norms,
        query_parts, kv_parts, out_parts,
    )
    normed_share, normed_got = meeting(
        normed_share, swap(after(one_away_half, attended), "seq", 1)
    )
    flip_got = swap(flip_away, "seq", 1)
    *three_parts, flip_got = meeting(*gather_near(normed_share), flip_got)
    flip_both = jnp.stack([flip_own, flip_got])
    flip_far = swap(flip_both, "tensor", 2)
    grad_parts = gather_staged(jnp.stack([out_grad, out_pair]), one_far, normed_share)
    (
        hidden, hidden_own, hidden_away, gate_grad, lifted_grad, three_away, three_own, three_low,
        grad_near, grad_pair,
    ) = ffn(lax.axis_size("seq"), places, three_parts, grad_parts, w_gate, w_up, w_down)
    three_away, three_low, flip_far = meeting(three_away, three_low, flip_far)
    three_got, _, three_far = scatter_near(three_away, three_low)
    hidden_got = swap(hidden_away, "seq", 1)
    flip_late, flip_far_late, gate_late, front_late = after(
        (flip_both, flip_far, gate_grad, jnp.concatenate([normed_two, crossed], 1)), three_far
    )
    flip_mate, flip_far_mate = swap(flip_late, "tensor", 1), swap(flip_far_late, "tensor", 1)
    gate_got = swap(gate_late, "seq", 1)
    front_far = swap(front_late, "tensor", 2)
    cross_full, cross_query_grad, kv_grad, norm_vectors, grad_one = cross_backward(
        three_own, three_got, three_far, grad_near, residual_one, residual_two, norms,
        query_parts, kv_parts, out_parts, cross_queries,
    )
    grad_one, hidden_got, flip_mate, flip_far_mate, front_far = meeting(
        grad_one, hidden_got, flip_mate, flip_far_mate, front_far
    )
    count = lax.axis_size("seq")

    def by_level(blocks):
        return blocks.reshape(count // 2, 2 * blocks.shape[0] // count, blocks.shape[1])

    down_keep, down_got = halve(
        by_level(meet((hidden_own, hidden_got), (grad_near, grad_pair))), 1
    )
    one_parts = gather_near(grad_one)
    back_late, lifted_late = after(
        (jnp.concatenate([cross_full, cross_query_grad], 1), lifted_grad), one_parts[3]
    )
    back_far = swap(back_late, "tensor", 2)
    lifted_got = swap(lifted_late, "seq", 1)
    query_grad, to_prev, kept, to_next, time_key_grad, time_value_grad = attend_back(
        spans, queries, keys, values, time_keys, time_values, label_row, label_column, w_out,
        attended, log_totals, one_parts,
    )
    to_prev, to_next, back_far, gate_got, down_got = meeting(
        to_prev, to_next, back_far, gate_got, down_got
    )
    from_next, from_prev = shift(to_prev, "seq", -1), shift(to_next, "seq", 1)
    down_keep, down_got = halve(added(down_keep, down_got).astype(BF16), 2)
    three_pair = [
        jnp.concatenate([value[i] for value in (flip_both, flip_mate, flip_far, flip_far_mate)], 1)
        for i in (0, 1)
    ]
    gate_keep, gate_cross = halve(by_level(meet(three_pair, (gate_grad, gate_got))), 1)
    down_away, down_own, down_low = down_parts(after(hidden, to_prev), w_down)
    from_next, from_prev, down_got, lifted_got = meeting(
        from_next, from_prev, down_got, lifted_got
    )
    raw, last_away, last_own, last_low = tail(
        places[1:], query_grad, kept, from_next, from_prev, tables, w_query, w_key, w_value
    )
    last_away, last_low, gate_cross = meeting(last_away, last_low, gate_cross)
    last_got, last_sum, last_far = scatter_near(last_away, last_low)
    frame_grad = last_own + last_got[:local_rows].astype(F32) + last_far.astype(F32)

    def to_frames(rows, weight):
        return jnp.einsum("fn,df->nd", rows, weight, preferred_element_type=F32)

    time_key_grad, time_value_grad = after((time_key_grad, time_value_grad), from_next)
    time_grad = to_frames(time_key_grad.astype(BF16), w_key) + to_frames(
        time_value_grad.astype(BF16), w_value
    )
    own_scaled = (frames.astype(F32) - means_one) * inverse_one
    scaled_grad = frame_grad * gain_attn[None]
    sums = jnp.concatenate(
        [
            jnp.sum(scaled_grad, -1),
            jnp.sum(scaled_grad * own_scaled, -1),
            time_grad[0],
            norm_vectors.reshape(-1),
        ]
    )[None]
    sums = sums + swap(sums, "tensor", 1)
    sums = sums + swap(sums, "tensor", 2)
    plain = sums[0, :local_rows, None] / model_width
    cross = sums[0, local_rows : 2 * local_rows, None] / model_width
    vectors = own_cols(sums[0, 2 * local_rows :].reshape(5, model_width))
    attend_full = ordered(*[after(one_parts, from_next)[i] for i in (0, 2, 1, 3)], 0)
    d_frames = own_cols(attend_full).astype(F32) + inverse_one * (
        scaled_grad - plain - own_scaled * cross
    )
    d_gain_attn = jnp.sum(frame_grad * own_scaled, 0) + vectors[0] * own_cols(scaled_time)[0]
    d_bias_attn = jnp.sum(frame_grad, 0) + vectors[0]
    small = reduce_small(
        jnp.stack([d_gain_attn, d_bias_attn, vectors[3], vectors[4], vectors[1], vectors[2]])
    )

    down_away, down_low = after((down_away, down_low), from_next)
    branch_got, _, branch_far = scatter_near(down_away, down_low)
    block_rows = (
        residual_two + down_own + branch_got[:share].astype(F32) + branch_far.astype(F32)
    ).astype(BF16)
    block_cols = rows_to_cols(
        *[
            lax.dynamic_slice_in_dim(block_rows, (place ^ r) * local_width, local_width, 1)
            for r in range(4)
        ],
        from_next,
    )
    block_out = jnp.concatenate([row_block(block_cols, place ^ b) for b in range(4)], 0)

    context_parts = quarters(after(kv_grad, from_next), 1)
    kv_got, _, kv_far = scatter_near(
        jnp.concatenate([context_parts[1], context_parts[3]], 0), context_parts[2]
    )
    context_own = (
        context_parts[0].astype(F32)
        + kv_got[: kv_far.shape[0]].astype(F32)
        + kv_far.astype(F32)
    )
    def spread(own, far):
        own_late, far_late = after((own, far), from_next)
        return own, swap(own_late, "tensor", 1), far, swap(far_late, "tensor", 1)

    forward_near = spread(front_late, front_far)
    back_near = spread(back_late, back_far)
    time_column = time_normed.astype(F32).T

    normed_pair = (one_own_half, normed_got)
    grad_down = halve_end(down_keep, down_got, 3)
    grad_gate_w = halve_end(gate_keep, gate_cross, 2)
    up_blocks = by_level(meet(three_pair, (lifted_grad, lifted_got)))
    grad_up_w = halve_all(up_blocks, 1)
    bundle = bundle_grads(
        count, places[1:], forward_near, back_near, one_parts, attended, row_context,
        context_own.astype(BF16),
    )
    middle = halve_all(bundle, 0)
    part, rows, half = head_cols // count, model_width // count, model_width // 2
    grad_c_query = middle[:, :head_cols]
    grad_c_key = middle[: rows // 2, head_cols:half]
    grad_c_value = middle[rows // 2 :, head_cols:half]
    grad_c_out = jnp.concatenate([middle[:part, half:], middle[part : 2 * part, half:]], 1)
    grad_w_out = jnp.concatenate(
        [middle[2 * part : 3 * part, half:], middle[3 * part :, half:]], 1
    )

    raw_pair = (raw, swap(raw, "seq", 1))
    time_both = jnp.concatenate([time_key_grad, time_value_grad], 0)
    time_both = time_both + swap(after(time_both, from_next), "seq", 1)
    own_time_rows = lax.dynamic_index_in_dim(
        time_column.reshape(count // 2, 2, -1), column, 1, False
    ).reshape(-1, 1)
    outer = own_time_rows * jnp.concatenate([jnp.zeros((head_cols, 1), F32), time_both], 0).T
    blocks = sum(
        jnp.einsum("dn,fn->df", r, c, preferred_element_type=F32)
        for r, c in zip(normed_pair, raw_pair)
    )
    blocks = by_level((blocks + outer).astype(BF16))
    heads_sum = halve_all(blocks, 1)
    grad_w_query, grad_w_key, grad_w_value = (
        heads_sum[:, i * head_cols : (i + 1) * head_cols] for i in range(3)
    )
    return (
        block_out,
        d_frames,
        small[0],
        small[1],
        small[2],
        small[3],
        small[4],
        small[5],
        grad_w_query,
        grad_w_key,
        grad_w_value,
        grad_w_out,
        grad_c_query,
        grad_c_key,
        grad_c_value,
        grad_c_out,
        grad_gate_w,
        grad_up_w,
        grad_down,
    )


def solution(mesh):
    return jax.shard_map(
        per_device,
        mesh=mesh,
        in_specs=(
            P("seq", "tensor"),
            P(),
            P(),
            P(),
            P("tensor"),
            P("tensor"),
            P("tensor"),
            P("tensor"),
            P("tensor"),
            P("tensor"),
            P(None, "tensor"),
            P(None, "tensor"),
            P(None, "tensor"),
            P("tensor", None),
            P(None, "tensor"),
            P(None, "tensor"),
            P(None, "tensor"),
            P("tensor", None),
            P(None, "tensor"),
            P(None, "tensor"),
            P("tensor", None),
            P("seq", "tensor"),
        ),
        out_specs=(
            P("seq", "tensor"),
            P("seq", "tensor"),
            P(("tensor", "seq")),
            P(("tensor", "seq")),
            P(("tensor", "seq")),
            P(("tensor", "seq")),
            P(("tensor", "seq")),
            P(("tensor", "seq")),
            P("seq", "tensor"),
            P("seq", "tensor"),
            P("seq", "tensor"),
            P(("tensor", "seq"), None),
            P("seq", "tensor"),
            P("seq", "tensor"),
            P("seq", "tensor"),
            P(("tensor", "seq"), None),
            P("seq", "tensor"),
            P("seq", "tensor"),
            P(("tensor", "seq"), None),
        ),
        check_vma=False,
    )
```

time: 611 us -> 535 us (0.88)
  waiting for transfers between devices: 237 us -> 183 us
  matrix products: 58.1 us -> 8.44 us
  Pallas kernels: 99.8 us -> 148 us
  starting transfers between devices: 96.4 us -> 77.4 us
  local copies, waits for them, and re-layouts: 60.1 us -> 52.8 us
    ppermute x65 -> x69, waiting for transfers between devices: 210 us -> 148 us  [swap(): lax.ppermute(value, axis, [(i, i ^ by) for i in range(lax.axis_size(axis))])]
    pallas_call x5 -> x11, Pallas kernels: 91.1 us -> 139 us  [the longest x1 26.6 us: ffn(): pl.pallas_call(functools.partial(ffn_body, units // devices), grid_spec=p...]
    dot_general x15 -> x2, matrix products: 33.4 us -> 5.42 us  [per_device(): jnp.einsum('dn,fn->df', r, c, preferred_element_type=F32)]
    ppermute x65 -> x69, starting transfers between devices: 87 us -> 61.8 us  [swap(): lax.ppermute(value, axis, [(i, i ^ by) for i in range(lax.axis_size(axis))])]
    dot_general x8 -> x2, matrix products: 13.3 us -> 1.59 us  [product(): return jnp.dot(left, right, preferred_element_type=jnp.float32)]
    dot_general x14 -> x2, matrix products: 10.7 us -> 0.84 us  [to_frames(): return jnp.einsum('fn,df->nd', rows, weight, preferred_element_type=F32)]
    ppermute x4, waiting for transfers between devices: 26.9 us -> 35.5 us  [shift(): return lax.ppermute(value, axis, pairs)]
    concatenate x4 -> x0, local copies, waits for them, and re-layouts: 7.53 us -> none  [the longest x2 4.61 us: per_device(): jnp.concatenate([value.reshape(count, part, model_width) for value in (gr...]
  transfers between devices with their start and end apart: 69 -> 73, of which waited for: 17 -> 25; matrix products, arithmetic and copies ran while one was open for 24% -> 18% of each run, Pallas kernels for 13% -> 25%
where the time goes in v3:
time: 535 us; the launch traced here: 526 us
  waiting for transfers between devices  183 us (34%)
  Pallas kernels  148 us (28%)
  starting transfers between devices  77.4 us (14%)
  local copies, waits for them, and re-layouts  52.8 us (10%)
  other arithmetic  52.3 us (10%)
  matrix products  8.44 us (2%)
    ppermute x69, waiting for transfers between devices, swap(): lax.ppermute(value, axis, [(i, i ^ by) for i in range(lax.axis_size(axis))])  148 us
    ppermute x69, starting transfers between devices, swap(): lax.ppermute(value, axis, [(i, i ^ by) for i in range(lax.axis_size(axis))])  61.8 us
    ppermute x4, waiting for transfers between devices, shift(): return lax.ppermute(value, axis, pairs)  35.5 us
    pallas_call x1, Pallas kernels, ffn(): pl.pallas_call(functools.partial(ffn_body, units // devices), grid_spec=p...  26.6 us
    pallas_call x1, Pallas kernels, cross_backward(): pl.pallas_call(cross_backward_body, grid=(1,), out_shape=[low(rows), low(...  20.5 us
    pallas_call x3, Pallas kernels, meet(): pl.pallas_call(meet_body, grid=(3,), in_specs=[left, left, right, right],...  18.6 us
    pallas_call x1, Pallas kernels, attend_back(): pl.pallas_call(backward_body, in_specs=[pl.BlockSpec(memory_space=pltpu.S...  17.8 us
    pallas_call x1, Pallas kernels, cross_forward(): pl.pallas_call(functools.partial(cross_forward_body, width // devices), g...  16.8 us
  transfers between devices with their start and end apart: 73, of which 25 were waited for; matrix products, arithmetic and copies ran while one was open for 18% of the time, Pallas kernels for 25%

profile of v3, /device:TPU:0, one launch (start us, length us, event | category | flops | bytes accessed | tf_op | source)
XLA Modules:
  0.0 526.0 jit_solution(1815763782471532099)
XLA Ops:
  1.2 2.6 collective-permute-start.1
  15.6 1.8 collective-permute-start.8
  21.0 8.8 %front.1 = (bf16[384,512]{1,0:T(8,128)(2,1)}, bf16[2,384,512]{2,1,0:T(8,128)(2,1)}, bf16[128,1536]{1,0:T(8,128)(2,1)}, bf16[512,1536]{1,0:T(8,128)(2,1)}, bf16[7...) custom-call(s32[2]{0:T(128)} %rev.4.place, ...), custom_call_target="tpu_custom_call" | custom-call | flops 1 | bytes 1 | tf_op jit(solution)/shard_map/front/pallas_call | solution.py:780
  29.8 4.5 collective-permute-start.6
  42.9 25.2 %collective-permute-done.6 = bf16[2,384,512]{2,1,0:T(8,128)(2,1)} collective-permute-done((bf16[2,384,512]{2,1,0:T(8,128)(2,1)}, bf16[2,384,512]{2,1,0:T(8,128)(2,1)}, u32[]{:S(2)}, u32[]{:S(2)}) %collective-permute-start.6) | collective-permute-done | bytes 786464 | tf_op jit(solution)/shard_map/ppermute | solution.py:33
  69.2 2.5 slice_bitcast_fusion
  71.7 16.4 %attend.1 = (bf16[384,512]{1,0:T(8,128)(2,1)}, f32[6,512]{1,0:T(8,128)}, bf16[256,1536]{1,0:T(8,128)(2,1)}, f32[128,1536]{1,0:T(8,128)}, bf16[128,1536]{1,0:T(8,128)(2,1)}) custom-call(s32[5]{0:T(128)} %pad_add_fusion.2.span, bf16[384,512]{1,0:T(8,128)(2,1)} %get-tuple-element.137.q, bf16[384,512]{1,0:T(8,128)(2,1)} %get-tuple-element.326.k0, ...), custom_call_target="tpu_custom_call" | custom-call | flops 1 | bytes 1 | tf_op jit(solution)/shard_map/attend/pallas_call | solution.py:282
  88.7 5.3 %collective-permute-start.24 = (bf16[512,384]{1,0:T(8,128)(2,1)}, bf16[512,384]{1,0:T(8,128)(2,1)S(1)}, u32[]{:S(2)}, u32[]{:S(2)}) collective-permute-start(bf16[512,384]{1,0:T(8,128)(2,1)} %param.43), channel_id=1, source_target_pairs={{0,1},{1,0},{2,3},{3,2},{4,5},{5,4},{6,7},{7,6},{8,9},{9,8},{10,11... | collective-permute-start | bytes 1179656 | tf_op jit(solution)/shard_map/ppermute | solution.py:27
  97.3 6.3 %collective-permute-done.24 = bf16[512,384]{1,0:T(8,128)(2,1)S(1)} collective-permute-done((bf16[512,384]{1,0:T(8,128)(2,1)}, bf16[512,384]{1,0:T(8,128)(2,1)S(1)}, u32[]{:S(2)}, u32[]{:S(2)}) %collective-permute-start.24) | collective-permute-done | bytes 393248 | tf_op jit(solution)/shard_map/ppermute | solution.py:27
  105.8 1.7 collective-permute-start.19
  107.6 7.9 %collective-permute-done.11.far = bf16[128,1536]{1,0:T(8,128)(2,1)} collective-permute-done((bf16[128,1536]{1,0:T(8,128)(2,1)S(1)}, bf16[128,1536]{1,0:T(8,128)(2,1)}, u32[]{:S(2)}, u32[]{:S(2)}) %collective-permute-start.11) | collective-permute-done | bytes 393248 | tf_op jit(solution)/shard_map/ppermute | solution.py:27
  115.5 2.0 pad_maximum_fusion.g0
  121.2 16.8 %cross.1 = (bf16[128,1536]{1,0:T(8,128)(2,1)}, bf16[128,1536]{1,0:T(8,128)(2,1)}, bf16[128,1536]{1,0:T(8,128)(2,1)}, f32[128,1536]{1,0:T(8,128)}, f32[128,1536]{...) custom-call(s32[2]{0:T(128)} %copy-done.71, ...), custom_call_target="tpu_custom_call" | custom-call | flops 1 | bytes 1 | tf_op jit(solution)/shard_map/cross/pallas_call | solution.py:484
  138.5 10.9 %collective-permute-done.21.n2 = bf16[128,1536]{1,0:T(8,128)(2,1)S(1)} collective-permute-done((bf16[128,1536]{1,0:T(8,128)(2,1)}, bf16[128,1536]{1,0:T(8,128)(2,1)S(1)}, u32[]{:S(2)}, u32[]{:S(2)}) %collective-permute-start.21) | collective-permute-done | bytes 393248 | tf_op jit(solution)/shard_map/ppermute | solution.py:27
  150.1 1.8 collective-permute-start.23
  151.8 5.7 %collective-permute-done.23 = bf16[768,128]{1,0:T(8,128)(2,1)S(1)} collective-permute-done((bf16[768,128]{1,0:T(8,128)(2,1)}, bf16[768,128]{1,0:T(8,128)(2,1)S(1)}, u32[]{:S(2)}, u32[]{:S(2)}) %collective-permute-start.23) | collective-permute-done | bytes 196640 | tf_op jit(solution)/shard_map/ppermute | solution.py:27
  161.3 26.6 %ffn.1 = (bf16[512,1536]{1,0:T(8,128)(2,1)}, bf16[768,512]{1,0:T(8,128)(2,1)}, bf16[768,512]{1,0:T(8,128)(2,1)}, bf16[512,1536]{1,0:T(8,128)(2,1)}, bf16[512,153...) custom-call(s32[2]{0:T(128)} %copy-done.71, ...), custom_call_target="tpu_custom_call" | custom-call | flops 1 | bytes 1 | tf_op jit(solution)/shard_map/ffn/pallas_call | solution.py:559
  188.0 2.5 collective-permute-done.29.got
  194.1 1.9 pad_maximum_fusion.1.f0
  196.0 1.7 collective-permute-start.31
  197.8 5.9 %collective-permute-done.30.far = bf16[128,1536]{1,0:T(8,128)(2,1)S(1)} collective-permute-done((bf16[128,1536]{1,0:T(8,128)(2,1)S(1)}, bf16[128,1536]{1,0:T(8,128)(2,1)S(1)}, u32[]{:S(2)}, u32[]{:S(2)}) %collective-permute-start.30) | collective-permute-done | bytes 393248 | tf_op jit(solution)/shard_map/ppermute | solution.py:27
  205.8 20.5 %cross_back.1 = (bf16[128,1536]{1,0:T(8,128)(2,1)}, bf16[128,1536]{1,0:T(8,128)(2,1)}, bf16[256,1536]{1,0:T(8,128)(2,1)}, f32[4,1536]{1,0:T(4,128)}, bf16[128,1536]{1,0:T(8,128)(2,1)}) custom-call(f32[128,1536]{1,0:T(8,128)} %get-tuple-element.174.own, bf16[256,1536]{1,0:T(8,128)(2,1)} %copy-done.20, bf16[128,1536]{1,0:T(8,128)(2,1)} %copy-done.57, ...), custom_call_target="tpu_custom_call" | custom-call | flops 1 | bytes 1 | tf_op jit(solution)/shard_map/cross_back/pallas_call | solution.py:633
  227.8 1.7 collective-permute-start.39
  229.5 6.1 %meet.3 = bf16[768,1536]{1,0:T(8,128)(2,1)} custom-call(bf16[768,512]{1,0:T(8,128)(2,1)} %get-tuple-element.201.left, bf16[768,512]{1,0:T(8,128)(2,1)} %collective-permute-done.31.left_pair, bf16[512,1536]{1,0:T(8,128)(2,1)} %get-tuple-element.181.grad.right, bf16[512,1536]{1,0:T(8,128)(2,1)} %get-tuple-element.203.right_pair), custom_call_target="tpu_custom_call" | custom-call | flops 1 | bytes 1 | tf_op jit(solution)/shard_map/meet/pallas_call | solution.py:656
  235.6 2.6 collective-permute-done.36.g2.a2
  238.3 2.5 dynamic-slice_bitcast_fusion.4
  240.8 2.4 collective-permute-start.40
  248.7 1.7 slice_bitcast_fusion.7
  252.0 1.8 slice_bitcast_fusion.6
  254.5 17.8 %attend_back.1 = (f32[384,512]{1,0:T(8,128)}, bf16[2,384,512]{2,1,0:T(8,128)(2,1)}, f32[2,384,512]{2,1,0:T(8,128)}, bf16[2,384,512]{2,1,0:T(8,128)(2,1)}, f32[384,1]{1,0:T(8,128)}, /*index=5*/f32[384,1]{1,0:T(8,128)}) custom-call(s32[5]{0:T(128)} %pad_add_fusion.2.span, bf16[384,512]{1,0:T(8,128)(2,1)} %get-tuple-element.137.q, ...), custom_call_target="tpu_custom_call" | custom-call | flops 1 | bytes 1 | tf_op jit(solution)/shard_map/attend_back/pallas_call | solution.py:299
  273.8 8.4 %collective-permute-start.42 = (bf16[2,384,512]{2,1,0:T(8,128)(2,1)}, bf16[2,384,512]{2,1,0:T(8,128)(2,1)}, u32[]{:S(2)}, u32[]{:S(2)}) collective-permute-start(bf16[2,384,512]{2,1,0:T(8,128)(2,1)} %get-tuple-element.209), channel_id=1, source_target_pairs={{0,1},{1,2},{2,3},{3,4},{4,5},{5,6},{6,7},{8,9},{9,10},{10,11},{11... | collective-permute-start | bytes 2359304 | tf_op jit(solution)/shard_map/ppermute | solution.py:33
  282.2 1.9 fusion.6
  287.8 6.4 %down.1 = (bf16[256,1536]{1,0:T(8,128)(2,1)}, f32[128,1536]{1,0:T(8,128)}, bf16[128,1536]{1,0:T(8,128)(2,1)}) custom-call(bf16[512,1536]{1,0:T(8,128)(2,1)} %get-tuple-element.205.hidden, bf16[1536,1536]{1,0:T(8,128)(2,1)} %down_w.3), custom_call_target="tpu_custom_call" | custom-call | flops 1 | bytes 1 | tf_op jit(solution)/shard_map/down/pallas_call | solution.py:681
  294.3 6.1 %meet.4 = bf16[768,1536]{1,0:T(8,128)(2,1)} custom-call(bf16[768,512]{1,0:T(8,128)(2,1)} %pad_maximum_fusion.3.left, bf16[768,512]{1,0:T(8,128)(2,1)} %pad_maximum_fusion.4.left_pair, bf16[512,1536]{1,0:T(8,128)(2,1)} %get-tuple-element.200.right, bf16[512,1536]{1,0:T(8,128)(2,1)} %collective-permute-done.39.right_pair), custom_call_target="tpu_custom_call" | custom-call | flops 1 | bytes 1 | tf_op jit(solution)/shard_map/meet/pallas_call | solution.py:656
  300.4 2.4 dynamic-slice_bitcast_fusion.3
  303.3 17.1 %collective-permute-done.43 = bf16[1,192,1536]{2,1,0:T(8,128)(2,1)} collective-permute-done((bf16[1,192,1536]{2,1,0:T(8,128)(2,1)}, bf16[1,192,1536]{2,1,0:T(8,128)(2,1)}, u32[]{:S(2)}, u32[]{:S(2)}) %collective-permute-start.43) | collective-permute-done | bytes 589856 | tf_op jit(solution)/shard_map/ppermute | solution.py:27
  320.5 10.3 %collective-permute-done.42.behind = bf16[2,384,512]{2,1,0:T(8,128)(2,1)} collective-permute-done((bf16[2,384,512]{2,1,0:T(8,128)(2,1)}, bf16[2,384,512]{2,1,0:T(8,128)(2,1)}, u32[]{:S(2)}, u32[]{:S(2)}) %collective-permute-start.42) | collective-permute-done | bytes 786464 | tf_op jit(solution)/shard_map/ppermute | solution.py:33
  331.8 2.5 collective-permute-start.58
  336.8 6.4 %meet.5 = bf16[768,1536]{1,0:T(8,128)(2,1)} custom-call(bf16[768,512]{1,0:T(8,128)(2,1)} %pad_maximum_fusion.3.left, bf16[768,512]{1,0:T(8,128)(2,1)} %pad_maximum_fusion.4.left_pair, bf16[512,1536]{1,0:T(8,128)(2,1)} %get-tuple-element.211.right, bf16[512,1536]{1,0:T(8,128)(2,1)} %collective-permute-done.44.right_pair), custom_call_target="tpu_custom_call" | custom-call | flops 1 | bytes 1 | tf_op jit(solution)/shard_map/meet/pallas_call | solution.py:656
  343.2 2.4 add_bitcast_fusion
  349.2 7.5 %tail.1 = (bf16[1152,512]{1,0:T(8,128)(2,1)}, bf16[1024,384]{1,0:T(8,128)(2,1)}, f32[512,384]{1,0:T(8,128)}, bf16[512,384]{1,0:T(8,128)(2,1)}) custom-call(s32[1]{0:T(128)} %bitcast.1.place, f32[384,512]{1,0:T(8,128)} %get-tuple-element.221.dq, f32[2,384,512]{2,1,0:T(8,128)} %get-tuple-element.222.kept, bf16[2,384,512]{2,1,0:T(8,128)(2,1)} %collective-permute-done.41.ahead, ...), custom_call_target="tpu_custom_call" | custom-call | flops 1 | bytes 1 | tf_op jit(solution)/shard_map/tail/pallas_call | solution.py:351
  360.2 1.9 fusion.4
  362.1 3.9 collective-permute-done.66
  368.9 1.8 add_convert_fusion.2
  370.7 2.3 collective-permute-start.71
  375.2 8.7 %bundle.1 = bf16[8,192,1536]{2,1,0:T(8,128)(2,1)} custom-call(s32[1]{0:T(128)} %bitcast.1.place, bf16[128,3072]{1,0:T(8,128)(2,1)} %pad_maximum_fusion.1.f0, bf16[128,3072]{1,0:T(8,128)(2,1)} %collective-permute-done.61.f1, bf16[128,3072]{1,0:T(8,128)(2,1)} %collective-permute-done.34.f2, bf16[128,3072]{1,0:T(8,128)(2,1)} %copy-done.40, ...), custom_call_target="tpu_custom_call" | custom-call | flops 1 | bytes 1 | tf_op jit(solution)/shard_map/bundle/pallas_call | solution.py:726
  384.0 3.3 dynamic-slice_bitcast_fusion
  387.3 9.9 %collective-permute-done.70 = bf16[1,192,1536]{2,1,0:T(8,128)(2,1)S(1)} collective-permute-done((bf16[1,192,1536]{2,1,0:T(8,128)(2,1)S(1)}, bf16[1,192,1536]{2,1,0:T(8,128)(2,1)S(1)}, u32[]{:S(2)}, u32[]{:S(2)}) %collective-permute-start.70) | collective-permute-done | bytes 589856 | tf_op jit(solution)/shard_map/ppermute | solution.py:27
  401.5 2.7 fusion.38
  404.3 2.7 fusion.2
  408.6 1.8 collective-permute-done.71
  413.4 1.9 collective-permute-start.47
  416.2 3.4 collective-permute-start.72
  422.4 1.7 collective-permute-start.53
  424.2 2.5 collective-permute-done.53
  436.5 2.9 collective-permute-start.54
  440.2 10.1 %collective-permute-done.54 = f32[4,6,48]{2,0,1:T(4,128)S(1)} collective-permute-done((f32[4,6,48]{2,0,1:T(4,128)S(1)}, f32[4,6,48]{2,0,1:T(4,128)S(1)}, u32[]{:S(2)}, u32[]{:S(2)}) %collective-permute-start.54) | collective-permute-done | bytes 4640 | tf_op jit(solution)/shard_map/ppermute | solution.py:27
  451.1 2.9 collective-permute-done.55
  454.9 2.2 multiply_add_fusion
  459.2 3.0 fusion
  462.8 2.3 add_bitcast_fusion.1
  466.5 2.4 collective-permute-start.60
  468.9 27.4 %collective-permute-done.68 = bf16[2,192,1536]{2,1,0:T(8,128)(2,1)S(1)} collective-permute-done((bf16[2,192,1536]{2,1,0:T(8,128)(2,1)S(1)}, bf16[2,192,1536]{2,1,0:T(8,128)(2,1)S(1)}, u32[]{:S(2)}, u32[]{:S(2)}) %collective-permute-start.68) | collective-permute-done | bytes 1179680 | tf_op jit(solution)/shard_map/ppermute | solution.py:27
  498.5 23.9 %collective-permute-done.69 = bf16[1,192,1536]{2,1,0:T(8,128)(2,1)S(1)} collective-permute-done((bf16[1,192,1536]{2,1,0:T(8,128)(2,1)S(1)}, bf16[1,192,1536]{2,1,0:T(8,128)(2,1)S(1)}, u32[]{:S(2)}, u32[]{:S(2)}) %collective-permute-start.69) | collective-permute-done | bytes 589856 | tf_op jit(solution)/shard_map/ppermute | solution.py:27
  (384 shorter events, 109.0 us)
Async XLA Ops:
  0.7 19.6 %collective-permute-start = (bf16[512,384]{1,0:T(8,128)(2,1)}, bf16[512,384]{1,0:T(8,128)(2,1)S(1)}, u32[]{:S(2)}, u32[]{:S(2)}) collective-permute-start(bf16[512,384]{1,0:T(8,128)(2,1)} %x0.1), channel_id=1, source_target_pairs={{0,8},{8,0},{16,24},{24,16},{1,9},{9,1},{17,25},{25,17},{2,10},{10... | collective-permute-start | bytes 1179656 | tf_op jit(solution)/shard_map/ppermute | solution.py:27
  1.2 12.6 %collective-permute-start.1 = (bf16[512,384]{1,0:T(8,128)(2,1)}, bf16[512,384]{1,0:T(8,128)(2,1)S(1)}, u32[]{:S(2)}, u32[]{:S(2)}) collective-permute-start(bf16[512,384]{1,0:T(8,128)(2,1)} %x0.1), channel_id=1, source_target_pairs={{0,16},{8,24},{16,0},{24,8},{1,17},{9,25},{17,1},{25,9},{2,18},{10... | collective-permute-start | bytes 1179656 | tf_op jit(solution)/shard_map/ppermute | solution.py:27
  7.9 12.3 %collective-permute-start.3 = (f32[6,384]{1,0:T(8,128)S(1)}, f32[6,384]{1,0:T(8,128)S(1)}, u32[]{:S(2)}, u32[]{:S(2)}) collective-permute-start(f32[6,384]{1,0:T(8,128)S(1)} %stack.80.g0), channel_id=1, source_target_pairs={{0,8},{8,0},{16,24},{24,16},{1,9},{9,1},{17,25},{25,17},{2,10},{10... | collective-permute-start | bytes 27656 | tf_op jit(solution)/shard_map/ppermute | solution.py:27
  8.2 9.7 %collective-permute-start.4 = (f32[6,384]{1,0:T(8,128)S(1)}, f32[6,384]{1,0:T(8,128)S(1)}, u32[]{:S(2)}, u32[]{:S(2)}) collective-permute-start(f32[6,384]{1,0:T(8,128)S(1)} %stack.80.g0), channel_id=1, source_target_pairs={{0,16},{8,24},{16,0},{24,8},{1,17},{9,25},{17,1},{25,9},{2,18},{10... | collective-permute-start | bytes 27656 | tf_op jit(solution)/shard_map/ppermute | solution.py:27
  15.6 52.5 %collective-permute-start.8 = (bf16[1536,384]{1,0:T(8,128)(2,1)}, bf16[1536,384]{1,0:T(8,128)(2,1)}, u32[]{:S(2)}, u32[]{:S(2)}) collective-permute-start(bf16[1536,384]{1,0:T(8,128)(2,1)} %q0.3), channel_id=1, source_target_pairs={{0,16},{8,24},{16,0},{24,8},{1,17},{9,25},{17,1},{25,9},{2,18},{10... | collective-permute-start | bytes 3538952 | tf_op jit(solution)/shard_map/ppermute | solution.py:27
  17.3 51.9 %collective-permute-start.9 = (bf16[384,1536]{1,0:T(8,128)(2,1)}, bf16[384,1536]{1,0:T(8,128)(2,1)}, u32[]{:S(2)}, u32[]{:S(2)}) collective-permute-start(bf16[384,1536]{1,0:T(8,128)(2,1)} %o0.3), channel_id=1, source_target_pairs={{0,16},{8,24},{16,0},{24,8},{1,17},{9,25},{17,1},{25,9},{2,18},{10... | collective-permute-start | bytes 3538952 | tf_op jit(solution)/shard_map/ppermute | solution.py:27
  29.8 38.3 %collective-permute-start.6 = (bf16[2,384,512]{2,1,0:T(8,128)(2,1)}, bf16[2,384,512]{2,1,0:T(8,128)(2,1)}, u32[]{:S(2)}, u32[]{:S(2)}) collective-permute-start(bf16[2,384,512]{2,1,0:T(8,128)(2,1)} %get-tuple-element.138), channel_id=1, source_target_pairs={{0,1},{1,2},{2,3},{3,4},{4,5},{5,6},{6,7},{8,9},{9,10},{10,11},{11... | collective-permute-start | bytes 2359304 | tf_op jit(solution)/shard_map/ppermute | solution.py:33
  34.3 33.7 %collective-permute-start.7 = (bf16[2,384,512]{2,1,0:T(8,128)(2,1)}, bf16[2,384,512]{2,1,0:T(8,128)(2,1)}, u32[]{:S(2)}, u32[]{:S(2)}) collective-permute-start(bf16[2,384,512]{2,1,0:T(8,128)(2,1)} %get-tuple-element.138), channel_id=1, source_target_pairs={{1,0},{2,1},{3,2},{4,3},{5,4},{6,5},{7,6},{9,8},{10,9},{11,10},{12... | collective-permute-start | bytes 2359304 | tf_op jit(solution)/shard_map/ppermute | solution.py:33
  88.2 15.4 %collective-permute-start.10 = (bf16[256,1536]{1,0:T(8,128)(2,1)}, bf16[256,1536]{1,0:T(8,128)(2,1)S(1)}, u32[]{:S(2)}, u32[]{:S(2)}) collective-permute-start(bf16[256,1536]{1,0:T(8,128)(2,1)} %get-tuple-element.146), channel_id=1, source_target_pairs={{0,8},{8,0},{16,24},{24,16},{1,9},{9,1},{17,25},{25,17},{2,10},{10... | collective-permute-start | bytes 2359304 | tf_op jit(solution)/shard_map/ppermute | solution.py:27
  88.2 17.7 %collective-permute-start.12 = (bf16[1536,384]{1,0:T(8,128)(2,1)}, bf16[1536,384]{1,0:T(8,128)(2,1)}, u32[]{:S(2)}, u32[]{:S(2)}) collective-permute-start(bf16[1536,384]{1,0:T(8,128)(2,1)} %q0.3), channel_id=1, source_target_pairs={{0,8},{8,0},{16,24},{24,16},{1,9},{9,1},{17,25},{25,17},{2,10},{10... | collective-permute-start | bytes 3538952 | tf_op jit(solution)/shard_map/ppermute | solution.py:27
  88.7 14.9 %collective-permute-start.24 = (bf16[512,384]{1,0:T(8,128)(2,1)}, bf16[512,384]{1,0:T(8,128)(2,1)S(1)}, u32[]{:S(2)}, u32[]{:S(2)}) collective-permute-start(bf16[512,384]{1,0:T(8,128)(2,1)} %param.43), channel_id=1, source_target_pairs={{0,1},{1,0},{2,3},{3,2},{4,5},{5,4},{6,7},{7,6},{8,9},{9,8},{10,11... | collective-permute-start | bytes 1179656 | tf_op jit(solution)/shard_map/ppermute | solution.py:27
  94.0 23.5 %collective-permute-start.17 = (bf16[384,1536]{1,0:T(8,128)(2,1)}, bf16[384,1536]{1,0:T(8,128)(2,1)}, u32[]{:S(2)}, u32[]{:S(2)}) collective-permute-start(bf16[384,1536]{1,0:T(8,128)(2,1)} %o0.3), channel_id=1, source_target_pairs={{0,8},{8,0},{16,24},{24,16},{1,9},{9,1},{17,25},{25,17},{2,10},{10... | collective-permute-start | bytes 3538952 | tf_op jit(solution)/shard_map/ppermute | solution.py:27
  95.7 8.5 %collective-permute-start.14 = (bf16[256,384]{1,0:T(8,128)(2,1)S(1)}, bf16[256,384]{1,0:T(8,128)(2,1)S(1)}, u32[]{:S(2)}, u32[]{:S(2)}) collective-permute-start(bf16[256,384]{1,0:T(8,128)(2,1)S(1)} %pad_maximum_fusion.11.c0), channel_id=1, source_target_pairs={{0,16},{8,24},{16,0},{24,8},{1,17},{9,25},{17,1},{25,9},{2,18},{10... | collective-permute-start | bytes 589832 | tf_op jit(solution)/shard_map/ppermute | solution.py:27
  103.6 16.9 %collective-permute-start.13 = (bf16[1536,384]{1,0:T(8,128)(2,1)}, bf16[1536,384]{1,0:T(8,128)(2,1)}, u32[]{:S(2)}, u32[]{:S(2)}) collective-permute-start(bf16[1536,384]{1,0:T(8,128)(2,1)} %collective-permute-done.8.q2), channel_id=1, source_target_pairs={{0,8},{8,0},{16,24},{24,16},{1,9},{9,1},{17,25},{25,17},{2,10},{10... | collective-permute-start | bytes 3538952 | tf_op jit(solution)/shard_map/ppermute | solution.py:27
  103.6 16.9 %collective-permute-start.18 = (bf16[384,1536]{1,0:T(8,128)(2,1)}, bf16[384,1536]{1,0:T(8,128)(2,1)}, u32[]{:S(2)}, u32[]{:S(2)}) collective-permute-start(bf16[384,1536]{1,0:T(8,128)(2,1)} %collective-permute-done.9.o2), channel_id=1, source_target_pairs={{0,8},{8,0},{16,24},{24,16},{1,9},{9,1},{17,25},{25,17},{2,10},{10... | collective-permute-start | bytes 3538952 | tf_op jit(solution)/shard_map/ppermute | solution.py:27
  104.2 11.3 %collective-permute-start.11 = (bf16[128,1536]{1,0:T(8,128)(2,1)S(1)}, bf16[128,1536]{1,0:T(8,128)(2,1)}, u32[]{:S(2)}, u32[]{:S(2)}) collective-permute-start(bf16[128,1536]{1,0:T(8,128)(2,1)S(1)} %add_convert_fusion.4), channel_id=1, source_target_pairs={{0,16},{8,24},{16,0},{24,8},{1,17},{9,25},{17,1},{25,9},{2,18},{10... | collective-permute-start | bytes 1179656 | tf_op jit(solution)/shard_map/ppermute | solution.py:27
  105.8 32.1 %collective-permute-start.19 = (bf16[768,512]{1,0:T(8,128)(2,1)}, bf16[768,512]{1,0:T(8,128)(2,1)}, u32[]{:S(2)}, u32[]{:S(2)}) collective-permute-start(bf16[768,512]{1,0:T(8,128)(2,1)} %get-tuple-element.160), channel_id=1, source_target_pairs={{0,1},{1,0},{2,3},{3,2},{4,5},{5,4},{6,7},{7,6},{8,9},{9,8},{10,11... | collective-permute-start | bytes 2359304 | tf_op jit(solution)/shard_map/ppermute | solution.py:27
  117.5 32.0 %collective-permute-start.25 = (bf16[2,512,384]{2,1,0:T(8,128)(2,1)}, bf16[2,512,384]{2,1,0:T(8,128)(2,1)}, u32[]{:S(2)}, u32[]{:S(2)}) collective-permute-start(bf16[2,512,384]{2,1,0:T(8,128)(2,1)} %pad_maximum_fusion.g0), channel_id=1, source_target_pairs={{0,16},{8,24},{16,0},{24,8},{1,17},{9,25},{17,1},{25,9},{2,18},{10... | collective-permute-start | bytes 2359304 | tf_op jit(solution)/shard_map/ppermute | solution.py:27
  138.0 11.5 %collective-permute-start.21 = (bf16[128,1536]{1,0:T(8,128)(2,1)}, bf16[128,1536]{1,0:T(8,128)(2,1)S(1)}, u32[]{:S(2)}, u32[]{:S(2)}) collective-permute-start(bf16[128,1536]{1,0:T(8,128)(2,1)} %get-tuple-element.163.n0), channel_id=1, source_target_pairs={{0,16},{8,24},{16,0},{24,8},{1,17},{9,25},{17,1},{25,9},{2,18},{10... | collective-permute-start | bytes 1179656 | tf_op jit(solution)/shard_map/ppermute | solution.py:27
  138.5 19.0 %collective-permute-start.20 = (bf16[128,1536]{1,0:T(8,128)(2,1)}, bf16[128,1536]{1,0:T(8,128)(2,1)S(1)}, u32[]{:S(2)}, u32[]{:S(2)}) collective-permute-start(bf16[128,1536]{1,0:T(8,128)(2,1)} %get-tuple-element.163.n0), channel_id=1, source_target_pairs={{0,8},{8,0},{16,24},{24,16},{1,9},{9,1},{17,25},{25,17},{2,10},{10... | collective-permute-start | bytes 1179656 | tf_op jit(solution)/shard_map/ppermute | solution.py:27
  149.5 8.1 %collective-permute-start.22 = (bf16[128,1536]{1,0:T(8,128)(2,1)S(1)}, bf16[128,1536]{1,0:T(8,128)(2,1)S(1)}, u32[]{:S(2)}, u32[]{:S(2)}) collective-permute-start(bf16[128,1536]{1,0:T(8,128)(2,1)S(1)} %collective-permute-done.21.n2), channel_id=1, source_target_pairs={{0,8},{8,0},{16,24},{24,16},{1,9},{9,1},{17,25},{25,17},{2,10},{10... | collective-permute-start | bytes 1179656 | tf_op jit(solution)/shard_map/ppermute | solution.py:27
  149.5 11.9 %collective-permute-start.26 = (bf16[2,512,384]{2,1,0:T(8,128)(2,1)}, bf16[2,512,384]{2,1,0:T(8,128)(2,1)}, u32[]{:S(2)}, u32[]{:S(2)}) collective-permute-start(bf16[2,512,384]{2,1,0:T(8,128)(2,1)} %pad_maximum_fusion.g0), channel_id=1, source_target_pairs={{0,8},{8,0},{16,24},{24,16},{1,9},{9,1},{17,25},{25,17},{2,10},{10... | collective-permute-start | bytes 2359304 | tf_op jit(solution)/shard_map/ppermute | solution.py:27
  150.0 11.3 %collective-permute-start.27 = (bf16[2,512,384]{2,1,0:T(8,128)(2,1)}, bf16[2,512,384]{2,1,0:T(8,128)(2,1)}, u32[]{:S(2)}, u32[]{:S(2)}) collective-permute-start(bf16[2,512,384]{2,1,0:T(8,128)(2,1)} %collective-permute-done.25.g2), channel_id=1, source_target_pairs={{0,8},{8,0},{16,24},{24,16},{1,9},{9,1},{17,25},{25,17},{2,10},{10... | collective-permute-start | bytes 2359304 | tf_op jit(solution)/shard_map/ppermute | solution.py:27
  150.1 7.5 %collective-permute-start.23 = (bf16[768,128]{1,0:T(8,128)(2,1)}, bf16[768,128]{1,0:T(8,128)(2,1)S(1)}, u32[]{:S(2)}, u32[]{:S(2)}) collective-permute-start(bf16[768,128]{1,0:T(8,128)(2,1)} %get-tuple-element.162), channel_id=1, source_target_pairs={{0,1},{1,0},{2,3},{3,2},{4,5},{5,4},{6,7},{7,6},{8,9},{9,8},{10,11... | collective-permute-start | bytes 589832 | tf_op jit(solution)/shard_map/ppermute | solution.py:27
  160.8 27.1 %collective-permute-start.28 = (bf16[2,768,128]{2,1,0:T(8,128)(2,1)}, bf16[2,768,128]{2,1,0:T(8,128)(2,1)S(1)}, u32[]{:S(2)}, u32[]{:S(2)}) collective-permute-start(bf16[2,768,128]{2,1,0:T(8,128)(2,1)} %pad_maximum_fusion.5), channel_id=1, source_target_pairs={{0,16},{8,24},{16,0},{24,8},{1,17},{9,25},{17,1},{25,9},{2,18},{10... | collective-permute-start | bytes 1179656 | tf_op jit(solution)/shard_map/ppermute | solution.py:27
  192.5 11.2 %collective-permute-start.30 = (bf16[128,1536]{1,0:T(8,128)(2,1)S(1)}, bf16[128,1536]{1,0:T(8,128)(2,1)S(1)}, u32[]{:S(2)}, u32[]{:S(2)}) collective-permute-start(bf16[128,1536]{1,0:T(8,128)(2,1)S(1)} %add_convert_fusion.3), channel_id=1, source_target_pairs={{0,16},{8,24},{16,0},{24,8},{1,17},{9,25},{17,1},{25,9},{2,18},{10... | collective-permute-start | bytes 1179656 | tf_op jit(solution)/shard_map/ppermute | solution.py:27
  196.0 30.2 %collective-permute-start.31 = (bf16[768,512]{1,0:T(8,128)(2,1)}, bf16[768,512]{1,0:T(8,128)(2,1)}, u32[]{:S(2)}, u32[]{:S(2)}) collective-permute-start(bf16[768,512]{1,0:T(8,128)(2,1)} %get-tuple-element.185), channel_id=1, source_target_pairs={{0,1},{1,0},{2,3},{3,2},{4,5},{5,4},{6,7},{7,6},{8,9},{9,8},{10,11... | collective-permute-start | bytes 2359304 | tf_op jit(solution)/shard_map/ppermute | solution.py:27
  203.7 22.6 %collective-permute-start.34 = (bf16[128,3072]{1,0:T(8,128)(2,1)}, bf16[128,3072]{1,0:T(8,128)(2,1)}, u32[]{:S(2)}, u32[]{:S(2)}) collective-permute-start(bf16[128,3072]{1,0:T(8,128)(2,1)} %pad_maximum_fusion.1.f0), channel_id=1, source_target_pairs={{0,16},{8,24},{16,0},{24,8},{1,17},{9,25},{17,1},{25,9},{2,18},{10... | collective-permute-start | bytes 2359304 | tf_op jit(solution)/shard_map/ppermute | solution.py:27
  205.3 21.0 %collective-permute-start.32 = (bf16[2,768,128]{2,1,0:T(8,128)(2,1)}, bf16[2,768,128]{2,1,0:T(8,128)(2,1)S(1)}, u32[]{:S(2)}, u32[]{:S(2)}) collective-permute-start(bf16[2,768,128]{2,1,0:T(8,128)(2,1)} %pad_maximum_fusion.5), channel_id=1, source_target_pairs={{0,8},{8,0},{16,24},{24,16},{1,9},{9,1},{17,25},{25,17},{2,10},{10... | collective-permute-start | bytes 1179656 | tf_op jit(solution)/shard_map/ppermute | solution.py:27
  205.3 21.1 %collective-permute-start.33 = (bf16[2,768,128]{2,1,0:T(8,128)(2,1)S(1)}, bf16[2,768,128]{2,1,0:T(8,128)(2,1)}, u32[]{:S(2)}, u32[]{:S(2)}) collective-permute-start(bf16[2,768,128]{2,1,0:T(8,128)(2,1)S(1)} %collective-permute-done.28), channel_id=1, source_target_pairs={{0,8},{8,0},{16,24},{24,16},{1,9},{9,1},{17,25},{25,17},{2,10},{10... | collective-permute-start | bytes 1179656 | tf_op jit(solution)/shard_map/ppermute | solution.py:27
  227.0 11.2 %collective-permute-start.36 = (bf16[128,1536]{1,0:T(8,128)(2,1)}, bf16[128,1536]{1,0:T(8,128)(2,1)S(1)}, u32[]{:S(2)}, u32[]{:S(2)}) collective-permute-start(bf16[128,1536]{1,0:T(8,128)(2,1)} %get-tuple-element.216.g0.a0), channel_id=1, source_target_pairs={{0,16},{8,24},{16,0},{24,8},{1,17},{9,25},{17,1},{25,9},{2,18},{10... | collective-permute-start | bytes 1179656 | tf_op jit(solution)/shard_map/ppermute | solution.py:27
  227.8 44.6 %collective-permute-start.39 = (bf16[512,1536]{1,0:T(8,128)(2,1)}, bf16[512,1536]{1,0:T(8,128)(2,1)}, u32[]{:S(2)}, u32[]{:S(2)}) collective-permute-start(bf16[512,1536]{1,0:T(8,128)(2,1)} %get-tuple-element.200.right), channel_id=1, source_target_pairs={{0,1},{1,0},{2,3},{3,2},{4,5},{5,4},{6,7},{7,6},{8,9},{9,8},{10,11... | collective-permute-start | bytes 4718600 | tf_op jit(solution)/shard_map/ppermute | solution.py:27
  238.3 5.9 %collective-permute-start.37 = (bf16[128,1536]{1,0:T(8,128)(2,1)S(1)}, bf16[128,1536]{1,0:T(8,128)(2,1)S(1)}, u32[]{:S(2)}, u32[]{:S(2)}) collective-permute-start(bf16[128,1536]{1,0:T(8,128)(2,1)S(1)} %collective-permute-done.36.g2.a2), channel_id=1, source_target_pairs={{0,8},{8,0},{16,24},{24,16},{1,9},{9,1},{17,25},{25,17},{2,10},{10... | collective-permute-start | bytes 1179656 | tf_op jit(solution)/shard_map/ppermute | solution.py:27
  240.8 31.6 %collective-permute-start.40 = (bf16[2,192,1536]{2,1,0:T(8,128)(2,1)}, bf16[2,192,1536]{2,1,0:T(8,128)(2,1)}, u32[]{:S(2)}, u32[]{:S(2)}) collective-permute-start(bf16[2,192,1536]{2,1,0:T(8,128)(2,1)} %dynamic-slice_bitcast_fusion.4), channel_id=1, source_target_pairs={{0,2},{1,3},{2,0},{3,1},{4,6},{5,7},{6,4},{7,5},{8,10},{9,11},{10,... | collective-permute-start | bytes 3538952 | tf_op jit(solution)/shard_map/ppermute | solution.py:27
  244.9 27.4 %collective-permute-start.38 = (bf16[128,3072]{1,0:T(8,128)(2,1)}, bf16[128,3072]{1,0:T(8,128)(2,1)}, u32[]{:S(2)}, u32[]{:S(2)}) collective-permute-start(bf16[128,3072]{1,0:T(8,128)(2,1)} %pad_maximum_fusion.2.b0), channel_id=1, source_target_pairs={{0,16},{8,24},{16,0},{24,8},{1,17},{9,25},{17,1},{25,9},{2,18},{10... | collective-permute-start | bytes 2359304 | tf_op jit(solution)/shard_map/ppermute | solution.py:27
  248.7 5.2 collective-permute-start.35
  251.7 68.7 %collective-permute-start.44 = (bf16[512,1536]{1,0:T(8,128)(2,1)}, bf16[512,1536]{1,0:T(8,128)(2,1)}, u32[]{:S(2)}, u32[]{:S(2)}) collective-permute-start(bf16[512,1536]{1,0:T(8,128)(2,1)} %get-tuple-element.211.right), channel_id=1, source_target_pairs={{0,1},{1,0},{2,3},{3,2},{4,5},{5,4},{6,7},{7,6},{8,9},{9,8},{10,11... | collective-permute-start | bytes 4718600 | tf_op jit(solution)/shard_map/ppermute | solution.py:27
  272.4 48.1 %collective-permute-start.41 = (bf16[2,384,512]{2,1,0:T(8,128)(2,1)}, bf16[2,384,512]{2,1,0:T(8,128)(2,1)}, u32[]{:S(2)}, u32[]{:S(2)}) collective-permute-start(bf16[2,384,512]{2,1,0:T(8,128)(2,1)} %get-tuple-element.204), channel_id=1, source_target_pairs={{1,0},{2,1},{3,2},{4,3},{5,4},{6,5},{7,6},{9,8},{10,9},{11,10},{12... | collective-permute-start | bytes 2359304 | tf_op jit(solution)/shard_map/ppermute | solution.py:33
  273.8 57.0 %collective-permute-start.42 = (bf16[2,384,512]{2,1,0:T(8,128)(2,1)}, bf16[2,384,512]{2,1,0:T(8,128)(2,1)}, u32[]{:S(2)}, u32[]{:S(2)}) collective-permute-start(bf16[2,384,512]{2,1,0:T(8,128)(2,1)} %get-tuple-element.209), channel_id=1, source_target_pairs={{0,1},{1,2},{2,3},{3,4},{4,5},{5,6},{6,7},{8,9},{9,10},{10,11},{11... | collective-permute-start | bytes 2359304 | tf_op jit(solution)/shard_map/ppermute | solution.py:33
  285.1 35.4 %collective-permute-start.43 = (bf16[1,192,1536]{2,1,0:T(8,128)(2,1)}, bf16[1,192,1536]{2,1,0:T(8,128)(2,1)}, u32[]{:S(2)}, u32[]{:S(2)}) collective-permute-start(bf16[1,192,1536]{2,1,0:T(8,128)(2,1)} %constant_dynamic-slice_fusion.21), channel_id=1, source_target_pairs={{0,4},{1,5},{2,6},{3,7},{4,0},{5,1},{6,2},{7,3},{8,12},{9,13},{10,... | collective-permute-start | bytes 1769480 | tf_op jit(solution)/shard_map/ppermute | solution.py:27
  302.8 54.8 %collective-permute-start.49 = (bf16[2,192,1536]{2,1,0:T(8,128)(2,1)}, bf16[2,192,1536]{2,1,0:T(8,128)(2,1)}, u32[]{:S(2)}, u32[]{:S(2)}) collective-permute-start(bf16[2,192,1536]{2,1,0:T(8,128)(2,1)} %dynamic-slice_bitcast_fusion.3), channel_id=1, source_target_pairs={{0,2},{1,3},{2,0},{3,1},{4,6},{5,7},{6,4},{7,5},{8,10},{9,11},{10,... | collective-permute-start | bytes 3538952 | tf_op jit(solution)/shard_map/ppermute | solution.py:27
  331.3 36.4 %collective-permute-start.45 = (bf16[256,1536]{1,0:T(8,128)(2,1)}, bf16[256,1536]{1,0:T(8,128)(2,1)}, u32[]{:S(2)}, u32[]{:S(2)}) collective-permute-start(bf16[256,1536]{1,0:T(8,128)(2,1)} %get-tuple-element.213), channel_id=1, source_target_pairs={{0,8},{8,0},{16,24},{24,16},{1,9},{9,1},{17,25},{25,17},{2,10},{10... | collective-permute-start | bytes 2359304 | tf_op jit(solution)/shard_map/ppermute | solution.py:27
  331.8 24.8 %collective-permute-start.58 = (f32[768,1]{0,1:T(1,128)S(1)}, f32[768,1]{0,1:T(1,128)S(1)}, u32[]{:S(2)}, u32[]{:S(2)}) collective-permute-start(f32[768,1]{0,1:T(1,128)S(1)} %pad_maximum_fusion.16), channel_id=1, source_target_pairs={{0,1},{1,0},{2,3},{3,2},{4,5},{5,4},{6,7},{7,6},{8,9},{9,8},{10,11... | collective-permute-start | bytes 9224 | tf_op jit(solution)/shard_map/ppermute | solution.py:27
  334.4 33.6 %collective-permute-start.61 = (bf16[128,3072]{1,0:T(8,128)(2,1)}, bf16[128,3072]{1,0:T(8,128)(2,1)}, u32[]{:S(2)}, u32[]{:S(2)}) collective-permute-start(bf16[128,3072]{1,0:T(8,128)(2,1)} %pad_maximum_fusion.1.f0), channel_id=1, source_target_pairs={{0,8},{8,0},{16,24},{24,16},{1,9},{9,1},{17,25},{25,17},{2,10},{10... | collective-permute-start | bytes 2359304 | tf_op jit(solution)/shard_map/ppermute | solution.py:27
  336.5 21.4 %collective-permute-start.65 = (bf16[512,384]{1,0:T(8,128)(2,1)}, bf16[512,384]{1,0:T(8,128)(2,1)}, u32[]{:S(2)}, u32[]{:S(2)}) collective-permute-start(bf16[512,384]{1,0:T(8,128)(2,1)} %pad_maximum_fusion.8), channel_id=1, source_target_pairs={{0,8},{8,0},{16,24},{24,16},{1,9},{9,1},{17,25},{25,17},{2,10},{10... | collective-permute-start | bytes 1179656 | tf_op jit(solution)/shard_map/ppermute | solution.py:27
  356.7 14.0 %collective-permute-start.62 = (bf16[128,3072]{1,0:T(8,128)(2,1)}, bf16[128,3072]{1,0:T(8,128)(2,1)S(1)}, u32[]{:S(2)}, u32[]{:S(2)}) collective-permute-start(bf16[128,3072]{1,0:T(8,128)(2,1)} %collective-permute-done.34.f2), channel_id=1, source_target_pairs={{0,8},{8,0},{16,24},{24,16},{1,9},{9,1},{17,25},{25,17},{2,10},{10... | collective-permute-start | bytes 2359304 | tf_op jit(solution)/shard_map/ppermute | solution.py:27
  357.6 15.4 %collective-permute-start.63 = (bf16[128,3072]{1,0:T(8,128)(2,1)}, bf16[128,3072]{1,0:T(8,128)(2,1)S(1)}, u32[]{:S(2)}, u32[]{:S(2)}) collective-permute-start(bf16[128,3072]{1,0:T(8,128)(2,1)} %pad_maximum_fusion.2.b0), channel_id=1, source_target_pairs={{0,8},{8,0},{16,24},{24,16},{1,9},{9,1},{17,25},{25,17},{2,10},{10... | collective-permute-start | bytes 2359304 | tf_op jit(solution)/shard_map/ppermute | solution.py:27
  358.9 7.1 %collective-permute-start.66 = (bf16[256,384]{1,0:T(8,128)(2,1)S(1)}, bf16[256,384]{1,0:T(8,128)(2,1)S(1)}, u32[]{:S(2)}, u32[]{:S(2)}) collective-permute-start(bf16[256,384]{1,0:T(8,128)(2,1)S(1)} %add_convert_fusion.6), channel_id=1, source_target_pairs={{0,16},{8,24},{16,0},{24,8},{1,17},{9,25},{17,1},{25,9},{2,18},{10... | collective-permute-start | bytes 589832 | tf_op jit(solution)/shard_map/ppermute | solution.py:27
  366.0 7.9 %collective-permute-start.64 = (bf16[128,3072]{1,0:T(8,128)(2,1)}, bf16[128,3072]{1,0:T(8,128)(2,1)}, u32[]{:S(2)}, u32[]{:S(2)}) collective-permute-start(bf16[128,3072]{1,0:T(8,128)(2,1)} %collective-permute-done.38.b2), channel_id=1, source_target_pairs={{0,8},{8,0},{16,24},{24,16},{1,9},{9,1},{17,25},{25,17},{2,10},{10... | collective-permute-start | bytes 2359304 | tf_op jit(solution)/shard_map/ppermute | solution.py:27
  367.7 33.8 %collective-permute-start.57 = (bf16[1152,512]{1,0:T(8,128)(2,1)}, bf16[1152,512]{1,0:T(8,128)(2,1)}, u32[]{:S(2)}, u32[]{:S(2)}) collective-permute-start(bf16[1152,512]{1,0:T(8,128)(2,1)} %get-tuple-element.239), channel_id=1, source_target_pairs={{0,1},{1,0},{2,3},{3,2},{4,5},{5,4},{6,7},{7,6},{8,9},{9,8},{10,11... | collective-permute-start | bytes 3538952 | tf_op jit(solution)/shard_map/ppermute | solution.py:27
  368.0 29.2 %collective-permute-start.70 = (bf16[1,192,1536]{2,1,0:T(8,128)(2,1)S(1)}, bf16[1,192,1536]{2,1,0:T(8,128)(2,1)S(1)}, u32[]{:S(2)}, u32[]{:S(2)}) collective-permute-start(bf16[1,192,1536]{2,1,0:T(8,128)(2,1)S(1)} %constant_dynamic-slice_fusion.1), channel_id=1, source_target_pairs={{0,4},{1,5},{2,6},{3,7},{4,0},{5,1},{6,2},{7,3},{8,12},{9,13},{10,... | collective-permute-start | bytes 1769480 | tf_op jit(solution)/shard_map/ppermute | solution.py:27
  370.7 39.6 %collective-permute-start.71 = (bf16[2,192,1536]{2,1,0:T(8,128)(2,1)}, bf16[2,192,1536]{2,1,0:T(8,128)(2,1)}, u32[]{:S(2)}, u32[]{:S(2)}) collective-permute-start(bf16[2,192,1536]{2,1,0:T(8,128)(2,1)} %dynamic-slice_bitcast_fusion.1), channel_id=1, source_target_pairs={{0,2},{1,3},{2,0},{3,1},{4,6},{5,7},{6,4},{7,5},{8,10},{9,11},{10,... | collective-permute-start | bytes 3538952 | tf_op jit(solution)/shard_map/ppermute | solution.py:27
  373.9 26.1 %collective-permute-start.50 = (bf16[1024,384]{1,0:T(8,128)(2,1)}, bf16[1024,384]{1,0:T(8,128)(2,1)S(1)}, u32[]{:S(2)}, u32[]{:S(2)}) collective-permute-start(bf16[1024,384]{1,0:T(8,128)(2,1)} %get-tuple-element.230), channel_id=1, source_target_pairs={{0,8},{8,0},{16,24},{24,16},{1,9},{9,1},{17,25},{25,17},{2,10},{10... | collective-permute-start | bytes 2359304 | tf_op jit(solution)/shard_map/ppermute | solution.py:27
  373.9 38.0 %collective-permute-start.46 = (bf16[128,1536]{1,0:T(8,128)(2,1)}, bf16[128,1536]{1,0:T(8,128)(2,1)}, u32[]{:S(2)}, u32[]{:S(2)}) collective-permute-start(bf16[128,1536]{1,0:T(8,128)(2,1)} %add_convert_fusion.2), channel_id=1, source_target_pairs={{0,16},{8,24},{16,0},{24,8},{1,17},{9,25},{17,1},{25,9},{2,18},{10... | collective-permute-start | bytes 1179656 | tf_op jit(solution)/shard_map/ppermute | solution.py:27
  397.2 62.0 %collective-permute-start.67 = (bf16[4,192,1536]{2,1,0:T(8,128)(2,1)}, bf16[4,192,1536]{2,1,0:T(8,128)(2,1)}, u32[]{:S(2)}, u32[]{:S(2)}) collective-permute-start(bf16[4,192,1536]{2,1,0:T(8,128)(2,1)} %dynamic-slice_bitcast_fusion), channel_id=1, source_target_pairs={{0,1},{1,0},{2,3},{3,2},{4,5},{5,4},{6,7},{7,6},{8,9},{9,8},{10,11... | collective-permute-start | bytes 7077896 | tf_op jit(solution)/shard_map/ppermute | solution.py:27
  400.2 19.6 %collective-permute-start.51 = (bf16[512,384]{1,0:T(8,128)(2,1)S(1)}, bf16[512,384]{1,0:T(8,128)(2,1)S(1)}, u32[]{:S(2)}, u32[]{:S(2)}) collective-permute-start(bf16[512,384]{1,0:T(8,128)(2,1)S(1)} %add_convert_fusion), channel_id=1, source_target_pairs={{0,16},{8,24},{16,0},{24,8},{1,17},{9,25},{17,1},{25,9},{2,18},{10... | collective-permute-start | bytes 1179656 | tf_op jit(solution)/shard_map/ppermute | solution.py:27
  408.1 56.9 %collective-permute-start.59 = (bf16[2,192,1152]{2,1,0:T(8,128)(2,1)}, bf16[2,192,1152]{2,1,0:T(8,128)(2,1)}, u32[]{:S(2)}, u32[]{:S(2)}) collective-permute-start(bf16[2,192,1152]{2,1,0:T(8,128)(2,1)} %dynamic-slice_bitcast_fusion.5), channel_id=1, source_target_pairs={{0,2},{1,3},{2,0},{3,1},{4,6},{5,7},{6,4},{7,5},{8,10},{9,11},{10,... | collective-permute-start | bytes 2654216 | tf_op jit(solution)/shard_map/ppermute | solution.py:27
  413.4 6.2 %collective-permute-start.47 = (bf16[128,768]{1,0:T(8,128)(2,1)S(1)}, bf16[128,768]{1,0:T(8,128)(2,1)S(1)}, u32[]{:S(2)}, u32[]{:S(2)}) collective-permute-start(bf16[128,768]{1,0:T(8,128)(2,1)S(1)} %pad_maximum_fusion.12), channel_id=1, source_target_pairs={{0,16},{8,24},{16,0},{24,8},{1,17},{9,25},{17,1},{25,9},{2,18},{10... | collective-permute-start | bytes 589832 | tf_op jit(solution)/shard_map/ppermute | solution.py:27
  416.2 46.6 %collective-permute-start.72 = (bf16[1,192,1536]{2,1,0:T(8,128)(2,1)}, bf16[1,192,1536]{2,1,0:T(8,128)(2,1)}, u32[]{:S(2)}, u32[]{:S(2)}) collective-permute-start(bf16[1,192,1536]{2,1,0:T(8,128)(2,1)} %constant_dynamic-slice_fusion), channel_id=1, source_target_pairs={{0,4},{1,5},{2,6},{3,7},{4,0},{5,1},{6,2},{7,3},{8,12},{9,13},{10,... | collective-permute-start | bytes 1769480 | tf_op jit(solution)/shard_map/ppermute | solution.py:27
  436.5 13.8 %collective-permute-start.54 = (f32[4,6,48]{2,0,1:T(4,128)S(1)}, f32[4,6,48]{2,0,1:T(4,128)S(1)}, u32[]{:S(2)}, u32[]{:S(2)}) collective-permute-start(f32[4,6,48]{2,0,1:T(4,128)S(1)} %bitcast.163), channel_id=1, source_target_pairs={{0,1},{1,0},{2,3},{3,2},{4,5},{5,4},{6,7},{7,6},{8,9},{9,8},{10,11... | collective-permute-start | bytes 13832 | tf_op jit(solution)/shard_map/ppermute | solution.py:27
  454.1 4.6 collective-permute-start.56
  462.3 34.0 %collective-permute-start.68 = (bf16[2,192,1536]{2,1,0:T(8,128)(2,1)S(1)}, bf16[2,192,1536]{2,1,0:T(8,128)(2,1)S(1)}, u32[]{:S(2)}, u32[]{:S(2)}) collective-permute-start(bf16[2,192,1536]{2,1,0:T(8,128)(2,1)S(1)} %dynamic-slice_bitcast_fusion.2), channel_id=1, source_target_pairs={{0,2},{1,3},{2,0},{3,1},{4,6},{5,7},{6,4},{7,5},{8,10},{9,11},{10,... | collective-permute-start | bytes 3538952 | tf_op jit(solution)/shard_map/ppermute | solution.py:27
  466.5 30.9 %collective-permute-start.60 = (bf16[1,192,1152]{2,1,0:T(8,128)(2,1)S(1)}, bf16[1,192,1152]{2,1,0:T(8,128)(2,1)S(1)}, u32[]{:S(2)}, u32[]{:S(2)}) collective-permute-start(bf16[1,192,1152]{2,1,0:T(8,128)(2,1)S(1)} %constant_dynamic-slice_fusion.3), channel_id=1, source_target_pairs={{0,4},{1,5},{2,6},{3,7},{4,0},{5,1},{6,2},{7,3},{8,12},{9,13},{10,... | collective-permute-start | bytes 1327112 | tf_op jit(solution)/shard_map/ppermute | solution.py:27
  496.6 25.8 %collective-permute-start.69 = (bf16[1,192,1536]{2,1,0:T(8,128)(2,1)S(1)}, bf16[1,192,1536]{2,1,0:T(8,128)(2,1)S(1)}, u32[]{:S(2)}, u32[]{:S(2)}) collective-permute-start(bf16[1,192,1536]{2,1,0:T(8,128)(2,1)S(1)} %constant_dynamic-slice_fusion.2), channel_id=1, source_target_pairs={{0,4},{1,5},{2,6},{3,7},{4,0},{5,1},{6,2},{7,3},{8,12},{9,13},{10,... | collective-permute-start | bytes 1769480 | tf_op jit(solution)/shard_map/ppermute | solution.py:27
  (82 other events, 1007.5 us)
